TPU v7x, 256 devices: a whole 4x4x8 slice. The times are simulated.
256 devices in a mesh: row: 8 (over x_lo, y), col: 32 (over z, x_hi, core).
Axes of the slice: x: 4 (x_hi: 2, x_lo: 2; x = x_hi * 2 + x_lo), y: 4, z: 8, core: 2. Of those that a mesh axis runs over, the one named last changes fastest.
Arguments:
- state: float32 [2, 2048, 4096], P(None, 'row', 'col'), may hold values from -6 to 6
- cotangent: float32 [2, 2048, 4096], P(None, 'row', 'col'), may hold values from -6 to 6
- first_kernel: bfloat16 [18, 32], replicated, may hold values from -1.5 to 1.5
- first_bias: float32 [32], replicated, may hold values from -1 to 1
- second_kernel: bfloat16 [32, 18], replicated, may hold values from -1.5 to 1.5
Outputs:
- grad_state: float32 [2, 2048, 4096], P(None, 'row', 'col')
- grad_first: float32 [18, 32], replicated
- grad_second: float32 [32, 18], replicated
- grad_bias: float32 [32], replicated
All inputs are finite; a program needn't handle non-finite values.
Results may differ from a plain program's by a relative error of at most 0.0047.
Values sent between devices are 32-bit elements; how exact they have to be, the bound alone decides.
No kernel may reach another device: no remote copies, remote signals or barrier semaphores. Data moves between devices by JAX's collectives and lax.ppermute only.
A program may use at most 64 MiB of HBM per device.

v0:
```python
import math

import jax
import jax.numpy as jnp
import numpy as np
from jax import lax
from jax.experimental import pallas as pl
from jax.experimental.pallas import tpu as pltpu
from jax.sharding import PartitionSpec as P

NX, NY = 2048, 4096
ROWS, COLS = 8, 32
DEV = ROWS * COLS
FEATS = 32
WIDE = 24
f32, bf16 = jnp.float32, jnp.bfloat16
STEP = 0.1
NT = (((1,), (1,)), ((), ()))
NN = (((1,), (0,)), ((), ()))


def pair(table):
    high = table.astype(jnp.bfloat16)
    low = (table - high.astype(np.float64)).astype(jnp.bfloat16)
    return np.stack([high, low])


def tables():
    index = np.arange(256)
    angle = 2 * np.pi * (np.outer(index, index) % 256) / 256
    dft = np.concatenate([pair(np.cos(angle)), pair(np.sin(angle))])
    small = 2 * np.pi * (np.outer(np.arange(16), np.arange(16)) % 16) / 16
    eye = np.eye(8)
    group = np.concatenate([np.kron(eye, np.cos(small)), np.kron(eye, np.sin(small))], 1)
    twist_y = 2 * np.pi * np.outer(index, np.arange(128) % 16) / NY
    twist_x = 2 * np.pi * np.outer(np.arange(1, 5), index) / NX
    return dict(
        dft=dft,
        group=pair(group),
        twist_y=np.stack([np.cos(twist_y), np.sin(twist_y)]).astype(np.float32),
        twist_x=np.concatenate([np.cos(twist_x), np.sin(twist_x)]).astype(np.float32),
    )


def picks():
    first = np.zeros((18, 256))
    second = np.zeros((18, 256))
    out_first = np.zeros((256, 128))
    out_second = np.zeros((256, 128))
    for a in range(3):
        for b in range(3):
            for c in range(2):
                row = 2 * (3 * a + b) + c
                lane = (2 * a + c) * WIDE
                first[row, lane + b] = 1
                second[row, lane + 2 - b] = 1
                out_first[lane + b, row] = 1
                out_second[lane + 2 - b, 32 + row] = 1
    out_first[6 * WIDE, 18] = 1
    return [x.astype(jnp.bfloat16) for x in (first, second, out_first, out_second)]


def split(values):
    high = values.astype(bf16)
    return high, (values - high.astype(f32)).astype(bf16)


def dot(left, right, dims=NN):
    return lax.dot_general(left, right, dims, preferred_element_type=f32)


def left_dot(table_ref, base, values, dims=NN, keep=None):
    high, low = split(values)
    t_high, t_low = table_ref[base], table_ref[base + 1]
    if keep is not None:
        t_high, t_low = t_high[:, :keep], t_low[:, :keep]
    return dot(t_high, high, dims) + (dot(t_high, low, dims) + dot(t_low, high, dims))


def right_dot(values, table_ref):
    high, low = split(values)
    return dot(high, table_ref[0]) + (dot(low, table_ref[0]) + dot(high, table_ref[1]))


def pack_kernel(cot_ref, state_ref, out_ref):
    for f, ref in enumerate((cot_ref, state_ref)):
        for c in range(2):
            turned = ref[c].T
            row = (2 * f + c) * 16
            for r in range(ROWS):
                out_ref[r, row : row + 16, :] = turned[16 * r : 16 * r + 16]


def ahead_kernel(in_ref, dft_ref, twist_ref, out_ref, low_ref, high_ref):
    u = [in_ref[r, 0:32, :] for r in range(8)]
    root = math.sqrt(0.5)
    a, b, c, d = (u[k] - u[k + 4] for k in range(4))
    e0, e1, e2, e3 = (u[k] + u[k + 4] for k in range(4))
    s0, s1 = e0 + e2, e1 + e3
    parts = [
        (a + root * (b - d), -c - root * (b + d)),
        (e0 - e2, e3 - e1),
        (a - root * (b - d), c - root * (b + d)),
    ]
    reals, imags = [], []
    for k, (re, im) in enumerate(parts):
        cos, sin = twist_ref[k : k + 1, :], twist_ref[4 + k : 5 + k, :]
        reals.append(re * cos + im * sin)
        imags.append(im * cos - re * sin)
    even, odd = s0 + s1, s0 - s1
    zero = jnp.zeros_like(even)
    last_re = odd * twist_ref[3:4, :]
    last_im = -odd * twist_ref[7:8, :]
    stack = jnp.concatenate(
        reals + [even] + imags + [zero] + [zero] * 3 + [last_re] + [zero] * 3 + [last_im], 0
    )
    cosine = left_dot(dft_ref, 0, stack, NT)
    sine = left_dot(dft_ref, 2, stack, NT)
    main_re = cosine[:, 0:128] + sine[:, 128:256]
    main_im = cosine[:, 128:256] - sine[:, 0:128]
    odd_re = cosine[:128, 256:384] + sine[:128, 384:512]
    odd_im = cosine[:128, 384:512] - sine[:128, 256:384]
    lane = lax.broadcasted_iota(jnp.int32, (128, 128), 1)
    row = lax.broadcasted_iota(jnp.int32, (128, 128), 0)
    last = lane >= 96
    edge = last & (row == 0)
    top_re = jnp.where(edge, main_re[128:129], main_re[:128])
    top_im = jnp.where(edge, main_re[0:1], main_im[:128])
    out_ref[pl.ds(0, 128, 2), :] = top_re
    out_ref[pl.ds(1, 128, 2), :] = top_im
    out_ref[pl.ds(256, 128, 2), :] = jnp.where(last, odd_re, main_re[128:])
    out_ref[pl.ds(257, 128, 2), :] = jnp.where(last, odd_im, main_im[128:])
    for r in range(8):
        for ch in range(2):
            row0 = 32 + 16 * ch
            low_ref[2 * ch : 2 * ch + 2, 256 * r : 256 * r + 256] = in_ref[r, row0 : row0 + 2, :]
            high_ref[2 * ch : 2 * ch + 2, 256 * r : 256 * r + 256] = in_ref[
                r, row0 + 14 : row0 + 16, :
            ]


def waves(place):
    lane = lax.broadcasted_iota(jnp.int32, (256, 128), 1)
    row = lax.broadcasted_iota(jnp.int32, (256, 128), 0)
    slot = lane // 32
    plain = 8 * place + slot + 1
    last = jnp.where(place == 0, NX // 2, jnp.where(place < 128, 8 * place, 8 * place - 1020))
    mx = jnp.where(slot == 3, last, plain)
    mx = jnp.where(mx >= NX // 2, mx - NX, mx)
    my = row + 256 * (lane % 16)
    my = jnp.where(my >= NY // 2, my - NY, my)
    kx = mx.astype(f32) * (1.0 / NX)
    ky = my.astype(f32) * (1.0 / NY)
    inverse = 1.0 / (kx * kx + ky * ky)
    cross = jnp.where((mx == -(NX // 2)) | (my == -(NY // 2)), 0.0, kx * ky)
    own = jnp.where((lane & 16) == 0, kx * kx, ky * ky)
    return 1.0 - own * inverse, -cross * inverse, lane


def swap16(values, lane):
    return jnp.where((lane & 16) == 0, pltpu.roll(values, 112, 1), pltpu.roll(values, 16, 1))


def middle_kernel(place_ref, in_ref, dft_ref, group_ref, twist_ref, out_ref):
    place = place_ref[0]
    re, im = in_ref[pl.ds(0, 256, 2), :], in_ref[pl.ds(1, 256, 2), :]
    cos, sin = twist_ref[0], twist_ref[1]
    both = jnp.concatenate([re, im], 1)
    cosine, sine = left_dot(dft_ref, 0, both), left_dot(dft_ref, 2, both)
    f_re, f_im = cosine[:, :128] + sine[:, 128:], cosine[:, 128:] - sine[:, :128]
    t_re, t_im = f_re * cos + f_im * sin, f_im * cos - f_re * sin
    g = right_dot(jnp.concatenate([t_re, t_im], 0), group_ref)
    g_re, g_im = g[:256, :128] + g[256:, 128:], g[256:, :128] - g[:256, 128:]
    keep, mix, lane = waves(place)
    p_re = keep * g_re + mix * swap16(g_re, lane)
    p_im = keep * g_im + mix * swap16(g_im, lane)
    h = right_dot(jnp.concatenate([p_re, p_im], 0), group_ref)
    h_re, h_im = h[:256, :128] - h[256:, 128:], h[256:, :128] + h[:256, 128:]
    t_re, t_im = h_re * cos - h_im * sin, h_im * cos + h_re * sin
    both = jnp.concatenate([t_re, t_im], 1)
    cosine, sine = left_dot(dft_ref, 0, both), left_dot(dft_ref, 2, both)
    scale = 1.0 / (NX * NY)
    o_re = (cosine[:, :128] - sine[:, 128:]) * scale
    o_im = (cosine[:, 128:] + sine[:, :128]) * scale
    sums = jnp.sum(im, 0, keepdims=True)
    sums = jnp.where(lane[:1] >= 112, sums, 0.0)
    mean = jnp.sum(sums, 1, keepdims=True) * scale
    zeroth = (lane >= 96) & (place == 0)
    o_im = jnp.where(zeroth, jnp.where(lane >= 112, mean, im * (1.0 / NX)), o_im)
    near = (lane & 8) == 0
    out_ref[pl.ds(0, 256, 4), :] = o_re
    out_ref[pl.ds(1, 256, 4), :] = o_im
    out_ref[pl.ds(2, 256, 4), :] = jnp.where(near, pltpu.roll(o_re, 255, 0), pltpu.roll(o_re, 1, 0))
    out_ref[pl.ds(3, 256, 4), :] = jnp.where(near, pltpu.roll(o_im, 255, 0), pltpu.roll(o_im, 1, 0))


def back_kernel(in_ref, dft_ref, twist_ref, out_ref):
    lane = lax.broadcasted_iota(jnp.int32, (128, 128), 1)
    row = lax.broadcasted_iota(jnp.int32, (128, 128), 0)
    last = lane >= 96
    edge = last & (row == 0)
    mains, odds = [], []
    for k in (0, 2):
        top_re, top_im = in_ref[pl.ds(k, 128, 4), :], in_ref[pl.ds(k + 1, 128, 4), :]
        low_re, low_im = in_ref[pl.ds(512 + k, 128, 4), :], in_ref[pl.ds(513 + k, 128, 4), :]
        nyquist = jnp.where(edge, 0.5 * top_re[0:1], 0.0)
        main_re = jnp.concatenate(
            [jnp.where(edge, 0.5 * top_im, top_re), jnp.where(last, nyquist, low_re)], 0
        )
        main_im = jnp.concatenate(
            [jnp.where(edge, 0.0, top_im), jnp.where(last, 0.0, low_im)], 0
        )
        mains += [main_re, main_im]
        odds += [low_re, low_im]
    main = jnp.concatenate(mains, 1).T
    odd = jnp.concatenate(odds, 1).T
    m_high, m_low = split(main)
    o_high, o_low = split(odd)

    def turn(high, low, base, keep):
        t_high, t_low = dft_ref[base][:keep], dft_ref[base + 1][:keep]
        return dot(high, t_high) + (dot(low, t_high) + dot(high, t_low))

    m_cos, m_sin = turn(m_high, m_low, 0, 256), turn(m_high, m_low, 2, 256)
    o_cos, o_sin = turn(o_high, o_low, 0, 128), turn(o_high, o_low, 2, 128)
    root = math.sqrt(0.5)
    for k in (0, 256):
        re = m_cos[k : k + 128] - m_sin[k + 128 : k + 256]
        im = m_cos[k + 128 : k + 256] + m_sin[k : k + 128]
        last_re = o_cos[k + 96 : k + 128] - o_sin[k + 224 : k + 256]
        last_im = o_cos[k + 224 : k + 256] + o_sin[k + 96 : k + 128]
        w4 = last_re * twist_ref[3:4, :] - last_im * twist_ref[7:8, :]
        w0 = re[96:128]
        ws = []
        for p in range(3):
            cos, sin = twist_ref[p : p + 1, :], twist_ref[4 + p : 5 + p, :]
            r_p, i_p = re[32 * p : 32 * p + 32], im[32 * p : 32 * p + 32]
            ws.append((r_p * cos - i_p * sin, i_p * cos + r_p * sin))
        for r in range(8):
            total = w0 + w4 if r % 2 == 0 else w0 - w4
            for p in range(3):
                turn_by = (r * (p + 1)) % 8
                cos_r = [1.0, root, 0.0, -root, -1.0, -root, 0.0, root][turn_by]
                sin_r = [0.0, root, 1.0, root, 0.0, -root, -1.0, -root][turn_by]
                if cos_r:
                    total = total + cos_r * ws[p][0]
                if sin_r:
                    total = total - sin_r * ws[p][1]
            total = total + total
            lanes = slice(256 * r, 256 * r + 256)
            for ch in range(2):
                if k == 0:
                    out_ref[ch, 2:18, lanes] = total[16 * ch : 16 * ch + 16]
                else:
                    out_ref[ch, 0:2, lanes] = total[16 * ch + 14 : 16 * ch + 16]
                    out_ref[ch, 18:20, lanes] = total[16 * ch : 16 * ch + 2]
                    if r == 0:
                        out_ref[ch, 20:24, :] = jnp.zeros((4, NX), f32)


def closure_kernel(
    proj_ref, own_ref, before_ref, after_ref, first_ref, bias_ref, second_ref,
    pick1_ref, pick2_ref, take1_ref, take2_ref,
    out_ref,
    field_ref, build_ref, state_low, scaled_low, grads, acts, w1_ref, w2_ref,
):
    lane = lax.broadcasted_iota(jnp.int32, (FEATS, 256), 1)
    bias = bias_ref[...]
    bias_high = bias.astype(bf16).astype(f32)
    bias_part = jnp.where(
        lane == 6 * WIDE, bias_high, jnp.where(lane == 6 * WIDE + 1, bias - bias_high, 0.0)
    )
    base1 = dot(first_ref[...].astype(f32).T.astype(bf16), pick1_ref[...])
    base2 = dot(second_ref[...], pick2_ref[...])
    for j in range(18):
        rows = slice(32 * j, 32 * j + 32)
        moved1 = pltpu.roll(base1, j, 1) if j else base1
        moved2 = pltpu.roll(base2, j, 1) if j else base2
        w1_ref[rows, :] = moved1 + bias_part
        w2_ref[rows, :] = moved2.astype(bf16)
    for c in range(2):
        field_ref[c, 20:24, :] = jnp.zeros((4, NX), f32)
        for r in range(8):
            field_ref[c, 2:18, 256 * r : 256 * r + 256] = own_ref[
                r, 32 + 16 * c : 48 + 16 * c, :
            ]
        field_ref[c, 0:2, :] = before_ref[2 * c : 2 * c + 2, :]
        field_ref[c, 18:20, :] = after_ref[2 * c : 2 * c + 2, :]

    def ahead(values):
        return pltpu.roll(values, NX - 1, 1)

    def behind(values):
        return pltpu.roll(values, 1, 1)

    for target, sign in ((state_low, 1), (scaled_low, -1)):
        for c in range(2):
            whole = field_ref[c] if sign == 1 else STEP * proj_ref[c]
            moves = (behind(whole), whole, ahead(whole))[::sign]
            for a in range(3):
                row = (2 * a + c) * WIDE
                build_ref[row : row + WIDE, :] = moves[a]
        build_ref[144:152, :] = jnp.ones((8, NX), f32)
        build_ref[152:160, :] = jnp.zeros((8, NX), f32)
        target[0:160, :] = build_ref[...].astype(bf16)
        target[160:256, :] = jnp.zeros((96, NX), bf16)

    w1 = w1_ref[...]
    w1_low = w1[:, :160].astype(bf16)
    w1_turn = w1.T[:160].astype(bf16)
    w2_low = w2_ref[:, :160]
    size = 256

    def chunk(k, carry):
        cols = pl.ds(pl.multiple_of(k * size, size), size)
        preact = dot(w1_low, state_low[0:160, cols])
        active = jnp.tanh(preact)
        acts[:, cols] = active.astype(bf16)
        back = dot(w2_low, scaled_low[0:160, cols])
        grads[:, cols] = (back * (1.0 - active * active)).astype(bf16)
        build_ref[:, cols] = dot(w1_turn, grads[:, cols])
        return carry

    lax.fori_loop(0, NX // size, chunk, 0)
    first_sums = dot(grads[32:544, :], state_low[...], NT)
    second_sums = dot(acts[32:544, :], scaled_low[...], NT)
    total1 = total2 = plain = jnp.zeros((FEATS, 256), f32)
    for j in range(16):
        rows = slice(32 * j, 32 * j + 32)
        total1 = total1 + pltpu.roll(first_sums[rows], 255 - j, 1)
        total2 = total2 + pltpu.roll(second_sums[rows], 255 - j, 1)
        plain = plain + first_sums[rows]
    total1 = jnp.where(lane >= 6 * WIDE, plain, total1)
    high1, low1 = split(total1)
    high2, low2 = split(total2)
    packed = (dot(high1, take1_ref[...]) + dot(low1, take1_ref[...])) + (
        dot(high2, take2_ref[...]) + dot(low2, take2_ref[...])
    )
    left = packed[0:8] + pltpu.roll(packed[8:16], 64, 1)
    right = packed[16:24] + pltpu.roll(packed[24:32], 64, 1)
    for r in range(8):
        out_ref[r, 32:40, 0:128] = left
        out_ref[r, 32:40, 128:256] = right

    inner, up, down = slice(2, 18), slice(3, 19), slice(1, 17)
    su, sv = field_ref[0, inner, :], field_ref[1, inner, :]
    centre = [STEP * proj_ref[c, inner, :] for c in range(2)]
    coupling = [None, None]
    for c, mine in enumerate((su, sv)):
        along_x = 0.5 * (ahead(mine) - behind(mine))
        along_y = 0.5 * (field_ref[c, up, :] - field_ref[c, down, :])
        coupling[0] = centre[c] * along_x + (coupling[0] if c else 0.0)
        coupling[1] = centre[c] * along_y + (coupling[1] if c else 0.0)
    for c in range(2):
        mine = centre[c]
        above = STEP * proj_ref[c, up, :]
        below = STEP * proj_ref[c, down, :]
        carried = su * mine
        total = 0.5 * (ahead(carried) - behind(carried))
        total = total + 0.5 * (field_ref[1, up, :] * above - field_ref[1, down, :] * below)
        total = total - coupling[c]
        total = total + (ahead(mine) + behind(mine) + above + below - 4.0 * mine)
        total = total + proj_ref[c, inner, :]
        for a, move in enumerate((ahead, None, behind)):
            row = (2 * a + c) * WIDE
            part = build_ref[row + 2 : row + 18, :]
            total = total + (move(part) if move else part)
        for r in range(8):
            out_ref[r, 16 * c : 16 * c + 16, :] = total[:, 256 * r : 256 * r + 256]


def unpack_kernel(in_ref, out_ref, part_ref):
    for c in range(2):
        lines = jnp.concatenate([in_ref[r, 16 * c : 16 * c + 16, :] for r in range(8)], 0)
        out_ref[c] = lines.T
    total = in_ref[0, 32:40, :]
    for r in range(1, 8):
        total = total + in_ref[r, 32:40, :]
    part_ref[...] = jnp.broadcast_to(total[None], (COLS, 8, 256))


def sums_kernel(in_ref, first_ref, second_ref, bias_ref):
    total = in_ref[0]
    for r in range(1, COLS):
        total = total + in_ref[r]
    total = total * (1.0 / math.sqrt(NX * NY))
    left, right = total[:, 0:128], total[:, 128:256]
    whole = jnp.concatenate(
        [left, pltpu.roll(left, 64, 1), right, pltpu.roll(right, 64, 1)], 0
    )
    turned = whole.T
    first_ref[...] = turned[0:18, :]
    bias_ref[...] = turned[18:19, :]
    second_ref[...] = pltpu.roll(whole, 96, 1)[:, 0:18]


def call(kernel, outs, scratch=(), scalars=0, count=0, name=None):
    space = [pl.BlockSpec(memory_space=pltpu.SMEM)] * scalars
    space += [pl.BlockSpec(memory_space=pltpu.VMEM)] * (count - scalars)
    many = isinstance(outs, (list, tuple))
    out_space = pl.BlockSpec(memory_space=pltpu.VMEM)
    return pl.pallas_call(
        kernel,
        out_shape=outs,
        in_specs=space,
        out_specs=[out_space] * len(outs) if many else out_space,
        scratch_shapes=list(scratch),
        compiler_params=pltpu.CompilerParams(vmem_limit_bytes=48 * 2**20),
        name=name,
    )


def shape(*dims, dtype=f32):
    return jax.ShapeDtypeStruct(dims, dtype)


def shards(state, cotangent, first_kernel, first_bias, second_kernel):
    t = tables()
    first_pick, second_pick, first_take, second_take = picks()
    dft = jnp.asarray(t["dft"])
    group = jnp.asarray(t["group"])
    twist_y = jnp.asarray(t["twist_y"])
    twist_x = jnp.asarray(t["twist_x"])
    every = ("col", "row")
    place = (lax.axis_index("col") * ROWS + lax.axis_index("row")).astype(jnp.int32).reshape(1)
    lanes = lax.broadcasted_iota(jnp.int32, (FEATS, 256), 1)
    bias = jnp.where(lanes >= 6 * WIDE, first_bias[:, None], 0.0)

    def exchange(values, axis):
        return lax.all_to_all(values, axis, 0, 0, tiled=True)

    packed = call(pack_kernel, shape(8, 64, 256), count=2, name="pack")(cotangent, state)
    lines = exchange(packed, "row")
    modes, low, high = call(
        ahead_kernel, [shape(512, 128), shape(4, NX), shape(4, NX)], count=3, name="ahead"
    )(lines, dft, twist_x)
    order = [(i % ROWS) * COLS + i // ROWS for i in range(DEV)]
    up = [(order[i], order[(i + 1) % DEV]) for i in range(DEV)]
    before = lax.ppermute(high, ("row", "col"), up)
    after = lax.ppermute(low, ("row", "col"), [(j, i) for i, j in up])
    modes = exchange(modes.reshape(DEV, 2, 128), every).reshape(512, 128)
    modes = call(middle_kernel, shape(1024, 128), scalars=1, count=5, name="middle")(
        place, modes, dft, group, twist_y
    )
    modes = exchange(modes.reshape(DEV, 4, 128), every).reshape(1024, 128)
    projected = call(back_kernel, shape(2, WIDE, NX), count=3, name="back")(modes, dft, twist_x)
    scratch = [
        pltpu.VMEM((2, WIDE, NX), f32),
        pltpu.VMEM((160, NX), f32),
        pltpu.VMEM((256, NX), bf16),
        pltpu.VMEM((256, NX), bf16),
        pltpu.VMEM((576, NX), bf16),
        pltpu.VMEM((576, NX), bf16),
        pltpu.VMEM((576, 256), f32),
        pltpu.VMEM((576, 256), bf16),
    ]
    result = call(closure_kernel, shape(8, 40, 256), scratch, count=11, name="closure")(
        projected, lines, before, after, first_kernel, bias, second_kernel,
        first_pick, second_pick, first_take, second_take,
    )
    result = exchange(result, "row")
    grad_state, part = call(
        unpack_kernel, [shape(2, 256, 128), shape(COLS, 8, 256)], count=1, name="unpack"
    )(result)
    part = exchange(part, "col")
    grad_first, grad_second, grad_bias = call(
        sums_kernel, [shape(18, 32), shape(32, 18), shape(1, 32)], count=1, name="sums"
    )(part)
    return grad_state, grad_first, grad_second, grad_bias.reshape(32)


def solution(mesh):
    placed = (P(None, "row", "col"), P(None, "row", "col"), P(), P(), P())
    return jax.shard_map(
        shards,
        mesh=mesh,
        in_specs=placed,
        out_specs=(P(None, "row", "col"), P(), P(), P()),
        check_vma=False,
    )
```

profile of v0, /device:TPU:1, one launch (start us, length us, event | category | flops | bytes accessed | tf_op | source)
XLA Modules:
  0.0 115.9 jit_solution(4253191241826000648)
XLA Ops:
  0.6 0.9 copy-done.2
  1.6 0.9 copy-done.3
  2.5 0.2 pack.1
  2.7 0.0 copy-start
  2.7 0.0 copy-start.7
  2.8 14.5 %all_to_all.25.in_ref.own_ref = f32[8,64,256]{2,1,0:T(8,128)S(1)} all-to-all(f32[8,64,256]{2,1,0:T(8,128)S(1)} %pack.1), channel_id=1, replica_groups=mesh['row'=8,'col'=32] {'row'}, dimensions={0} | all-to-all | bytes 1048576 | tf_op jit(solution)/shard_map/all_to_all | solution.py:430
  17.3 0.0 copy-done.7
  17.3 1.3 %ahead.1 = (f32[512,128]{1,0:T(8,128)}, f32[4,2048]{1,0:T(4,128)S(1)}, f32[4,2048]{1,0:T(4,128)S(1)}) custom-call(f32[8,64,256]{2,1,0:T(8,128)S(1)} %all_to_all.25.in_ref.own_ref, bf16[4,256,256]{2,1,0:T(8,128)(2,1)S(1)} %copy-done, f32[8,256]{1,0:T(8,128)S(1)} %copy-done.7), custom_call_target="tpu_custom_call" | custom-call | tf_op jit(solution)/shard_map/ahead/pallas_call | solution.py:434
  18.6 14.0 %all-to-all-start.1 = ((f32[256,2,128]{2,1,0:T(2,128)}), f32[256,2,128]{2,1,0:T(2,128)S(1)}, u32[]{:S(2)}, u32[]{:S(2)}) async-start(f32[256,2,128]{2,1,0:T(2,128)} %bitcast.1), calls=%async_computation.1 | async-start | bytes 524288 | tf_op jit(solution)/shard_map/all_to_all | solution.py:430
  32.6 14.6 %all-to-all-done.1 = f32[256,2,128]{2,1,0:T(2,128)S(1)} async-done(((f32[256,2,128]{2,1,0:T(2,128)}), f32[256,2,128]{2,1,0:T(2,128)S(1)}, u32[]{:S(2)}, u32[]{:S(2)}) %all-to-all-start.1) | async-done | bytes 262176 | tf_op jit(solution)/shard_map/all_to_all | solution.py:430
  47.2 2.5 %middle.1 = f32[1024,128]{1,0:T(8,128)} custom-call(s32[1]{0:T(128)} %bitcast.place_ref, f32[512,128]{1,0:T(8,128)S(1)} %bitcast.7, bf16[4,256,256]{2,1,0:T(8,128)(2,1)S(1)} %copy-done, bf16[2,128,256]{2,1,0:T(8,128)(2,1)S(1)} %copy-done.4, f32[2,256,128]{2,1,0:T(8,128)S(1)} %copy-done.1), custom_call_target="tpu_custom_call" | custom-call | tf_op jit(solution)/shard_map/middle/pallas_call | solution.py:442
  49.7 6.2 %all-to-all-start.2 = ((f32[256,4,128]{2,1,0:T(4,128)}), f32[256,4,128]{2,1,0:T(4,128)S(1)}, u32[]{:S(2)}, u32[]{:S(2)}) async-start(f32[256,4,128]{2,1,0:T(4,128)} %bitcast.3), calls=%async_computation.2 | async-start | bytes 1048576 | tf_op jit(solution)/shard_map/all_to_all | solution.py:430
  56.0 0.0 copy-start.12
  56.0 1.5 %collective-permute-start = (f32[4,2048]{1,0:T(4,128)S(1)}, f32[4,2048]{1,0:T(4,128)S(1)}, u32[]{:S(2)}, u32[]{:S(2)}) collective-permute-start(f32[4,2048]{1,0:T(4,128)S(1)} %get-tuple-element.13), channel_id=1, source_target_pairs={{0,32},{32,64},{64,96},{96,128},{128,160},{160,192},{192,224},{224... | collective-permute-start | bytes 98312 | tf_op jit(solution)/shard_map/ppermute | solution.py:439
  57.5 2.6 %collective-permute-start.1 = (f32[4,2048]{1,0:T(4,128)S(1)}, f32[4,2048]{1,0:T(4,128)S(1)}, u32[]{:S(2)}, u32[]{:S(2)}) collective-permute-start(f32[4,2048]{1,0:T(4,128)S(1)} %get-tuple-element.14), channel_id=1, source_target_pairs={{32,0},{64,32},{96,64},{128,96},{160,128},{192,160},{224,192},{1,2... | collective-permute-start | bytes 98312 | tf_op jit(solution)/shard_map/ppermute | solution.py:440
  60.1 0.0 copy-done.12
  60.1 0.1 broadcast_select_fusion.bias_ref
  60.2 0.1 copy.17.second_ref
  60.3 15.9 %all-to-all-done.2 = f32[256,4,128]{2,1,0:T(4,128)S(1)} async-done(((f32[256,4,128]{2,1,0:T(4,128)}), f32[256,4,128]{2,1,0:T(4,128)S(1)}, u32[]{:S(2)}, u32[]{:S(2)}) %all-to-all-start.2) | async-done | bytes 524320 | tf_op jit(solution)/shard_map/all_to_all | solution.py:430
  76.3 0.0 copy-start.10
  76.3 1.2 %back.1.proj_ref = f32[2,24,2048]{2,1,0:T(8,128)S(1)} custom-call(f32[1024,128]{1,0:T(8,128)S(1)} %bitcast.6, bf16[4,256,256]{2,1,0:T(8,128)(2,1)S(1)} %copy-done, f32[8,256]{1,0:T(8,128)S(1)} %copy-done.7), custom_call_target="tpu_custom_call" | custom-call | tf_op jit(solution)/shard_map/back/pallas_call | solution.py:446
  77.5 0.0 collective-permute-done.before_ref
  77.5 0.0 collective-permute-done.1.after_ref
  77.5 0.0 copy-done.5
  77.5 0.0 copy-done.6
  77.5 0.0 copy-done.8
  77.6 7.5 %closure.1 = f32[8,40,256]{2,1,0:T(8,128)S(1)} custom-call(f32[2,24,2048]{2,1,0:T(8,128)S(1)} %back.1.proj_ref, f32[8,64,256]{2,1,0:T(8,128)S(1)} %all_to_all.25.in_ref.own_ref, f32[4,2048]{1,0:T(4,128)S(1)} %collective-permute-done.before_ref, f32[4,2048]{1,0:T(4,128)S(1)} %collective-permute-done.1.after_ref, bf16[18,32]{1,0:T(8,128)(2,1)S(1)} %copy-done.10, ...), custom_call_target="tpu_custom_call" | custom-call | tf_op jit(solution)/shard_map/closure/pallas_call | solution.py:457
  85.0 11.2 %all_to_all.26.in_ref = f32[8,40,256]{2,1,0:T(8,128)S(1)} all-to-all(f32[8,40,256]{2,1,0:T(8,128)S(1)} %closure.1), channel_id=1, replica_groups=mesh['row'=8,'col'=32] {'row'}, dimensions={0} | all-to-all | bytes 655360 | tf_op jit(solution)/shard_map/all_to_all | solution.py:430
  96.2 0.8 unpack.1
  97.0 17.5 %all_to_all.27.in_ref = f32[32,8,256]{2,1,0:T(8,128)S(1)} all-to-all(f32[32,8,256]{2,1,0:T(8,128)S(1)} %get-tuple-element.16), channel_id=1, replica_groups=mesh['row'=8,'col'=32] {'col'}, dimensions={0} | all-to-all | bytes 524288 | tf_op jit(solution)/shard_map/all_to_all | solution.py:430
  114.5 0.8 sums.1
  115.3 0.7 copy.18
  (16 shorter events, 0.0 us)
Async XLA Ops:
  0.6 1.0 copy-start.2
  1.6 0.9 copy-start.3
  2.7 14.5 %copy-start = (bf16[4,256,256]{2,1,0:T(8,128)(2,1)S(1)}, bf16[4,256,256]{2,1,0:T(8,128)(2,1)}, u32[]{:S(2)}) copy-start(bf16[4,256,256]{2,1,0:T(8,128)(2,1)} %constant.31.clone.dft_ref) | copy-start | bytes 1572868
  2.7 14.5 %copy-start.7 = (f32[8,256]{1,0:T(8,128)S(1)}, f32[8,256]{1,0:T(8,128)}, u32[]{:S(2)}) copy-start(f32[8,256]{1,0:T(8,128)} %constant.34.clone.twist_ref) | copy-start | bytes 24580
  18.6 28.6 %copy-start.1 = (f32[2,256,128]{2,1,0:T(8,128)S(1)}, f32[2,256,128]{2,1,0:T(8,128)}, u32[]{:S(2)}) copy-start(f32[2,256,128]{2,1,0:T(8,128)} %constant.33.clone.twist_ref) | copy-start | bytes 786436
  18.6 28.6 %copy-start.4 = (bf16[2,128,256]{2,1,0:T(8,128)(2,1)S(1)}, bf16[2,128,256]{2,1,0:T(8,128)(2,1)}, u32[]{:S(2)}) copy-start(bf16[2,128,256]{2,1,0:T(8,128)(2,1)} %constant.32.clone.group_ref) | copy-start | bytes 393220
  18.6 28.6 %all-to-all-start.1 = ((f32[256,2,128]{2,1,0:T(2,128)}), f32[256,2,128]{2,1,0:T(2,128)S(1)}, u32[]{:S(2)}, u32[]{:S(2)}) async-start(f32[256,2,128]{2,1,0:T(2,128)} %bitcast.1), calls=%async_computation.1 | async-start | bytes 524288 | tf_op jit(solution)/shard_map/all_to_all | solution.py:430
  49.7 26.5 %all-to-all-start.2 = ((f32[256,4,128]{2,1,0:T(4,128)}), f32[256,4,128]{2,1,0:T(4,128)S(1)}, u32[]{:S(2)}, u32[]{:S(2)}) async-start(f32[256,4,128]{2,1,0:T(4,128)} %bitcast.3), calls=%async_computation.2 | async-start | bytes 1048576 | tf_op jit(solution)/shard_map/all_to_all | solution.py:430
  56.0 4.2 %copy-start.12 = (f32[32]{0:T(128)S(1)}, f32[32]{0:T(128)}, u32[]{:S(2)}) copy-start(f32[32]{0:T(128)} %param.16) | copy-start | bytes 388
  56.0 21.5 %collective-permute-start = (f32[4,2048]{1,0:T(4,128)S(1)}, f32[4,2048]{1,0:T(4,128)S(1)}, u32[]{:S(2)}, u32[]{:S(2)}) collective-permute-start(f32[4,2048]{1,0:T(4,128)S(1)} %get-tuple-element.13), channel_id=1, source_target_pairs={{0,32},{32,64},{64,96},{96,128},{128,160},{160,192},{192,224},{224... | collective-permute-start | bytes 98312 | tf_op jit(solution)/shard_map/ppermute | solution.py:439
  57.5 2.7 %copy-start.11 = (bf16[32,18]{0,1:T(8,128)(2,1)S(1)}, bf16[32,18]{0,1:T(8,128)(2,1)}, u32[]{:S(2)}) copy-start(bf16[32,18]{0,1:T(8,128)(2,1)} %param.17) | copy-start | bytes 3460
  57.5 20.0 %collective-permute-start.1 = (f32[4,2048]{1,0:T(4,128)S(1)}, f32[4,2048]{1,0:T(4,128)S(1)}, u32[]{:S(2)}, u32[]{:S(2)}) collective-permute-start(f32[4,2048]{1,0:T(4,128)S(1)} %get-tuple-element.14), channel_id=1, source_target_pairs={{32,0},{64,32},{96,64},{128,96},{160,128},{192,160},{224,192},{1,2... | collective-permute-start | bytes 98312 | tf_op jit(solution)/shard_map/ppermute | solution.py:440
  76.2 1.3 %copy-start.5 = (bf16[256,128]{1,0:T(8,128)(2,1)S(1)}, bf16[256,128]{1,0:T(8,128)(2,1)}, u32[]{:S(2)}) copy-start(bf16[256,128]{1,0:T(8,128)(2,1)} %constant.37.clone.take1_ref) | copy-start | bytes 196612
  76.2 1.3 %copy-start.6 = (bf16[256,128]{1,0:T(8,128)(2,1)S(1)}, bf16[256,128]{1,0:T(8,128)(2,1)}, u32[]{:S(2)}) copy-start(bf16[256,128]{1,0:T(8,128)(2,1)} %constant.38.clone.take2_ref) | copy-start | bytes 196612
  76.3 1.3 %copy-start.8 = (bf16[18,256]{1,0:T(8,128)(2,1)S(1)}, bf16[18,256]{1,0:T(8,128)(2,1)}, u32[]{:S(2)}) copy-start(bf16[18,256]{1,0:T(8,128)(2,1)} %constant.35.clone.pick1_ref) | copy-start | bytes 27652
  76.3 1.3 %copy-start.9 = (bf16[18,256]{1,0:T(8,128)(2,1)S(1)}, bf16[18,256]{1,0:T(8,128)(2,1)}, u32[]{:S(2)}) copy-start(bf16[18,256]{1,0:T(8,128)(2,1)} %constant.36.clone.pick2_ref) | copy-start | bytes 27652
  76.3 1.3 %copy-start.10 = (bf16[18,32]{1,0:T(8,128)(2,1)S(1)}, bf16[18,32]{1,0:T(8,128)(2,1)}, u32[]{:S(2)}) copy-start(bf16[18,32]{1,0:T(8,128)(2,1)} %first_ref.1) | copy-start | bytes 3460
where the time goes:
time: 116 us
  blocking collectives  43.1 us (37%)
  waiting for transfers between devices  30.6 us (26%)
  starting transfers between devices  24.3 us (21%)
  Pallas kernels  14.3 us (12%)
  local copies, waits for them, and re-layouts  2.72 us (2%)
    all_to_all x3, blocking collectives, exchange(): return lax.all_to_all(values, axis, 0, 0, tiled=True)  43.1 us
    all_to_all x2, waiting for transfers between devices, exchange(): return lax.all_to_all(values, axis, 0, 0, tiled=True)  30.5 us
    all_to_all x2, starting transfers between devices, exchange(): return lax.all_to_all(values, axis, 0, 0, tiled=True)  20.2 us
    pallas_call x1, Pallas kernels, shards(): call(closure_kernel, shape(8, 40, 256), scratch, count=11, name='closure')  7.48 us
    unnamed x28, local copies, waits for them, and re-layouts  2.72 us
    ppermute x1, starting transfers between devices, shards(): after = lax.ppermute(low, ('row', 'col'), [(j, i) for i, j in up])  2.63 us
    pallas_call x1, Pallas kernels, shards(): call(middle_kernel, shape(1024, 128), scalars=1, count=5, name='middle')  2.52 us
  transfers between devices with their start and end apart: 4, of which 2 were waited for; matrix products, arithmetic and copies ran while one was open for 0% of the time, Pallas kernels for 1%

commit v1 on v0

--- a/solution.py
+++ b/solution.py
@@ -55,7 +55,7 @@
                 first[row, lane + b] = 1
                 second[row, lane + 2 - b] = 1
                 out_first[lane + b, row] = 1
-                out_second[lane + 2 - b, 32 + row] = 1
+                out_second[lane + 2 - b, 19 + row] = 1
     out_first[6 * WIDE, 18] = 1
     return [x.astype(jnp.bfloat16) for x in (first, second, out_first, out_second)]
 
@@ -82,16 +82,39 @@
     return dot(high, table_ref[0]) + (dot(low, table_ref[0]) + dot(high, table_ref[1]))
 
 
-def pack_kernel(cot_ref, state_ref, out_ref):
+def far(values):
+    return pltpu.with_memory_space_constraint(values, pltpu.HBM)
+
+
+def fetch(sources, targets, sems):
+    copies = [
+        pltpu.make_async_copy(source, target, sems.at[k])
+        for k, (source, target) in enumerate(zip(sources, targets))
+    ]
+    for copy in copies:
+        copy.start()
+    return copies
+
+
+def pack_kernel(cot_ref, state_ref, out_ref, buffer_ref, sems):
+    copies = []
     for f, ref in enumerate((cot_ref, state_ref)):
         for c in range(2):
-            turned = ref[c].T
-            row = (2 * f + c) * 16
-            for r in range(ROWS):
-                out_ref[r, row : row + 16, :] = turned[16 * r : 16 * r + 16]
-
-
-def ahead_kernel(in_ref, dft_ref, twist_ref, out_ref, low_ref, high_ref):
+            k = 2 * f + c
+            copies.append(pltpu.make_async_copy(ref.at[c], buffer_ref.at[k], sems.at[k]))
+    for copy in copies:
+        copy.start()
+    for k, copy in enumerate(copies):
+        copy.wait()
+        turned = buffer_ref[k].T
+        for r in range(ROWS):
+            out_ref[r, 16 * k : 16 * k + 16, :] = turned[16 * r : 16 * r + 16]
+
+
+def ahead_kernel(
+    dft_far, twist_far, in_ref, out_ref, low_ref, high_ref, dft_ref, twist_ref, sems
+):
+    copies = fetch((twist_far, dft_far), (twist_ref, dft_ref), sems)
     u = [in_ref[r, 0:32, :] for r in range(8)]
     root = math.sqrt(0.5)
     a, b, c, d = (u[k] - u[k + 4] for k in range(4))
@@ -102,6 +125,7 @@
         (e0 - e2, e3 - e1),
         (a - root * (b - d), c - root * (b + d)),
     ]
+    copies[0].wait()
     reals, imags = [], []
     for k, (re, im) in enumerate(parts):
         cos, sin = twist_ref[k : k + 1, :], twist_ref[4 + k : 5 + k, :]
@@ -114,6 +138,7 @@
     stack = jnp.concatenate(
         reals + [even] + imags + [zero] + [zero] * 3 + [last_re] + [zero] * 3 + [last_im], 0
     )
+    copies[1].wait()
     cosine = left_dot(dft_ref, 0, stack, NT)
     sine = left_dot(dft_ref, 2, stack, NT)
     main_re = cosine[:, 0:128] + sine[:, 128:256]
@@ -139,7 +164,8 @@
             ]
 
 
-def waves(place):
+def waves_kernel(place_ref, keep_ref, mix_ref):
+    place = place_ref[0]
     lane = lax.broadcasted_iota(jnp.int32, (256, 128), 1)
     row = lax.broadcasted_iota(jnp.int32, (256, 128), 0)
     slot = lane // 32
@@ -154,24 +180,33 @@
     inverse = 1.0 / (kx * kx + ky * ky)
     cross = jnp.where((mx == -(NX // 2)) | (my == -(NY // 2)), 0.0, kx * ky)
     own = jnp.where((lane & 16) == 0, kx * kx, ky * ky)
-    return 1.0 - own * inverse, -cross * inverse, lane
+    keep_ref[...] = 1.0 - own * inverse
+    mix_ref[...] = -cross * inverse
 
 
 def swap16(values, lane):
     return jnp.where((lane & 16) == 0, pltpu.roll(values, 112, 1), pltpu.roll(values, 16, 1))
 
 
-def middle_kernel(place_ref, in_ref, dft_ref, group_ref, twist_ref, out_ref):
+def middle_kernel(
+    place_ref, dft_far, twist_far, group_far, in_ref, keep_ref, mix_ref, out_ref,
+    dft_ref, twist_ref, group_ref, sems,
+):
+    copies = fetch((dft_far, twist_far, group_far), (dft_ref, twist_ref, group_ref), sems)
     place = place_ref[0]
     re, im = in_ref[pl.ds(0, 256, 2), :], in_ref[pl.ds(1, 256, 2), :]
-    cos, sin = twist_ref[0], twist_ref[1]
     both = jnp.concatenate([re, im], 1)
+    copies[0].wait()
     cosine, sine = left_dot(dft_ref, 0, both), left_dot(dft_ref, 2, both)
     f_re, f_im = cosine[:, :128] + sine[:, 128:], cosine[:, 128:] - sine[:, :128]
+    copies[1].wait()
+    copies[2].wait()
+    cos, sin = twist_ref[0], twist_ref[1]
     t_re, t_im = f_re * cos + f_im * sin, f_im * cos - f_re * sin
     g = right_dot(jnp.concatenate([t_re, t_im], 0), group_ref)
     g_re, g_im = g[:256, :128] + g[256:, 128:], g[256:, :128] - g[:256, 128:]
-    keep, mix, lane = waves(place)
+    keep, mix = keep_ref[...], mix_ref[...]
+    lane = lax.broadcasted_iota(jnp.int32, (256, 128), 1)
     p_re = keep * g_re + mix * swap16(g_re, lane)
     p_im = keep * g_im + mix * swap16(g_im, lane)
     h = right_dot(jnp.concatenate([p_re, p_im], 0), group_ref)
@@ -188,47 +223,70 @@
     zeroth = (lane >= 96) & (place == 0)
     o_im = jnp.where(zeroth, jnp.where(lane >= 112, mean, im * (1.0 / NX)), o_im)
     near = (lane & 8) == 0
-    out_ref[pl.ds(0, 256, 4), :] = o_re
-    out_ref[pl.ds(1, 256, 4), :] = o_im
-    out_ref[pl.ds(2, 256, 4), :] = jnp.where(near, pltpu.roll(o_re, 255, 0), pltpu.roll(o_re, 1, 0))
-    out_ref[pl.ds(3, 256, 4), :] = jnp.where(near, pltpu.roll(o_im, 255, 0), pltpu.roll(o_im, 1, 0))
-
-
-def back_kernel(in_ref, dft_ref, twist_ref, out_ref):
+    outer = ((lane + 2) & 15) < 4
+
+    def beside(values):
+        return jnp.where(near, pltpu.roll(values, 255, 0), pltpu.roll(values, 1, 0))
+
+    out_ref[pl.ds(0, 256, 3), :] = o_re
+    out_ref[pl.ds(1, 256, 3), :] = o_im
+    edge_im = beside(o_im)
+    edge_im = jnp.where(near, pltpu.roll(edge_im, 4, 1), pltpu.roll(edge_im, 124, 1))
+    out_ref[pl.ds(2, 256, 3), :] = jnp.where(outer, beside(o_re), edge_im)
+
+
+def back_part(in_ref, dft_ref, twist_ref, out_ref, copies):
     lane = lax.broadcasted_iota(jnp.int32, (128, 128), 1)
     row = lax.broadcasted_iota(jnp.int32, (128, 128), 0)
     last = lane >= 96
     edge = last & (row == 0)
-    mains, odds = [], []
-    for k in (0, 2):
-        top_re, top_im = in_ref[pl.ds(k, 128, 4), :], in_ref[pl.ds(k + 1, 128, 4), :]
-        low_re, low_im = in_ref[pl.ds(512 + k, 128, 4), :], in_ref[pl.ds(513 + k, 128, 4), :]
-        nyquist = jnp.where(edge, 0.5 * top_re[0:1], 0.0)
-        main_re = jnp.concatenate(
+    near = (lane & 8) == 0
+    outer = ((lane + 2) & 15) < 4
+    top_re, top_im, top_h = (in_ref[pl.ds(k, 128, 3), :] for k in range(3))
+    low_re, low_im, low_h = (in_ref[pl.ds(384 + k, 128, 3), :] for k in range(3))
+    head = top_h[0:1]
+    head_im = jnp.where(near[0:1], pltpu.roll(head, 124, 1), pltpu.roll(head, 4, 1))
+    half_im = jnp.where(outer[0:1], 0.5 * head_im, 0.0)
+    half_re = jnp.where(outer[0:1], 0.5 * head, 0.0)
+    nyquist = jnp.where(edge, 0.5 * top_re[0:1], 0.0)
+    mains = [
+        jnp.concatenate(
             [jnp.where(edge, 0.5 * top_im, top_re), jnp.where(last, nyquist, low_re)], 0
-        )
-        main_im = jnp.concatenate(
-            [jnp.where(edge, 0.0, top_im), jnp.where(last, 0.0, low_im)], 0
-        )
-        mains += [main_re, main_im]
-        odds += [low_re, low_im]
-    main = jnp.concatenate(mains, 1).T
-    odd = jnp.concatenate(odds, 1).T
-    m_high, m_low = split(main)
-    o_high, o_low = split(odd)
+        ),
+        jnp.concatenate([jnp.where(edge, 0.0, top_im), jnp.where(last, 0.0, low_im)], 0),
+        jnp.concatenate(
+            [
+                jnp.where(edge, half_im, top_h),
+                jnp.where(last, jnp.where(edge, half_re, 0.0), low_h),
+            ],
+            0,
+        ),
+    ]
+    m_high, m_low = split(jnp.concatenate(mains, 1).T)
+    o_high, o_low = split(jnp.concatenate([low_re, low_im, low_h], 1).T)
 
     def turn(high, low, base, keep):
         t_high, t_low = dft_ref[base][:keep], dft_ref[base + 1][:keep]
         return dot(high, t_high) + (dot(low, t_high) + dot(high, t_low))
 
+    for copy in copies:
+        copy.wait()
     m_cos, m_sin = turn(m_high, m_low, 0, 256), turn(m_high, m_low, 2, 256)
     o_cos, o_sin = turn(o_high, o_low, 0, 128), turn(o_high, o_low, 2, 128)
     root = math.sqrt(0.5)
+    near_row = (lax.broadcasted_iota(jnp.int32, (128, 256), 0) & 8) == 0
+
+    def imag_rows(values):
+        return jnp.where(near_row, pltpu.roll(values, 124, 0), pltpu.roll(values, 4, 0))
+
     for k in (0, 256):
-        re = m_cos[k : k + 128] - m_sin[k + 128 : k + 256]
-        im = m_cos[k + 128 : k + 256] + m_sin[k : k + 128]
-        last_re = o_cos[k + 96 : k + 128] - o_sin[k + 224 : k + 256]
-        last_im = o_cos[k + 224 : k + 256] + o_sin[k + 96 : k + 128]
+        if k == 0:
+            re, im = m_cos[0:128] - m_sin[128:256], m_cos[128:256] + m_sin[0:128]
+            last_re, last_im = o_cos[96:128] - o_sin[224:256], o_cos[224:256] + o_sin[96:128]
+        else:
+            m_c, m_s, o_c, o_s = (v[256:384] for v in (m_cos, m_sin, o_cos, o_sin))
+            re, im = m_c - imag_rows(m_s), imag_rows(m_c) + m_s
+            last_re, last_im = (o_c - imag_rows(o_s))[96:], (imag_rows(o_c) + o_s)[96:]
         w4 = last_re * twist_ref[3:4, :] - last_im * twist_ref[7:8, :]
         w0 = re[96:128]
         ws = []
@@ -258,11 +316,34 @@
                         out_ref[ch, 20:24, :] = jnp.zeros((4, NX), f32)
 
 
-def closure_kernel(
-    proj_ref, own_ref, before_ref, after_ref, first_ref, bias_ref, second_ref,
-    pick1_ref, pick2_ref, take1_ref, take2_ref,
-    out_ref,
-    field_ref, build_ref, state_low, scaled_low, grads, acts, w1_ref, w2_ref,
+def ahead_of(values):
+    return pltpu.roll(values, NX - 1, 1)
+
+
+def behind_of(values):
+    return pltpu.roll(values, 1, 1)
+
+
+def fill_taps(build_ref, target, fields, sign):
+    for c in range(2):
+        whole = fields[c]
+        moves = (behind_of(whole), whole, ahead_of(whole))[::sign]
+        for a in range(3):
+            row = (2 * a + c) * WIDE
+            build_ref[row : row + WIDE, :] = moves[a]
+    build_ref[144:152, :] = jnp.ones((8, NX), f32)
+    build_ref[152:160, :] = jnp.zeros((8, NX), f32)
+    target[0:160, :] = build_ref[...].astype(bf16)
+    target[160:256, :] = jnp.zeros((96, NX), bf16)
+
+
+CHUNK = 256
+
+
+def state_kernel(
+    own_ref, before_ref, after_ref, first_ref, bias_ref, second_ref, pick1_ref, pick2_ref,
+    field_ref, slope_ref, state_low, acts, acts_turn, w2_ref, turn_ref,
+    build_ref, w1_ref,
 ):
     lane = lax.broadcasted_iota(jnp.int32, (FEATS, 256), 1)
     bias = bias_ref[...]
@@ -286,44 +367,60 @@
             ]
         field_ref[c, 0:2, :] = before_ref[2 * c : 2 * c + 2, :]
         field_ref[c, 18:20, :] = after_ref[2 * c : 2 * c + 2, :]
-
-    def ahead(values):
-        return pltpu.roll(values, NX - 1, 1)
-
-    def behind(values):
-        return pltpu.roll(values, 1, 1)
-
-    for target, sign in ((state_low, 1), (scaled_low, -1)):
-        for c in range(2):
-            whole = field_ref[c] if sign == 1 else STEP * proj_ref[c]
-            moves = (behind(whole), whole, ahead(whole))[::sign]
-            for a in range(3):
-                row = (2 * a + c) * WIDE
-                build_ref[row : row + WIDE, :] = moves[a]
-        build_ref[144:152, :] = jnp.ones((8, NX), f32)
-        build_ref[152:160, :] = jnp.zeros((8, NX), f32)
-        target[0:160, :] = build_ref[...].astype(bf16)
-        target[160:256, :] = jnp.zeros((96, NX), bf16)
-
+    fill_taps(build_ref, state_low, (field_ref[0], field_ref[1]), 1)
+    for c in range(2):
+        mine = field_ref[c, 2:18, :]
+        slope_ref[2 * c] = 0.5 * (ahead_of(mine) - behind_of(mine))
+        slope_ref[2 * c + 1] = 0.5 * (field_ref[c, 3:19, :] - field_ref[c, 1:17, :])
     w1 = w1_ref[...]
+    turn_ref[...] = w1.T[:160].astype(bf16)
     w1_low = w1[:, :160].astype(bf16)
-    w1_turn = w1.T[:160].astype(bf16)
+
+    def chunk(k, carry):
+        cols = pl.ds(pl.multiple_of(k * CHUNK, CHUNK), CHUNK)
+        active = jnp.tanh(dot(w1_low, state_low[0:160, cols]))
+        acts[:, cols] = active[32:544].astype(bf16)
+        acts_turn[:, cols] = 1.0 - active * active
+        return carry
+
+    lax.fori_loop(0, NX // CHUNK, chunk, 0)
+
+
+def closure_kernel(
+    dft_far, twist_far, w2_far, acts_turn_far, turn_far, state_far, acts_far,
+    field_far, slope_far, take1_far, take2_far, in_ref,
+    out_ref,
+    dft_ref, twist_ref, w2_ref, acts_turn, turn_ref, state_low, acts,
+    field_ref, slope_ref, take1_ref, take2_ref, sems,
+    proj_ref, build_ref, scaled_low, grads,
+):
+    copies = fetch(
+        (dft_far, twist_far, w2_far, acts_turn_far, turn_far, state_far, acts_far,
+         field_far, slope_far, take1_far, take2_far),
+        (dft_ref, twist_ref, w2_ref, acts_turn, turn_ref, state_low, acts,
+         field_ref, slope_ref, take1_ref, take2_ref),
+        sems,
+    )
+    back_part(in_ref, dft_ref, twist_ref, proj_ref, copies[:2])
+    fill_taps(build_ref, scaled_low, (STEP * proj_ref[0], STEP * proj_ref[1]), -1)
+    for copy in copies[2:5]:
+        copy.wait()
     w2_low = w2_ref[:, :160]
-    size = 256
+    w1_turn = turn_ref[...]
 
     def chunk(k, carry):
-        cols = pl.ds(pl.multiple_of(k * size, size), size)
-        preact = dot(w1_low, state_low[0:160, cols])
-        active = jnp.tanh(preact)
-        acts[:, cols] = active.astype(bf16)
+        cols = pl.ds(pl.multiple_of(k * CHUNK, CHUNK), CHUNK)
         back = dot(w2_low, scaled_low[0:160, cols])
-        grads[:, cols] = (back * (1.0 - active * active)).astype(bf16)
+        grads[:, cols] = (back * acts_turn[:, cols]).astype(bf16)
         build_ref[:, cols] = dot(w1_turn, grads[:, cols])
         return carry
 
-    lax.fori_loop(0, NX // size, chunk, 0)
+    lax.fori_loop(0, NX // CHUNK, chunk, 0)
+    for copy in copies[5:]:
+        copy.wait()
     first_sums = dot(grads[32:544, :], state_low[...], NT)
-    second_sums = dot(acts[32:544, :], scaled_low[...], NT)
+    second_sums = dot(acts[...], scaled_low[...], NT)
+    lane = lax.broadcasted_iota(jnp.int32, (FEATS, 256), 1)
     total1 = total2 = plain = jnp.zeros((FEATS, 256), f32)
     for j in range(16):
         rows = slice(32 * j, 32 * j + 32)
@@ -336,32 +433,29 @@
     packed = (dot(high1, take1_ref[...]) + dot(low1, take1_ref[...])) + (
         dot(high2, take2_ref[...]) + dot(low2, take2_ref[...])
     )
-    left = packed[0:8] + pltpu.roll(packed[8:16], 64, 1)
-    right = packed[16:24] + pltpu.roll(packed[24:32], 64, 1)
+    turned = jnp.concatenate([packed, jnp.zeros((96, 128), f32)], 0).T
+    ten = turned[0:10]
+    for g in range(1, 4):
+        ten = ten + pltpu.roll(turned[10 * g : 10 * g + 10], 32 * g, 1)
     for r in range(8):
-        out_ref[r, 32:40, 0:128] = left
-        out_ref[r, 32:40, 128:256] = right
+        out_ref[r, 32:40, 0:128] = ten[0:8]
+        out_ref[r, 32:34, 128:256] = ten[8:10]
+        out_ref[r, 34:40, 128:256] = jnp.zeros((6, 128), f32)
 
     inner, up, down = slice(2, 18), slice(3, 19), slice(1, 17)
-    su, sv = field_ref[0, inner, :], field_ref[1, inner, :]
+    su = field_ref[0, inner, :]
     centre = [STEP * proj_ref[c, inner, :] for c in range(2)]
-    coupling = [None, None]
-    for c, mine in enumerate((su, sv)):
-        along_x = 0.5 * (ahead(mine) - behind(mine))
-        along_y = 0.5 * (field_ref[c, up, :] - field_ref[c, down, :])
-        coupling[0] = centre[c] * along_x + (coupling[0] if c else 0.0)
-        coupling[1] = centre[c] * along_y + (coupling[1] if c else 0.0)
     for c in range(2):
         mine = centre[c]
         above = STEP * proj_ref[c, up, :]
         below = STEP * proj_ref[c, down, :]
         carried = su * mine
-        total = 0.5 * (ahead(carried) - behind(carried))
+        total = 0.5 * (ahead_of(carried) - behind_of(carried))
         total = total + 0.5 * (field_ref[1, up, :] * above - field_ref[1, down, :] * below)
-        total = total - coupling[c]
-        total = total + (ahead(mine) + behind(mine) + above + below - 4.0 * mine)
+        total = total - (centre[0] * slope_ref[c] + centre[1] * slope_ref[2 + c])
+        total = total + (ahead_of(mine) + behind_of(mine) + above + below - 4.0 * mine)
         total = total + proj_ref[c, inner, :]
-        for a, move in enumerate((ahead, None, behind)):
+        for a, move in enumerate((ahead_of, None, behind_of)):
             row = (2 * a + c) * WIDE
             part = build_ref[row + 2 : row + 18, :]
             total = total + (move(part) if move else part)
@@ -370,33 +464,35 @@
 
 
 def unpack_kernel(in_ref, out_ref, part_ref):
+    total = in_ref[0, 32:40, :]
+    for r in range(1, 8):
+        total = total + in_ref[r, 32:40, :]
+    ten = jnp.concatenate([total[:, 0:128], total[0:2, 128:256]], 0)
+    for d in range(COLS):
+        part_ref[10 * d : 10 * d + 10, :] = ten
     for c in range(2):
         lines = jnp.concatenate([in_ref[r, 16 * c : 16 * c + 16, :] for r in range(8)], 0)
         out_ref[c] = lines.T
-    total = in_ref[0, 32:40, :]
-    for r in range(1, 8):
-        total = total + in_ref[r, 32:40, :]
-    part_ref[...] = jnp.broadcast_to(total[None], (COLS, 8, 256))
 
 
 def sums_kernel(in_ref, first_ref, second_ref, bias_ref):
-    total = in_ref[0]
-    for r in range(1, COLS):
-        total = total + in_ref[r]
+    total = in_ref[0:10, :]
+    for d in range(1, COLS):
+        total = total + in_ref[10 * d : 10 * d + 10, :]
     total = total * (1.0 / math.sqrt(NX * NY))
-    left, right = total[:, 0:128], total[:, 128:256]
-    whole = jnp.concatenate(
-        [left, pltpu.roll(left, 64, 1), right, pltpu.roll(right, 64, 1)], 0
-    )
-    turned = whole.T
-    first_ref[...] = turned[0:18, :]
-    bias_ref[...] = turned[18:19, :]
-    second_ref[...] = pltpu.roll(whole, 96, 1)[:, 0:18]
-
-
-def call(kernel, outs, scratch=(), scalars=0, count=0, name=None):
+    moved = [total] + [pltpu.roll(total, 128 - 32 * g, 1) for g in range(1, 4)]
+    first_ref[0:10, :] = moved[0][:, 0:32]
+    first_ref[10:18, :] = moved[1][0:8, 0:32]
+    bias_ref[...] = moved[1][8:9, 0:32]
+    second_ref[0:1, :] = moved[1][9:10, 0:32]
+    second_ref[1:11, :] = moved[2][:, 0:32]
+    second_ref[11:18, :] = moved[3][0:7, 0:32]
+
+
+def call(kernel, outs, scratch=(), scalars=0, count=0, name=None, remote=0, mib=8):
     space = [pl.BlockSpec(memory_space=pltpu.SMEM)] * scalars
-    space += [pl.BlockSpec(memory_space=pltpu.VMEM)] * (count - scalars)
+    space += [pl.BlockSpec(memory_space=pltpu.HBM)] * remote
+    space += [pl.BlockSpec(memory_space=pltpu.VMEM)] * (count - scalars - remote)
     many = isinstance(outs, (list, tuple))
     out_space = pl.BlockSpec(memory_space=pltpu.VMEM)
     return pl.pallas_call(
@@ -405,7 +501,7 @@
         in_specs=space,
         out_specs=[out_space] * len(outs) if many else out_space,
         scratch_shapes=list(scratch),
-        compiler_params=pltpu.CompilerParams(vmem_limit_bytes=48 * 2**20),
+        compiler_params=pltpu.CompilerParams(vmem_limit_bytes=mib * 2**20),
         name=name,
     )
 
@@ -417,10 +513,10 @@
 def shards(state, cotangent, first_kernel, first_bias, second_kernel):
     t = tables()
     first_pick, second_pick, first_take, second_take = picks()
-    dft = jnp.asarray(t["dft"])
-    group = jnp.asarray(t["group"])
-    twist_y = jnp.asarray(t["twist_y"])
-    twist_x = jnp.asarray(t["twist_x"])
+    dft, group, twist_y, twist_x = (
+        far(jnp.asarray(t[k])) for k in ("dft", "group", "twist_y", "twist_x")
+    )
+    dma = lambda count: pltpu.SemaphoreType.DMA((count,))
     every = ("col", "row")
     place = (lax.axis_index("col") * ROWS + lax.axis_index("row")).astype(jnp.int32).reshape(1)
     lanes = lax.broadcasted_iota(jnp.int32, (FEATS, 256), 1)
@@ -429,44 +525,68 @@
     def exchange(values, axis):
         return lax.all_to_all(values, axis, 0, 0, tiled=True)
 
-    packed = call(pack_kernel, shape(8, 64, 256), count=2, name="pack")(cotangent, state)
+    space = [pltpu.VMEM((4, 256, 128), f32), pltpu.SemaphoreType.DMA((4,))]
+    packed = call(pack_kernel, shape(8, 64, 256), space, count=2, name="pack", remote=2)(
+        far(cotangent), far(state)
+    )
     lines = exchange(packed, "row")
     modes, low, high = call(
-        ahead_kernel, [shape(512, 128), shape(4, NX), shape(4, NX)], count=3, name="ahead"
-    )(lines, dft, twist_x)
+        ahead_kernel, [shape(512, 128), shape(4, NX), shape(4, NX)],
+        [pltpu.VMEM((4, 256, 256), bf16), pltpu.VMEM((8, 256), f32), dma(2)],
+        count=3, remote=2, name="ahead",
+    )(dft, twist_x, lines)
     order = [(i % ROWS) * COLS + i // ROWS for i in range(DEV)]
     up = [(order[i], order[(i + 1) % DEV]) for i in range(DEV)]
     before = lax.ppermute(high, ("row", "col"), up)
     after = lax.ppermute(low, ("row", "col"), [(j, i) for i, j in up])
     modes = exchange(modes.reshape(DEV, 2, 128), every).reshape(512, 128)
-    modes = call(middle_kernel, shape(1024, 128), scalars=1, count=5, name="middle")(
-        place, modes, dft, group, twist_y
-    )
-    modes = exchange(modes.reshape(DEV, 4, 128), every).reshape(1024, 128)
-    projected = call(back_kernel, shape(2, WIDE, NX), count=3, name="back")(modes, dft, twist_x)
-    scratch = [
+    keep, mix = call(
+        waves_kernel, [shape(256, 128), shape(256, 128)], scalars=1, count=1, name="waves"
+    )(place)
+    space = [
+        pltpu.VMEM((4, 256, 256), bf16), pltpu.VMEM((2, 256, 128), f32),
+        pltpu.VMEM((2, 128, 256), bf16), dma(3),
+    ]
+    modes = call(
+        middle_kernel, shape(768, 128), space, scalars=1, count=7, remote=3, name="middle"
+    )(place, dft, twist_y, group, modes, keep, mix)
+    modes = exchange(modes.reshape(DEV, 1, 384), every).reshape(768, 128)
+    prepared = call(
+        state_kernel,
+        [
+            shape(2, WIDE, NX), shape(4, 16, NX), shape(256, NX, dtype=bf16),
+            shape(512, NX, dtype=bf16), shape(576, NX), shape(576, 256, dtype=bf16),
+            shape(160, 576, dtype=bf16),
+        ],
+        [pltpu.VMEM((160, NX), f32), pltpu.VMEM((576, 256), f32)],
+        count=8,
+        name="state",
+        mib=12,
+    )(lines, before, after, first_kernel, bias, second_kernel, first_pick, second_pick)
+    field, slope, low_state, acts, acts_turn, second_taps, first_turn = map(far, prepared)
+    remote = (
+        dft, twist_x, second_taps, acts_turn, first_turn, low_state, acts, field, slope,
+        far(jnp.asarray(first_take)), far(jnp.asarray(second_take)),
+    )
+    scratch = [pltpu.VMEM(x.shape, x.dtype) for x in remote] + [
+        dma(len(remote)),
         pltpu.VMEM((2, WIDE, NX), f32),
         pltpu.VMEM((160, NX), f32),
         pltpu.VMEM((256, NX), bf16),
-        pltpu.VMEM((256, NX), bf16),
         pltpu.VMEM((576, NX), bf16),
-        pltpu.VMEM((576, NX), bf16),
-        pltpu.VMEM((576, 256), f32),
-        pltpu.VMEM((576, 256), bf16),
     ]
-    result = call(closure_kernel, shape(8, 40, 256), scratch, count=11, name="closure")(
-        projected, lines, before, after, first_kernel, bias, second_kernel,
-        first_pick, second_pick, first_take, second_take,
-    )
+    result = call(
+        closure_kernel, shape(8, 40, 256), scratch, count=12, remote=11, name="closure", mib=32
+    )(*remote, modes)
     result = exchange(result, "row")
     grad_state, part = call(
-        unpack_kernel, [shape(2, 256, 128), shape(COLS, 8, 256)], count=1, name="unpack"
+        unpack_kernel, [shape(2, 256, 128), shape(320, 128)], count=1, name="unpack"
     )(result)
-    part = exchange(part, "col")
+    part = exchange(part.reshape(COLS, 1, 1280), "col").reshape(320, 128)
     grad_first, grad_second, grad_bias = call(
-        sums_kernel, [shape(18, 32), shape(32, 18), shape(1, 32)], count=1, name="sums"
+        sums_kernel, [shape(18, 32), shape(18, 32), shape(1, 32)], count=1, name="sums"
     )(part)
-    return grad_state, grad_first, grad_second, grad_bias.reshape(32)
+    return grad_state, grad_first, grad_second.T, grad_bias.reshape(32)
 
 
 def solution(mesh):

time: 116 us -> 121 us (1.043)
  waiting for transfers between devices: 30.6 us -> 17.4 us
  blocking collectives: 43.1 us -> 49.8 us
  Pallas kernels: 14.3 us -> 20.5 us
  local copies, waits for them, and re-layouts: 2.72 us -> 7.57 us
    all_to_all x2, waiting for transfers between devices: 30.5 us -> 15.7 us  [exchange(): return lax.all_to_all(values, axis, 0, 0, tiled=True)]
    all_to_all x3, blocking collectives: 43.1 us -> 49.8 us  [exchange(): return lax.all_to_all(values, axis, 0, 0, tiled=True)]
    pallas_call x7 -> x8, Pallas kernels: 14.3 us -> 20.5 us  [the longest x1 8.65 us: shards(): call(closure_kernel, shape(8, 40, 256), scratch, count=12, remote=11, nam...]
    unnamed x28 -> x25, local copies, waits for them, and re-layouts: 2.72 us -> 7.57 us
    ppermute x1, waiting for transfers between devices: 0.01 us -> 1.7 us  [shards(): before = lax.ppermute(high, ('row', 'col'), up)]
  transfers between devices with their start and end apart: 4 -> 4, of which waited for: 2 -> 3; matrix products, arithmetic and copies ran while one was open for 0% -> 0% of each run, Pallas kernels for 1% -> 2%
where the time goes in v1:
time: 121 us
  blocking collectives  49.8 us (41%)
  starting transfers between devices  24.3 us (20%)
  Pallas kernels  20.5 us (17%)
  waiting for transfers between devices  17.4 us (14%)
  local copies, waits for them, and re-layouts  7.57 us (6%)
    all_to_all x3, blocking collectives, exchange(): return lax.all_to_all(values, axis, 0, 0, tiled=True)  49.8 us
    all_to_all x2, starting transfers between devices, exchange(): return lax.all_to_all(values, axis, 0, 0, tiled=True)  20.2 us
    all_to_all x2, waiting for transfers between devices, exchange(): return lax.all_to_all(values, axis, 0, 0, tiled=True)  15.7 us
    pallas_call x1, Pallas kernels, shards(): call(closure_kernel, shape(8, 40, 256), scratch, count=12, remote=11, nam...  8.65 us
    unnamed x25, local copies, waits for them, and re-layouts  7.57 us
    pallas_call x1, Pallas kernels, shards(): call(middle_kernel, shape(768, 128), space, scalars=1, count=7, remote=3,...  3.72 us
    pallas_call x1, Pallas kernels, shards(): call(state_kernel, [shape(2, WIDE, NX), shape(4, 16, NX), shape(256, NX,...  2.79 us
    ppermute x1, starting transfers between devices, shards(): after = lax.ppermute(low, ('row', 'col'), [(j, i) for i, j in up])  2.62 us
  transfers between devices with their start and end apart: 4, of which 3 were waited for; matrix products, arithmetic and copies ran while one was open for 0% of the time, Pallas kernels for 2%

profile of v1, /device:TPU:1, one launch (start us, length us, event | category | flops | bytes accessed | tf_op | source)
XLA Modules:
  0.0 120.5 jit_solution(17450625900536982244)
XLA Ops:
  0.6 0.0 copy-start.7
  0.6 0.0 copy-start.8
  0.7 1.4 %pack.1 = f32[8,64,256]{2,1,0:T(8,128)S(1)} custom-call(f32[2,256,128]{2,1,0:T(8,128)} %cot_ref.1, f32[2,256,128]{2,1,0:T(8,128)} %state_ref.1), custom_call_target="tpu_custom_call" | custom-call | tf_op jit(solution)/shard_map/pack/pallas_call | solution.py:529
  2.1 14.4 %all_to_all.25.in_ref.own_ref = f32[8,64,256]{2,1,0:T(8,128)S(1)} all-to-all(f32[8,64,256]{2,1,0:T(8,128)S(1)} %pack.1), channel_id=1, replica_groups=mesh['row'=8,'col'=32] {'row'}, dimensions={0} | all-to-all | bytes 1048576 | tf_op jit(solution)/shard_map/all_to_all | solution.py:526
  16.4 2.4 %ahead.1 = (f32[512,128]{1,0:T(8,128)}, f32[4,2048]{1,0:T(4,128)S(1)}, f32[4,2048]{1,0:T(4,128)S(1)}) custom-call(bf16[4,256,256]{2,1,0:T(8,128)(2,1)} %constant.31.clone.dft_far, f32[8,256]{1,0:T(8,128)} %constant.34.clone.twist_far, f32[8,64,256]{2,1,0:T(8,128)S(1)} %all_to_all.25.in_ref.own_ref), custom_call_target="tpu_custom_call" | custom-call | tf_op jit(solution)/shard_map/ahead/pallas_call | solution.py:533
  18.8 14.0 %all-to-all-start.1 = ((f32[256,2,128]{2,1,0:T(2,128)}), f32[256,2,128]{2,1,0:T(2,128)S(1)}, u32[]{:S(2)}, u32[]{:S(2)}) async-start(f32[256,2,128]{2,1,0:T(2,128)} %bitcast.1), calls=%async_computation.1 | async-start | bytes 524288 | tf_op jit(solution)/shard_map/all_to_all | solution.py:526
  32.8 0.1 waves.1
  32.9 14.5 %all-to-all-done.1 = f32[256,2,128]{2,1,0:T(2,128)S(1)} async-done(((f32[256,2,128]{2,1,0:T(2,128)}), f32[256,2,128]{2,1,0:T(2,128)S(1)}, u32[]{:S(2)}, u32[]{:S(2)}) %all-to-all-start.1) | async-done | bytes 262176 | tf_op jit(solution)/shard_map/all_to_all | solution.py:526
  47.4 3.7 %middle.1 = f32[768,128]{1,0:T(8,128)} custom-call(s32[1]{0:T(128)} %bitcast.place_ref, bf16[4,256,256]{2,1,0:T(8,128)(2,1)} %constant.31.clone.dft_far, f32[2,256,128]{2,1,0:T(8,128)} %constant.33.clone.twist_far, bf16[2,128,256]{2,1,0:T(8,128)(2,1)} %constant.32.clone.group_far, f32[512,128]{1,0:T(8,128)S(1)} %bitcast.10, ...), custom_call_target="tpu_custom_call" | custom-call | tf_op jit(solution)/shard_map/middle/pallas_call | solution.py:550
  51.1 6.2 %all-to-all-start.2 = ((f32[256,1,384]{2,1,0:T(1,128)}), f32[256,1,384]{2,1,0:T(1,128)S(1)}, u32[]{:S(2)}, u32[]{:S(2)}) async-start(f32[256,1,384]{2,1,0:T(1,128)} %bitcast.3), calls=%async_computation.2 | async-start | bytes 786432 | tf_op jit(solution)/shard_map/all_to_all | solution.py:526
  57.4 1.5 %collective-permute-start = (f32[4,2048]{1,0:T(4,128)S(1)}, f32[4,2048]{1,0:T(4,128)S(1)}, u32[]{:S(2)}, u32[]{:S(2)}) collective-permute-start(f32[4,2048]{1,0:T(4,128)S(1)} %get-tuple-element.21), channel_id=1, source_target_pairs={{0,32},{32,64},{64,96},{96,128},{128,160},{160,192},{192,224},{224... | collective-permute-start | bytes 98312 | tf_op jit(solution)/shard_map/ppermute | solution.py:540
  58.9 2.6 %collective-permute-start.1 = (f32[4,2048]{1,0:T(4,128)S(1)}, f32[4,2048]{1,0:T(4,128)S(1)}, u32[]{:S(2)}, u32[]{:S(2)}) collective-permute-start(f32[4,2048]{1,0:T(4,128)S(1)} %get-tuple-element.22), channel_id=1, source_target_pairs={{32,0},{64,32},{96,64},{128,96},{160,128},{192,160},{224,192},{1,2... | collective-permute-start | bytes 98312 | tf_op jit(solution)/shard_map/ppermute | solution.py:541
  61.5 0.0 copy-done.11
  61.5 0.1 broadcast_select_fusion.bias_ref
  61.6 0.1 copy.18.second_ref
  61.7 1.7 %collective-permute-done.before_ref = f32[4,2048]{1,0:T(4,128)S(1)} collective-permute-done((f32[4,2048]{1,0:T(4,128)S(1)}, f32[4,2048]{1,0:T(4,128)S(1)}, u32[]{:S(2)}, u32[]{:S(2)}) %collective-permute-start) | collective-permute-done | bytes 32800 | tf_op jit(solution)/shard_map/ppermute | solution.py:540
  63.4 0.0 collective-permute-done.1.after_ref
  63.4 0.0 copy-done.7
  63.4 2.8 %state.1 = (f32[2,24,2048]{2,1,0:T(8,128)S(1)}, f32[4,16,2048]{2,1,0:T(8,128)S(1)}, bf16[256,2048]{1,0:T(8,128)(2,1)S(1)}, bf16[512,2048]{1,0:T(8,128)(2,1)S(1)}...) custom-call(f32[8,64,256]{2,1,0:T(8,128)S(1)} %all_to_all.25.in_ref.own_ref, ...), custom_call_target="tpu_custom_call" | custom-call | tf_op jit(solution)/shard_map/state/pallas_call | solution.py:554
  66.2 2.1 %copy-done = f32[576,2048]{1,0:T(8,128)} copy-done((f32[576,2048]{1,0:T(8,128)}, f32[576,2048]{1,0:T(8,128)S(1)}, u32[]{:S(2)}) %copy-start) | copy-done | bytes 4718616
  68.4 1.4 %copy-done.1 = bf16[512,2048]{1,0:T(8,128)(2,1)} copy-done((bf16[512,2048]{1,0:T(8,128)(2,1)}, bf16[512,2048]{1,0:T(8,128)(2,1)S(1)}, u32[]{:S(2)}) %copy-start.1) | copy-done | bytes 2097176
  69.7 1.0 copy-done.2
  70.7 0.8 copy-done.3
  71.5 0.8 copy-done.4
  72.3 0.7 copy-done.5
  73.0 0.7 copy-done.6
  73.7 1.2 all-to-all-done.2
  74.9 8.6 %closure.1 = f32[8,40,256]{2,1,0:T(8,128)S(1)} custom-call(bf16[4,256,256]{2,1,0:T(8,128)(2,1)} %constant.31.clone.dft_far, f32[8,256]{1,0:T(8,128)} %constant.34.clone.twist_far, bf16[576,256]{1,0:T(8,128)(2,1)} %copy-done.5, f32[576,2048]{1,0:T(8,128)} %copy-done, bf16[160,576]{1,0:T(8,128)(2,1)} %copy-done.6, bf16[256,2048]{1,0:T(8,128)(2,1)} %copy-done.2, ...), custom_call_target="tpu_custom_call" | custom-call | tf_op jit(solution)/shard_map/closure/pallas_call | solution.py:578
  83.5 11.5 %all_to_all.26.in_ref = f32[8,40,256]{2,1,0:T(8,128)S(1)} all-to-all(f32[8,40,256]{2,1,0:T(8,128)S(1)} %closure.1), channel_id=1, replica_groups=mesh['row'=8,'col'=32] {'row'}, dimensions={0} | all-to-all | bytes 655360 | tf_op jit(solution)/shard_map/all_to_all | solution.py:526
  95.0 0.8 unpack.1
  95.9 23.9 %all_to_all.27 = f32[32,1,1280]{2,1,0:T(1,128)S(1)} all-to-all(f32[32,1,1280]{2,1,0:T(1,128)S(1)} %bitcast.12), channel_id=1, replica_groups=mesh['row'=8,'col'=32] {'col'}, dimensions={0} | all-to-all | bytes 327680 | tf_op jit(solution)/shard_map/all_to_all | solution.py:526
  119.8 0.7 sums.1
  (14 shorter events, 0.0 us)
Async XLA Ops:
  0.6 62.8 %copy-start.7 = (bf16[18,256]{1,0:T(8,128)(2,1)S(1)}, bf16[18,256]{1,0:T(8,128)(2,1)}, u32[]{:S(2)}) copy-start(bf16[18,256]{1,0:T(8,128)(2,1)} %constant.35.clone.pick1_ref) | copy-start | bytes 27652
  0.6 62.8 %copy-start.8 = (bf16[18,256]{1,0:T(8,128)(2,1)S(1)}, bf16[18,256]{1,0:T(8,128)(2,1)}, u32[]{:S(2)}) copy-start(bf16[18,256]{1,0:T(8,128)(2,1)} %constant.36.clone.pick2_ref) | copy-start | bytes 27652
  0.7 60.9 %copy-start.11 = (f32[32]{0:T(128)S(1)}, f32[32]{0:T(128)}, u32[]{:S(2)}) copy-start(f32[32]{0:T(128)} %param.16) | copy-start | bytes 388
  0.7 60.9 %copy-start.10 = (bf16[32,18]{0,1:T(8,128)(2,1)S(1)}, bf16[32,18]{0,1:T(8,128)(2,1)}, u32[]{:S(2)}) copy-start(bf16[32,18]{0,1:T(8,128)(2,1)} %param.17) | copy-start | bytes 3460
  0.7 62.7 %copy-start.9 = (bf16[18,32]{1,0:T(8,128)(2,1)S(1)}, bf16[18,32]{1,0:T(8,128)(2,1)}, u32[]{:S(2)}) copy-start(bf16[18,32]{1,0:T(8,128)(2,1)} %first_ref.1) | copy-start | bytes 3460
  18.8 28.6 %all-to-all-start.1 = ((f32[256,2,128]{2,1,0:T(2,128)}), f32[256,2,128]{2,1,0:T(2,128)S(1)}, u32[]{:S(2)}, u32[]{:S(2)}) async-start(f32[256,2,128]{2,1,0:T(2,128)} %bitcast.1), calls=%async_computation.1 | async-start | bytes 524288 | tf_op jit(solution)/shard_map/all_to_all | solution.py:526
  51.1 23.7 %all-to-all-start.2 = ((f32[256,1,384]{2,1,0:T(1,128)}), f32[256,1,384]{2,1,0:T(1,128)S(1)}, u32[]{:S(2)}, u32[]{:S(2)}) async-start(f32[256,1,384]{2,1,0:T(1,128)} %bitcast.3), calls=%async_computation.2 | async-start | bytes 786432 | tf_op jit(solution)/shard_map/all_to_all | solution.py:526
  57.4 6.0 %collective-permute-start = (f32[4,2048]{1,0:T(4,128)S(1)}, f32[4,2048]{1,0:T(4,128)S(1)}, u32[]{:S(2)}, u32[]{:S(2)}) collective-permute-start(f32[4,2048]{1,0:T(4,128)S(1)} %get-tuple-element.21), channel_id=1, source_target_pairs={{0,32},{32,64},{64,96},{96,128},{128,160},{160,192},{192,224},{224... | collective-permute-start | bytes 98312 | tf_op jit(solution)/shard_map/ppermute | solution.py:540
  58.9 4.5 %collective-permute-start.1 = (f32[4,2048]{1,0:T(4,128)S(1)}, f32[4,2048]{1,0:T(4,128)S(1)}, u32[]{:S(2)}, u32[]{:S(2)}) collective-permute-start(f32[4,2048]{1,0:T(4,128)S(1)} %get-tuple-element.22), channel_id=1, source_target_pairs={{32,0},{64,32},{96,64},{128,96},{160,128},{192,160},{224,192},{1,2... | collective-permute-start | bytes 98312 | tf_op jit(solution)/shard_map/ppermute | solution.py:541
  66.2 2.1 %copy-start = (f32[576,2048]{1,0:T(8,128)}, f32[576,2048]{1,0:T(8,128)S(1)}, u32[]{:S(2)}) copy-start(f32[576,2048]{1,0:T(8,128)S(1)} %get-tuple-element.24.acts_turn_far) | copy-start | bytes 14155780
  68.4 1.4 %copy-start.1 = (bf16[512,2048]{1,0:T(8,128)(2,1)}, bf16[512,2048]{1,0:T(8,128)(2,1)S(1)}, u32[]{:S(2)}) copy-start(bf16[512,2048]{1,0:T(8,128)(2,1)S(1)} %get-tuple-element.27.acts_far) | copy-start | bytes 6291460
  69.7 1.0 copy-start.2
  70.7 0.8 copy-start.3
  71.5 0.8 copy-start.4
  72.3 0.7 copy-start.5
  73.0 0.7 copy-start.6

commit v2 on v1

--- a/solution.py
+++ b/solution.py
@@ -111,10 +111,7 @@
             out_ref[r, 16 * k : 16 * k + 16, :] = turned[16 * r : 16 * r + 16]
 
 
-def ahead_kernel(
-    dft_far, twist_far, in_ref, out_ref, low_ref, high_ref, dft_ref, twist_ref, sems
-):
-    copies = fetch((twist_far, dft_far), (twist_ref, dft_ref), sems)
+def ahead_kernel(dft_ref, twist_ref, in_ref, out_ref, low_ref, high_ref):
     u = [in_ref[r, 0:32, :] for r in range(8)]
     root = math.sqrt(0.5)
     a, b, c, d = (u[k] - u[k + 4] for k in range(4))
@@ -125,7 +122,6 @@
         (e0 - e2, e3 - e1),
         (a - root * (b - d), c - root * (b + d)),
     ]
-    copies[0].wait()
     reals, imags = [], []
     for k, (re, im) in enumerate(parts):
         cos, sin = twist_ref[k : k + 1, :], twist_ref[4 + k : 5 + k, :]
@@ -138,7 +134,6 @@
     stack = jnp.concatenate(
         reals + [even] + imags + [zero] + [zero] * 3 + [last_re] + [zero] * 3 + [last_im], 0
     )
-    copies[1].wait()
     cosine = left_dot(dft_ref, 0, stack, NT)
     sine = left_dot(dft_ref, 2, stack, NT)
     main_re = cosine[:, 0:128] + sine[:, 128:256]
@@ -189,18 +184,13 @@
 
 
 def middle_kernel(
-    place_ref, dft_far, twist_far, group_far, in_ref, keep_ref, mix_ref, out_ref,
-    dft_ref, twist_ref, group_ref, sems,
+    place_ref, dft_ref, twist_ref, group_ref, in_ref, keep_ref, mix_ref, out_ref
 ):
-    copies = fetch((dft_far, twist_far, group_far), (dft_ref, twist_ref, group_ref), sems)
     place = place_ref[0]
     re, im = in_ref[pl.ds(0, 256, 2), :], in_ref[pl.ds(1, 256, 2), :]
     both = jnp.concatenate([re, im], 1)
-    copies[0].wait()
     cosine, sine = left_dot(dft_ref, 0, both), left_dot(dft_ref, 2, both)
     f_re, f_im = cosine[:, :128] + sine[:, 128:], cosine[:, 128:] - sine[:, :128]
-    copies[1].wait()
-    copies[2].wait()
     cos, sin = twist_ref[0], twist_ref[1]
     t_re, t_im = f_re * cos + f_im * sin, f_im * cos - f_re * sin
     g = right_dot(jnp.concatenate([t_re, t_im], 0), group_ref)
@@ -235,7 +225,7 @@
     out_ref[pl.ds(2, 256, 3), :] = jnp.where(outer, beside(o_re), edge_im)
 
 
-def back_part(in_ref, dft_ref, twist_ref, out_ref, copies):
+def back_part(in_ref, dft_ref, twist_ref, out_ref):
     lane = lax.broadcasted_iota(jnp.int32, (128, 128), 1)
     row = lax.broadcasted_iota(jnp.int32, (128, 128), 0)
     last = lane >= 96
@@ -269,8 +259,6 @@
         t_high, t_low = dft_ref[base][:keep], dft_ref[base + 1][:keep]
         return dot(high, t_high) + (dot(low, t_high) + dot(high, t_low))
 
-    for copy in copies:
-        copy.wait()
     m_cos, m_sin = turn(m_high, m_low, 0, 256), turn(m_high, m_low, 2, 256)
     o_cos, o_sin = turn(o_high, o_low, 0, 128), turn(o_high, o_low, 2, 128)
     root = math.sqrt(0.5)
@@ -342,7 +330,8 @@
 
 def state_kernel(
     own_ref, before_ref, after_ref, first_ref, bias_ref, second_ref, pick1_ref, pick2_ref,
-    field_ref, slope_ref, state_low, acts, acts_turn, w2_ref, turn_ref,
+    w2_far, acts_turn_far, turn_far, state_far, acts_far, field_far,
+    w2_ref, acts_turn, turn_ref, state_low, acts, field_ref, sems,
     build_ref, w1_ref,
 ):
     lane = lax.broadcasted_iota(jnp.int32, (FEATS, 256), 1)
@@ -368,10 +357,6 @@
         field_ref[c, 0:2, :] = before_ref[2 * c : 2 * c + 2, :]
         field_ref[c, 18:20, :] = after_ref[2 * c : 2 * c + 2, :]
     fill_taps(build_ref, state_low, (field_ref[0], field_ref[1]), 1)
-    for c in range(2):
-        mine = field_ref[c, 2:18, :]
-        slope_ref[2 * c] = 0.5 * (ahead_of(mine) - behind_of(mine))
-        slope_ref[2 * c + 1] = 0.5 * (field_ref[c, 3:19, :] - field_ref[c, 1:17, :])
     w1 = w1_ref[...]
     turn_ref[...] = w1.T[:160].astype(bf16)
     w1_low = w1[:, :160].astype(bf16)
@@ -380,30 +365,35 @@
         cols = pl.ds(pl.multiple_of(k * CHUNK, CHUNK), CHUNK)
         active = jnp.tanh(dot(w1_low, state_low[0:160, cols]))
         acts[:, cols] = active[32:544].astype(bf16)
-        acts_turn[:, cols] = 1.0 - active * active
+        acts_turn[:, cols] = (1.0 - active * active).astype(bf16)
         return carry
 
     lax.fori_loop(0, NX // CHUNK, chunk, 0)
+    copies = fetch(
+        (w2_ref, acts_turn, turn_ref, state_low.at[0:160], acts, field_ref),
+        (w2_far, acts_turn_far, turn_far, state_far, acts_far, field_far),
+        sems,
+    )
+    for copy in copies:
+        copy.wait()
 
 
 def closure_kernel(
-    dft_far, twist_far, w2_far, acts_turn_far, turn_far, state_far, acts_far,
-    field_far, slope_far, take1_far, take2_far, in_ref,
+    w2_far, acts_turn_far, turn_far, state_far, acts_far, field_far,
+    dft_ref, twist_ref, take1_ref, take2_ref, in_ref,
     out_ref,
-    dft_ref, twist_ref, w2_ref, acts_turn, turn_ref, state_low, acts,
-    field_ref, slope_ref, take1_ref, take2_ref, sems,
+    w2_ref, acts_turn, turn_ref, state_low, acts, field_ref, sems,
     proj_ref, build_ref, scaled_low, grads,
 ):
     copies = fetch(
-        (dft_far, twist_far, w2_far, acts_turn_far, turn_far, state_far, acts_far,
-         field_far, slope_far, take1_far, take2_far),
-        (dft_ref, twist_ref, w2_ref, acts_turn, turn_ref, state_low, acts,
-         field_ref, slope_ref, take1_ref, take2_ref),
+        (w2_far, acts_turn_far, turn_far, state_far, acts_far, field_far),
+        (w2_ref, acts_turn, turn_ref, state_low.at[0:160], acts, field_ref),
         sems,
     )
-    back_part(in_ref, dft_ref, twist_ref, proj_ref, copies[:2])
+    state_low[160:256, :] = jnp.zeros((96, NX), bf16)
+    back_part(in_ref, dft_ref, twist_ref, proj_ref)
     fill_taps(build_ref, scaled_low, (STEP * proj_ref[0], STEP * proj_ref[1]), -1)
-    for copy in copies[2:5]:
+    for copy in copies[:3]:
         copy.wait()
     w2_low = w2_ref[:, :160]
     w1_turn = turn_ref[...]
@@ -411,12 +401,12 @@
     def chunk(k, carry):
         cols = pl.ds(pl.multiple_of(k * CHUNK, CHUNK), CHUNK)
         back = dot(w2_low, scaled_low[0:160, cols])
-        grads[:, cols] = (back * acts_turn[:, cols]).astype(bf16)
+        grads[:, cols] = (back * acts_turn[:, cols].astype(f32)).astype(bf16)
         build_ref[:, cols] = dot(w1_turn, grads[:, cols])
         return carry
 
     lax.fori_loop(0, NX // CHUNK, chunk, 0)
-    for copy in copies[5:]:
+    for copy in copies[3:]:
         copy.wait()
     first_sums = dot(grads[32:544, :], state_low[...], NT)
     second_sums = dot(acts[...], scaled_low[...], NT)
@@ -444,6 +434,12 @@
 
     inner, up, down = slice(2, 18), slice(3, 19), slice(1, 17)
     su = field_ref[0, inner, :]
+    along_x, along_y = [], []
+    for c in range(2):
+        mine = field_ref[c, inner, :]
+        along_x.append(0.5 * (ahead_of(mine) - behind_of(mine)))
+        along_y.append(0.5 * (field_ref[c, up, :] - field_ref[c, down, :]))
+    along = (along_x, along_y)
     centre = [STEP * proj_ref[c, inner, :] for c in range(2)]
     for c in range(2):
         mine = centre[c]
@@ -452,7 +448,7 @@
         carried = su * mine
         total = 0.5 * (ahead_of(carried) - behind_of(carried))
         total = total + 0.5 * (field_ref[1, up, :] * above - field_ref[1, down, :] * below)
-        total = total - (centre[0] * slope_ref[c] + centre[1] * slope_ref[2 + c])
+        total = total - (centre[0] * along[c][0] + centre[1] * along[c][1])
         total = total + (ahead_of(mine) + behind_of(mine) + above + below - 4.0 * mine)
         total = total + proj_ref[c, inner, :]
         for a, move in enumerate((ahead_of, None, behind_of)):
@@ -489,12 +485,12 @@
     second_ref[11:18, :] = moved[3][0:7, 0:32]
 
 
-def call(kernel, outs, scratch=(), scalars=0, count=0, name=None, remote=0, mib=8):
+def call(kernel, outs, scratch=(), scalars=0, count=0, name=None, remote=0, mib=8, leave=False):
     space = [pl.BlockSpec(memory_space=pltpu.SMEM)] * scalars
     space += [pl.BlockSpec(memory_space=pltpu.HBM)] * remote
     space += [pl.BlockSpec(memory_space=pltpu.VMEM)] * (count - scalars - remote)
     many = isinstance(outs, (list, tuple))
-    out_space = pl.BlockSpec(memory_space=pltpu.VMEM)
+    out_space = pl.BlockSpec(memory_space=pltpu.HBM if leave else pltpu.VMEM)
     return pl.pallas_call(
         kernel,
         out_shape=outs,
@@ -514,7 +510,7 @@
     t = tables()
     first_pick, second_pick, first_take, second_take = picks()
     dft, group, twist_y, twist_x = (
-        far(jnp.asarray(t[k])) for k in ("dft", "group", "twist_y", "twist_x")
+        jnp.asarray(t[k]) for k in ("dft", "group", "twist_y", "twist_x")
     )
     dma = lambda count: pltpu.SemaphoreType.DMA((count,))
     every = ("col", "row")
@@ -532,8 +528,7 @@
     lines = exchange(packed, "row")
     modes, low, high = call(
         ahead_kernel, [shape(512, 128), shape(4, NX), shape(4, NX)],
-        [pltpu.VMEM((4, 256, 256), bf16), pltpu.VMEM((8, 256), f32), dma(2)],
-        count=3, remote=2, name="ahead",
+        count=3, name="ahead",
     )(dft, twist_x, lines)
     order = [(i % ROWS) * COLS + i // ROWS for i in range(DEV)]
     up = [(order[i], order[(i + 1) % DEV]) for i in range(DEV)]
@@ -543,41 +538,33 @@
     keep, mix = call(
         waves_kernel, [shape(256, 128), shape(256, 128)], scalars=1, count=1, name="waves"
     )(place)
-    space = [
-        pltpu.VMEM((4, 256, 256), bf16), pltpu.VMEM((2, 256, 128), f32),
-        pltpu.VMEM((2, 128, 256), bf16), dma(3),
+    modes, before, after = lax.optimization_barrier((modes, before, after))
+    modes = call(middle_kernel, shape(768, 128), scalars=1, count=7, name="middle")(place, dft, twist_y, group, modes, keep, mix)
+    modes = exchange(modes.reshape(DEV, 1, 384), every).reshape(768, 128)
+    kept = [
+        ((576, 256), bf16), ((576, NX), bf16), ((160, 576), bf16), ((256, NX), bf16),
+        ((512, NX), bf16), ((2, WIDE, NX), f32),
     ]
-    modes = call(
-        middle_kernel, shape(768, 128), space, scalars=1, count=7, remote=3, name="middle"
-    )(place, dft, twist_y, group, modes, keep, mix)
-    modes = exchange(modes.reshape(DEV, 1, 384), every).reshape(768, 128)
+    local = [pltpu.VMEM(*k) for k in kept] + [dma(len(kept))]
+    kept[3] = ((160, NX), bf16)
     prepared = call(
         state_kernel,
-        [
-            shape(2, WIDE, NX), shape(4, 16, NX), shape(256, NX, dtype=bf16),
-            shape(512, NX, dtype=bf16), shape(576, NX), shape(576, 256, dtype=bf16),
-            shape(160, 576, dtype=bf16),
-        ],
-        [pltpu.VMEM((160, NX), f32), pltpu.VMEM((576, 256), f32)],
+        [pltpu.HBM(*k) for k in kept],
+        local + [pltpu.VMEM((160, NX), f32), pltpu.VMEM((576, 256), f32)],
         count=8,
         name="state",
-        mib=12,
+        mib=24,
+        leave=True,
     )(lines, before, after, first_kernel, bias, second_kernel, first_pick, second_pick)
-    field, slope, low_state, acts, acts_turn, second_taps, first_turn = map(far, prepared)
-    remote = (
-        dft, twist_x, second_taps, acts_turn, first_turn, low_state, acts, field, slope,
-        far(jnp.asarray(first_take)), far(jnp.asarray(second_take)),
-    )
-    scratch = [pltpu.VMEM(x.shape, x.dtype) for x in remote] + [
-        dma(len(remote)),
+    scratch = local + [
         pltpu.VMEM((2, WIDE, NX), f32),
         pltpu.VMEM((160, NX), f32),
         pltpu.VMEM((256, NX), bf16),
         pltpu.VMEM((576, NX), bf16),
     ]
     result = call(
-        closure_kernel, shape(8, 40, 256), scratch, count=12, remote=11, name="closure", mib=32
-    )(*remote, modes)
+        closure_kernel, shape(8, 40, 256), scratch, count=11, remote=6, name="closure", mib=32
+    )(*map(far, prepared), dft, twist_x, first_take, second_take, modes)
     result = exchange(result, "row")
     grad_state, part = call(
         unpack_kernel, [shape(2, 256, 128), shape(320, 128)], count=1, name="unpack"

time: 121 us -> 112 us (0.926)
  blocking collectives: 49.8 us -> 41.4 us
  local copies, waits for them, and re-layouts: 7.57 us -> 0.86 us
  waiting for transfers between devices: 17.4 us -> 22.4 us
    all_to_all x3, blocking collectives: 49.8 us -> 41.4 us  [exchange(): return lax.all_to_all(values, axis, 0, 0, tiled=True)]
    unnamed x25, local copies, waits for them, and re-layouts: 7.57 us -> 0.86 us
    all_to_all x2, waiting for transfers between devices: 15.7 us -> 20.6 us  [exchange(): return lax.all_to_all(values, axis, 0, 0, tiled=True)]
    all_to_all x2, starting transfers between devices: 20.2 us -> 21.5 us  [exchange(): return lax.all_to_all(values, axis, 0, 0, tiled=True)]
  transfers between devices with their start and end apart: 4 -> 4, of which waited for: 3 -> 3; matrix products, arithmetic and copies ran while one was open for 0% -> 0% of each run, Pallas kernels for 2% -> 5%
where the time goes in v2:
time: 112 us
  blocking collectives  41.4 us (37%)
  starting transfers between devices  25.5 us (23%)
  waiting for transfers between devices  22.4 us (20%)
  Pallas kernels  20.9 us (19%)
    all_to_all x3, blocking collectives, exchange(): return lax.all_to_all(values, axis, 0, 0, tiled=True)  41.4 us
    all_to_all x2, starting transfers between devices, exchange(): return lax.all_to_all(values, axis, 0, 0, tiled=True)  21.5 us
    all_to_all x2, waiting for transfers between devices, exchange(): return lax.all_to_all(values, axis, 0, 0, tiled=True)  20.6 us
    pallas_call x1, Pallas kernels, shards(): call(closure_kernel, shape(8, 40, 256), scratch, count=11, remote=6, name...  8.61 us
    pallas_call x1, Pallas kernels, shards(): call(state_kernel, [pltpu.HBM(*k) for k in kept], local + [pltpu.VMEM((16...  5.3 us
    ppermute x1, starting transfers between devices, shards(): after = lax.ppermute(low, ('row', 'col'), [(j, i) for i, j in up])  2.55 us
    pallas_call x1, Pallas kernels, shards(): call(middle_kernel, shape(768, 128), scalars=1, count=7, name='middle')  2.55 us
  transfers between devices with their start and end apart: 4, of which 3 were waited for; matrix products, arithmetic and copies ran while one was open for 0% of the time, Pallas kernels for 5%

profile of v2, /device:TPU:1, one launch (start us, length us, event | category | flops | bytes accessed | tf_op | source)
XLA Modules:
  0.0 111.8 jit_solution(15720846267835772769)
XLA Ops:
  0.6 0.0 copy-start
  0.6 0.0 copy-start.2
  0.7 0.0 copy-start.1
  0.7 1.4 %pack.1 = f32[8,64,256]{2,1,0:T(8,128)S(1)} custom-call(f32[2,256,128]{2,1,0:T(8,128)} %cot_ref.1, f32[2,256,128]{2,1,0:T(8,128)} %state_ref.1), custom_call_target="tpu_custom_call" | custom-call | tf_op jit(solution)/shard_map/pack/pallas_call | solution.py:525
  2.1 14.4 %all_to_all.25.in_ref.own_ref = f32[8,64,256]{2,1,0:T(8,128)S(1)} all-to-all(f32[8,64,256]{2,1,0:T(8,128)S(1)} %pack.1), channel_id=1, replica_groups=mesh['row'=8,'col'=32] {'row'}, dimensions={0} | all-to-all | bytes 1048576 | tf_op jit(solution)/shard_map/all_to_all | solution.py:522
  16.5 0.0 copy-done
  16.5 0.7 copy-done.5
  17.2 0.0 copy-start.9
  17.2 0.0 copy-start.3
  17.2 0.0 copy-start.4
  17.2 0.0 copy-start.6
  17.2 1.3 %ahead.1 = (f32[512,128]{1,0:T(8,128)}, f32[4,2048]{1,0:T(4,128)S(1)}, f32[4,2048]{1,0:T(4,128)S(1)}) custom-call(bf16[4,256,256]{2,1,0:T(8,128)(2,1)S(1)} %copy-done, f32[8,256]{1,0:T(8,128)S(1)} %copy-done.5, f32[8,64,256]{2,1,0:T(8,128)S(1)} %all_to_all.25.in_ref.own_ref), custom_call_target="tpu_custom_call" | custom-call | tf_op jit(solution)/shard_map/ahead/pallas_call | solution.py:529
  18.6 14.0 %all-to-all-start.1 = ((f32[256,2,128]{2,1,0:T(2,128)}), f32[256,2,128]{2,1,0:T(2,128)S(1)}, u32[]{:S(2)}, u32[]{:S(2)}) async-start(f32[256,2,128]{2,1,0:T(2,128)} %bitcast), calls=%async_computation.1 | async-start | bytes 524288 | tf_op jit(solution)/shard_map/all_to_all | solution.py:522
  32.5 1.4 %collective-permute-start = (f32[4,2048]{1,0:T(4,128)S(1)}, f32[4,2048]{1,0:T(4,128)S(1)}, u32[]{:S(2)}, u32[]{:S(2)}) collective-permute-start(f32[4,2048]{1,0:T(4,128)S(1)} %get-tuple-element.24), channel_id=1, source_target_pairs={{0,32},{32,64},{64,96},{96,128},{128,160},{160,192},{192,224},{224... | collective-permute-start | bytes 98312 | tf_op jit(solution)/shard_map/ppermute | solution.py:535
  34.0 2.5 %collective-permute-start.1 = (f32[4,2048]{1,0:T(4,128)S(1)}, f32[4,2048]{1,0:T(4,128)S(1)}, u32[]{:S(2)}, u32[]{:S(2)}) collective-permute-start(f32[4,2048]{1,0:T(4,128)S(1)} %get-tuple-element.25), channel_id=1, source_target_pairs={{32,0},{64,32},{96,64},{128,96},{160,128},{192,160},{224,192},{1,2... | collective-permute-start | bytes 98312 | tf_op jit(solution)/shard_map/ppermute | solution.py:536
  36.5 0.1 waves.1
  36.6 1.8 %collective-permute-done.before_ref = f32[4,2048]{1,0:T(4,128)S(1)} collective-permute-done((f32[4,2048]{1,0:T(4,128)S(1)}, f32[4,2048]{1,0:T(4,128)S(1)}, u32[]{:S(2)}, u32[]{:S(2)}) %collective-permute-start) | collective-permute-done | bytes 32800 | tf_op jit(solution)/shard_map/ppermute | solution.py:535
  38.4 0.0 collective-permute-done.1.after_ref
  38.4 8.7 %all-to-all-done.1 = f32[256,2,128]{2,1,0:T(2,128)S(1)} async-done(((f32[256,2,128]{2,1,0:T(2,128)}), f32[256,2,128]{2,1,0:T(2,128)S(1)}, u32[]{:S(2)}, u32[]{:S(2)}) %all-to-all-start.1) | async-done | bytes 262176 | tf_op jit(solution)/shard_map/all_to_all | solution.py:522
  47.2 0.0 copy-done.2
  47.2 2.5 %middle.1 = f32[768,128]{1,0:T(8,128)} custom-call(s32[1]{0:T(128)} %bitcast.2.place_ref, bf16[4,256,256]{2,1,0:T(8,128)(2,1)S(1)} %copy-done, f32[2,256,128]{2,1,0:T(8,128)S(1)} %copy-done.1, bf16[2,128,256]{2,1,0:T(8,128)(2,1)S(1)} %copy-done.2, f32[512,128]{1,0:T(8,128)S(1)} %bitcast.10, f32[256,128]{1,0:T(8,128)S(1)} %get-tuple-element.35.keep_ref, ...), custom_call_target="tpu_custom_call" | custom-call | tf_op jit(solution)/shard_map/middle/pallas_call | solution.py:542
  49.7 7.5 %all-to-all-start.2 = ((f32[256,1,384]{2,1,0:T(1,128)}), f32[256,1,384]{2,1,0:T(1,128)S(1)}, u32[]{:S(2)}, u32[]{:S(2)}) async-start(f32[256,1,384]{2,1,0:T(1,128)} %bitcast.3), calls=%async_computation.2 | async-start | bytes 786432 | tf_op jit(solution)/shard_map/all_to_all | solution.py:522
  57.2 0.1 copy.18.second_ref
  57.3 0.1 broadcast_select_fusion.bias_ref
  57.4 5.3 %state.1 = (bf16[576,256]{1,0:T(8,128)(2,1)}, bf16[576,2048]{1,0:T(8,128)(2,1)}, bf16[160,576]{1,0:T(8,128)(2,1)}, bf16[160,2048]{1,0:T(8,128)(2,1)}, bf16[512,2048]{1,0:T(8,128)(2,1)}, /*index=5*/f32[2,24,2048]{2,1,0:T(8,128)}) custom-call(f32[8,64,256]{2,1,0:T(8,128)S(1)} %all_to_all.25.in_ref.own_ref, f32[4,2048]{1,0:T(4,128)S(1)} %collective-permute-done.before_ref, ...), custom_call_target="tpu_custom_call" | custom-call | tf_op jit(solution)/shard_map/state/pallas_call | solution.py:550
  62.7 11.8 %all-to-all-done.2 = f32[256,1,384]{2,1,0:T(1,128)S(1)} async-done(((f32[256,1,384]{2,1,0:T(1,128)}), f32[256,1,384]{2,1,0:T(1,128)S(1)}, u32[]{:S(2)}, u32[]{:S(2)}) %all-to-all-start.2) | async-done | bytes 393248 | tf_op jit(solution)/shard_map/all_to_all | solution.py:522
  74.6 0.0 copy-done.3
  74.6 8.6 %closure.1 = f32[8,40,256]{2,1,0:T(8,128)S(1)} custom-call(bf16[576,256]{1,0:T(8,128)(2,1)} %get-tuple-element.28.w2_far, bf16[576,2048]{1,0:T(8,128)(2,1)} %get-tuple-element.29.acts_turn_far, bf16[160,576]{1,0:T(8,128)(2,1)} %get-tuple-element.30.turn_far, bf16[160,2048]{1,0:T(8,128)(2,1)} %get-tuple-element.31.state_far, ...), custom_call_target="tpu_custom_call" | custom-call | tf_op jit(solution)/shard_map/closure/pallas_call | solution.py:565
  83.2 11.3 %all_to_all.26.in_ref = f32[8,40,256]{2,1,0:T(8,128)S(1)} all-to-all(f32[8,40,256]{2,1,0:T(8,128)S(1)} %closure.1), channel_id=1, replica_groups=mesh['row'=8,'col'=32] {'row'}, dimensions={0} | all-to-all | bytes 655360 | tf_op jit(solution)/shard_map/all_to_all | solution.py:522
  94.5 0.8 unpack.1
  95.4 15.7 %all_to_all.27 = f32[32,1,1280]{2,1,0:T(1,128)S(1)} all-to-all(f32[32,1,1280]{2,1,0:T(1,128)S(1)} %bitcast.12), channel_id=1, replica_groups=mesh['row'=8,'col'=32] {'col'}, dimensions={0} | all-to-all | bytes 327680 | tf_op jit(solution)/shard_map/all_to_all | solution.py:522
  111.1 0.7 sums.1
  (14 shorter events, 0.0 us)
Async XLA Ops:
  0.6 15.8 %copy-start = (bf16[4,256,256]{2,1,0:T(8,128)(2,1)S(1)}, bf16[4,256,256]{2,1,0:T(8,128)(2,1)}, u32[]{:S(2)}) copy-start(bf16[4,256,256]{2,1,0:T(8,128)(2,1)} %constant.31.clone.dft_ref) | copy-start | bytes 1572868
  0.6 46.5 %copy-start.2 = (bf16[2,128,256]{2,1,0:T(8,128)(2,1)S(1)}, bf16[2,128,256]{2,1,0:T(8,128)(2,1)}, u32[]{:S(2)}) copy-start(bf16[2,128,256]{2,1,0:T(8,128)(2,1)} %constant.32.clone.group_ref) | copy-start | bytes 393220
  0.7 46.5 %copy-start.1 = (f32[2,256,128]{2,1,0:T(8,128)S(1)}, f32[2,256,128]{2,1,0:T(8,128)}, u32[]{:S(2)}) copy-start(f32[2,256,128]{2,1,0:T(8,128)} %constant.33.clone.twist_ref) | copy-start | bytes 786436
  16.5 0.7 copy-start.5
  17.2 40.0 %copy-start.10 = (bf16[32,18]{0,1:T(8,128)(2,1)S(1)}, bf16[32,18]{0,1:T(8,128)(2,1)}, u32[]{:S(2)}) copy-start(bf16[32,18]{0,1:T(8,128)(2,1)} %param.17) | copy-start | bytes 3460
  17.2 40.2 %copy-start.11 = (f32[32]{0:T(128)S(1)}, f32[32]{0:T(128)}, u32[]{:S(2)}) copy-start(f32[32]{0:T(128)} %param.16) | copy-start | bytes 388
  17.2 40.2 %copy-start.7 = (bf16[18,256]{1,0:T(8,128)(2,1)S(1)}, bf16[18,256]{1,0:T(8,128)(2,1)}, u32[]{:S(2)}) copy-start(bf16[18,256]{1,0:T(8,128)(2,1)} %constant.35.clone.pick1_ref) | copy-start | bytes 27652
  17.2 40.2 %copy-start.8 = (bf16[18,256]{1,0:T(8,128)(2,1)S(1)}, bf16[18,256]{1,0:T(8,128)(2,1)}, u32[]{:S(2)}) copy-start(bf16[18,256]{1,0:T(8,128)(2,1)} %constant.36.clone.pick2_ref) | copy-start | bytes 27652
  17.2 40.2 %copy-start.9 = (bf16[18,32]{1,0:T(8,128)(2,1)S(1)}, bf16[18,32]{1,0:T(8,128)(2,1)}, u32[]{:S(2)}) copy-start(bf16[18,32]{1,0:T(8,128)(2,1)} %first_ref.1) | copy-start | bytes 3460
  17.2 57.4 %copy-start.3 = (bf16[256,128]{1,0:T(8,128)(2,1)S(1)}, bf16[256,128]{1,0:T(8,128)(2,1)}, u32[]{:S(2)}) copy-start(bf16[256,128]{1,0:T(8,128)(2,1)} %constant.37.clone.take1_ref) | copy-start | bytes 196612
  17.2 57.4 %copy-start.4 = (bf16[256,128]{1,0:T(8,128)(2,1)S(1)}, bf16[256,128]{1,0:T(8,128)(2,1)}, u32[]{:S(2)}) copy-start(bf16[256,128]{1,0:T(8,128)(2,1)} %constant.38.clone.take2_ref) | copy-start | bytes 196612
  17.2 57.4 %copy-start.6 = (f32[8,256]{1,0:T(8,128)S(1)}, f32[8,256]{1,0:T(8,128)}, u32[]{:S(2)}) copy-start(f32[8,256]{1,0:T(8,128)} %constant.34.clone.twist_ref) | copy-start | bytes 24580
  18.6 28.6 %all-to-all-start.1 = ((f32[256,2,128]{2,1,0:T(2,128)}), f32[256,2,128]{2,1,0:T(2,128)S(1)}, u32[]{:S(2)}, u32[]{:S(2)}) async-start(f32[256,2,128]{2,1,0:T(2,128)} %bitcast), calls=%async_computation.1 | async-start | bytes 524288 | tf_op jit(solution)/shard_map/all_to_all | solution.py:522
  32.5 5.9 %collective-permute-start = (f32[4,2048]{1,0:T(4,128)S(1)}, f32[4,2048]{1,0:T(4,128)S(1)}, u32[]{:S(2)}, u32[]{:S(2)}) collective-permute-start(f32[4,2048]{1,0:T(4,128)S(1)} %get-tuple-element.24), channel_id=1, source_target_pairs={{0,32},{32,64},{64,96},{96,128},{128,160},{160,192},{192,224},{224... | collective-permute-start | bytes 98312 | tf_op jit(solution)/shard_map/ppermute | solution.py:535
  34.0 4.4 %collective-permute-start.1 = (f32[4,2048]{1,0:T(4,128)S(1)}, f32[4,2048]{1,0:T(4,128)S(1)}, u32[]{:S(2)}, u32[]{:S(2)}) collective-permute-start(f32[4,2048]{1,0:T(4,128)S(1)} %get-tuple-element.25), channel_id=1, source_target_pairs={{32,0},{64,32},{96,64},{128,96},{160,128},{192,160},{224,192},{1,2... | collective-permute-start | bytes 98312 | tf_op jit(solution)/shard_map/ppermute | solution.py:536
  49.7 24.8 %all-to-all-start.2 = ((f32[256,1,384]{2,1,0:T(1,128)}), f32[256,1,384]{2,1,0:T(1,128)S(1)}, u32[]{:S(2)}, u32[]{:S(2)}) async-start(f32[256,1,384]{2,1,0:T(1,128)} %bitcast.3), calls=%async_computation.2 | async-start | bytes 786432 | tf_op jit(solution)/shard_map/all_to_all | solution.py:522

commit v3 on v2

--- a/solution.py
+++ b/solution.py
@@ -86,29 +86,22 @@
     return pltpu.with_memory_space_constraint(values, pltpu.HBM)
 
 
-def fetch(sources, targets, sems):
-    copies = [
-        pltpu.make_async_copy(source, target, sems.at[k])
-        for k, (source, target) in enumerate(zip(sources, targets))
-    ]
-    for copy in copies:
-        copy.start()
-    return copies
-
-
-def pack_kernel(cot_ref, state_ref, out_ref, buffer_ref, sems):
+def pack_kernel(cot_ref, state_ref, twist_far, out_ref, twist_ref, buffer_ref, sems):
     copies = []
+    twist_copy = pltpu.make_async_copy(twist_far, twist_ref, sems.at[4])
     for f, ref in enumerate((cot_ref, state_ref)):
         for c in range(2):
             k = 2 * f + c
             copies.append(pltpu.make_async_copy(ref.at[c], buffer_ref.at[k], sems.at[k]))
     for copy in copies:
         copy.start()
+    twist_copy.start()
     for k, copy in enumerate(copies):
         copy.wait()
         turned = buffer_ref[k].T
         for r in range(ROWS):
             out_ref[r, 16 * k : 16 * k + 16, :] = turned[16 * r : 16 * r + 16]
+    twist_copy.wait()
 
 
 def ahead_kernel(dft_ref, twist_ref, in_ref, out_ref, low_ref, high_ref):
@@ -322,17 +315,12 @@
     build_ref[144:152, :] = jnp.ones((8, NX), f32)
     build_ref[152:160, :] = jnp.zeros((8, NX), f32)
     target[0:160, :] = build_ref[...].astype(bf16)
-    target[160:256, :] = jnp.zeros((96, NX), bf16)
-
-
-CHUNK = 256
 
 
 def state_kernel(
     own_ref, before_ref, after_ref, first_ref, bias_ref, second_ref, pick1_ref, pick2_ref,
-    w2_far, acts_turn_far, turn_far, state_far, acts_far, field_far,
-    w2_ref, acts_turn, turn_ref, state_low, acts, field_ref, sems,
-    build_ref, w1_ref,
+    w1_out, w2_out, turn_ref, state_low, field_ref,
+    build_ref, w1_ref, w2_ref,
 ):
     lane = lax.broadcasted_iota(jnp.int32, (FEATS, 256), 1)
     bias = bias_ref[...]
@@ -347,7 +335,7 @@
         moved1 = pltpu.roll(base1, j, 1) if j else base1
         moved2 = pltpu.roll(base2, j, 1) if j else base2
         w1_ref[rows, :] = moved1 + bias_part
-        w2_ref[rows, :] = moved2.astype(bf16)
+        w2_ref[rows, :] = moved2
     for c in range(2):
         field_ref[c, 20:24, :] = jnp.zeros((4, NX), f32)
         for r in range(8):
@@ -359,55 +347,26 @@
     fill_taps(build_ref, state_low, (field_ref[0], field_ref[1]), 1)
     w1 = w1_ref[...]
     turn_ref[...] = w1.T[:160].astype(bf16)
-    w1_low = w1[:, :160].astype(bf16)
-
-    def chunk(k, carry):
-        cols = pl.ds(pl.multiple_of(k * CHUNK, CHUNK), CHUNK)
-        active = jnp.tanh(dot(w1_low, state_low[0:160, cols]))
-        acts[:, cols] = active[32:544].astype(bf16)
-        acts_turn[:, cols] = (1.0 - active * active).astype(bf16)
-        return carry
-
-    lax.fori_loop(0, NX // CHUNK, chunk, 0)
-    copies = fetch(
-        (w2_ref, acts_turn, turn_ref, state_low.at[0:160], acts, field_ref),
-        (w2_far, acts_turn_far, turn_far, state_far, acts_far, field_far),
-        sems,
-    )
-    for copy in copies:
-        copy.wait()
+    w1_out[...] = w1[:, :160].astype(bf16)
+    w2_out[...] = w2_ref[:, :160].astype(bf16)
 
 
 def closure_kernel(
-    w2_far, acts_turn_far, turn_far, state_far, acts_far, field_far,
-    dft_ref, twist_ref, take1_ref, take2_ref, in_ref,
+    w1_ref, w2_ref, turn_ref, state_ref, field_ref, dft_ref, twist_ref, take1_ref, take2_ref,
+    in_ref,
     out_ref,
-    w2_ref, acts_turn, turn_ref, state_low, acts, field_ref, sems,
-    proj_ref, build_ref, scaled_low, grads,
+    proj_ref, build_ref, state_low, scaled_low, grads, acts,
 ):
-    copies = fetch(
-        (w2_far, acts_turn_far, turn_far, state_far, acts_far, field_far),
-        (w2_ref, acts_turn, turn_ref, state_low.at[0:160], acts, field_ref),
-        sems,
-    )
+    back_part(in_ref, dft_ref, twist_ref, proj_ref)
+    state_low[0:160, :] = state_ref[...]
     state_low[160:256, :] = jnp.zeros((96, NX), bf16)
-    back_part(in_ref, dft_ref, twist_ref, proj_ref)
+    scaled_low[160:256, :] = jnp.zeros((96, NX), bf16)
     fill_taps(build_ref, scaled_low, (STEP * proj_ref[0], STEP * proj_ref[1]), -1)
-    for copy in copies[:3]:
-        copy.wait()
-    w2_low = w2_ref[:, :160]
-    w1_turn = turn_ref[...]
-
-    def chunk(k, carry):
-        cols = pl.ds(pl.multiple_of(k * CHUNK, CHUNK), CHUNK)
-        back = dot(w2_low, scaled_low[0:160, cols])
-        grads[:, cols] = (back * acts_turn[:, cols].astype(f32)).astype(bf16)
-        build_ref[:, cols] = dot(w1_turn, grads[:, cols])
-        return carry
-
-    lax.fori_loop(0, NX // CHUNK, chunk, 0)
-    for copy in copies[3:]:
-        copy.wait()
+    active = jnp.tanh(dot(w1_ref[...], state_ref[...]))
+    acts[...] = active[32:544].astype(bf16)
+    back = dot(w2_ref[...], scaled_low[0:160, :])
+    grads[...] = (back * (1.0 - active * active)).astype(bf16)
+    build_ref[...] = dot(turn_ref[...], grads[...])
     first_sums = dot(grads[32:544, :], state_low[...], NT)
     second_sums = dot(acts[...], scaled_low[...], NT)
     lane = lax.broadcasted_iota(jnp.int32, (FEATS, 256), 1)
@@ -485,12 +444,12 @@
     second_ref[11:18, :] = moved[3][0:7, 0:32]
 
 
-def call(kernel, outs, scratch=(), scalars=0, count=0, name=None, remote=0, mib=8, leave=False):
+def call(kernel, outs, scratch=(), scalars=0, count=0, name=None, remote=0, mib=8):
     space = [pl.BlockSpec(memory_space=pltpu.SMEM)] * scalars
     space += [pl.BlockSpec(memory_space=pltpu.HBM)] * remote
     space += [pl.BlockSpec(memory_space=pltpu.VMEM)] * (count - scalars - remote)
     many = isinstance(outs, (list, tuple))
-    out_space = pl.BlockSpec(memory_space=pltpu.HBM if leave else pltpu.VMEM)
+    out_space = pl.BlockSpec(memory_space=pltpu.VMEM)
     return pl.pallas_call(
         kernel,
         out_shape=outs,
@@ -512,7 +471,6 @@
     dft, group, twist_y, twist_x = (
         jnp.asarray(t[k]) for k in ("dft", "group", "twist_y", "twist_x")
     )
-    dma = lambda count: pltpu.SemaphoreType.DMA((count,))
     every = ("col", "row")
     place = (lax.axis_index("col") * ROWS + lax.axis_index("row")).astype(jnp.int32).reshape(1)
     lanes = lax.broadcasted_iota(jnp.int32, (FEATS, 256), 1)
@@ -521,10 +479,10 @@
     def exchange(values, axis):
         return lax.all_to_all(values, axis, 0, 0, tiled=True)
 
-    space = [pltpu.VMEM((4, 256, 128), f32), pltpu.SemaphoreType.DMA((4,))]
-    packed = call(pack_kernel, shape(8, 64, 256), space, count=2, name="pack", remote=2)(
-        far(cotangent), far(state)
-    )
+    space = [pltpu.VMEM((4, 256, 128), f32), pltpu.SemaphoreType.DMA((5,))]
+    packed, twist_x = call(
+        pack_kernel, [shape(8, 64, 256), shape(8, 256)], space, count=3, name="pack", remote=3
+    )(far(cotangent), far(state), far(twist_x))
     lines = exchange(packed, "row")
     modes, low, high = call(
         ahead_kernel, [shape(512, 128), shape(4, NX), shape(4, NX)],
@@ -541,30 +499,27 @@
     modes, before, after = lax.optimization_barrier((modes, before, after))
     modes = call(middle_kernel, shape(768, 128), scalars=1, count=7, name="middle")(place, dft, twist_y, group, modes, keep, mix)
     modes = exchange(modes.reshape(DEV, 1, 384), every).reshape(768, 128)
-    kept = [
-        ((576, 256), bf16), ((576, NX), bf16), ((160, 576), bf16), ((256, NX), bf16),
-        ((512, NX), bf16), ((2, WIDE, NX), f32),
-    ]
-    local = [pltpu.VMEM(*k) for k in kept] + [dma(len(kept))]
-    kept[3] = ((160, NX), bf16)
     prepared = call(
         state_kernel,
-        [pltpu.HBM(*k) for k in kept],
-        local + [pltpu.VMEM((160, NX), f32), pltpu.VMEM((576, 256), f32)],
+        [
+            shape(576, 160, dtype=bf16), shape(576, 160, dtype=bf16),
+            shape(160, 576, dtype=bf16), shape(160, NX, dtype=bf16), shape(2, WIDE, NX),
+        ],
+        [pltpu.VMEM((160, NX), f32), pltpu.VMEM((576, 256), f32), pltpu.VMEM((576, 256), f32)],
         count=8,
         name="state",
-        mib=24,
-        leave=True,
     )(lines, before, after, first_kernel, bias, second_kernel, first_pick, second_pick)
-    scratch = local + [
+    scratch = [
         pltpu.VMEM((2, WIDE, NX), f32),
         pltpu.VMEM((160, NX), f32),
         pltpu.VMEM((256, NX), bf16),
+        pltpu.VMEM((256, NX), bf16),
         pltpu.VMEM((576, NX), bf16),
+        pltpu.VMEM((512, NX), bf16),
     ]
     result = call(
-        closure_kernel, shape(8, 40, 256), scratch, count=11, remote=6, name="closure", mib=32
-    )(*map(far, prepared), dft, twist_x, first_take, second_take, modes)
+        closure_kernel, shape(8, 40, 256), scratch, count=10, name="closure", mib=40
+    )(*prepared, dft, twist_x, first_take, second_take, modes)
     result = exchange(result, "row")
     grad_state, part = call(
         unpack_kernel, [shape(2, 256, 128), shape(320, 128)], count=1, name="unpack"

time: 112 us -> 108 us (0.964)
  Pallas kernels: 20.9 us -> 12.3 us
  waiting for transfers between devices: 22.4 us -> 25.7 us
    pallas_call x3, Pallas kernels: 15.3 us -> 6.81 us  [the longest x1 4.77 us: shards(): call(closure_kernel, shape(8, 40, 256), scratch, count=10, name='closure'...]
    all_to_all x2, waiting for transfers between devices: 20.6 us -> 23.9 us  [exchange(): return lax.all_to_all(values, axis, 0, 0, tiled=True)]
  transfers between devices with their start and end apart: 4 -> 4, of which waited for: 3 -> 3; matrix products, arithmetic and copies ran while one was open for 0% -> 0% of each run, Pallas kernels for 5% -> 1%
where the time goes in v3:
time: 108 us; the launch traced here: 107 us
  blocking collectives  41.6 us (39%)
  waiting for transfers between devices  25.7 us (24%)
  starting transfers between devices  25.4 us (24%)
  Pallas kernels  12.3 us (11%)
  local copies, waits for them, and re-layouts  1.42 us (1%)
    all_to_all x3, blocking collectives, exchange(): return lax.all_to_all(values, axis, 0, 0, tiled=True)  41.6 us
    all_to_all x2, waiting for transfers between devices, exchange(): return lax.all_to_all(values, axis, 0, 0, tiled=True)  23.9 us
    all_to_all x2, starting transfers between devices, exchange(): return lax.all_to_all(values, axis, 0, 0, tiled=True)  21.5 us
    pallas_call x1, Pallas kernels, shards(): call(closure_kernel, shape(8, 40, 256), scratch, count=10, name='closure'...  4.77 us
    ppermute x1, starting transfers between devices, shards(): after = lax.ppermute(low, ('row', 'col'), [(j, i) for i, j in up])  2.55 us
    pallas_call x1, Pallas kernels, shards(): call(middle_kernel, shape(768, 128), scalars=1, count=7, name='middle')  2.55 us
  transfers between devices with their start and end apart: 4, of which 3 were waited for; matrix products, arithmetic and copies ran while one was open for 0% of the time, Pallas kernels for 1%

profile of v3, /device:TPU:1, one launch (start us, length us, event | category | flops | bytes accessed | tf_op | source)
XLA Modules:
  0.0 107.2 jit_solution(5067316041876315787)
XLA Ops:
  0.6 1.4 %pack.1 = (f32[8,64,256]{2,1,0:T(8,128)S(1)}, f32[8,256]{1,0:T(8,128)S(1)}) custom-call(f32[2,256,128]{2,1,0:T(8,128)} %cot_ref.1, f32[2,256,128]{2,1,0:T(8,128)} %state_ref.1, f32[8,256]{1,0:T(8,128)} %constant.34.clone.twist_far), custom_call_target="tpu_custom_call" | custom-call | tf_op jit(solution)/shard_map/pack/pallas_call | solution.py:483
  2.0 0.0 copy-start
  2.0 14.5 %all_to_all.25.in_ref.own_ref = f32[8,64,256]{2,1,0:T(8,128)S(1)} all-to-all(f32[8,64,256]{2,1,0:T(8,128)S(1)} %get-tuple-element.24), channel_id=1, replica_groups=mesh['row'=8,'col'=32] {'row'}, dimensions={0} | all-to-all | bytes 1048576 | tf_op jit(solution)/shard_map/all_to_all | solution.py:480
  16.5 0.0 copy-done
  16.5 1.3 %ahead.1 = (f32[512,128]{1,0:T(8,128)}, f32[4,2048]{1,0:T(4,128)S(1)}, f32[4,2048]{1,0:T(4,128)S(1)}) custom-call(bf16[4,256,256]{2,1,0:T(8,128)(2,1)S(1)} %copy-done, f32[8,256]{1,0:T(8,128)S(1)} %get-tuple-element.25.twist_ref, f32[8,64,256]{2,1,0:T(8,128)S(1)} %all_to_all.25.in_ref.own_ref), custom_call_target="tpu_custom_call" | custom-call | tf_op jit(solution)/shard_map/ahead/pallas_call | solution.py:487
  17.8 14.0 %all-to-all-start.1 = ((f32[256,2,128]{2,1,0:T(2,128)}), f32[256,2,128]{2,1,0:T(2,128)S(1)}, u32[]{:S(2)}, u32[]{:S(2)}) async-start(f32[256,2,128]{2,1,0:T(2,128)} %bitcast), calls=%async_computation.1 | async-start | bytes 524288 | tf_op jit(solution)/shard_map/all_to_all | solution.py:480
  31.8 1.4 %collective-permute-start = (f32[4,2048]{1,0:T(4,128)S(1)}, f32[4,2048]{1,0:T(4,128)S(1)}, u32[]{:S(2)}, u32[]{:S(2)}) collective-permute-start(f32[4,2048]{1,0:T(4,128)S(1)} %get-tuple-element.27), channel_id=1, source_target_pairs={{0,32},{32,64},{64,96},{96,128},{128,160},{160,192},{192,224},{224... | collective-permute-start | bytes 98312 | tf_op jit(solution)/shard_map/ppermute | solution.py:493
  33.3 2.5 %collective-permute-start.1 = (f32[4,2048]{1,0:T(4,128)S(1)}, f32[4,2048]{1,0:T(4,128)S(1)}, u32[]{:S(2)}, u32[]{:S(2)}) collective-permute-start(f32[4,2048]{1,0:T(4,128)S(1)} %get-tuple-element.28), channel_id=1, source_target_pairs={{32,0},{64,32},{96,64},{128,96},{160,128},{192,160},{224,192},{1,2... | collective-permute-start | bytes 98312 | tf_op jit(solution)/shard_map/ppermute | solution.py:494
  35.8 0.1 waves.1
  35.9 1.8 %collective-permute-done.before_ref = f32[4,2048]{1,0:T(4,128)S(1)} collective-permute-done((f32[4,2048]{1,0:T(4,128)S(1)}, f32[4,2048]{1,0:T(4,128)S(1)}, u32[]{:S(2)}, u32[]{:S(2)}) %collective-permute-start) | collective-permute-done | bytes 32800 | tf_op jit(solution)/shard_map/ppermute | solution.py:493
  37.7 0.0 collective-permute-done.1.after_ref
  37.7 8.7 %all-to-all-done.1 = f32[256,2,128]{2,1,0:T(2,128)S(1)} async-done(((f32[256,2,128]{2,1,0:T(2,128)}), f32[256,2,128]{2,1,0:T(2,128)S(1)}, u32[]{:S(2)}, u32[]{:S(2)}) %all-to-all-start.1) | async-done | bytes 262176 | tf_op jit(solution)/shard_map/all_to_all | solution.py:480
  46.4 0.0 copy-done.1
  46.5 0.0 copy-done.2
  46.5 2.5 %middle.1 = f32[768,128]{1,0:T(8,128)} custom-call(s32[1]{0:T(128)} %bitcast.2.place_ref, bf16[4,256,256]{2,1,0:T(8,128)(2,1)S(1)} %copy-done, f32[2,256,128]{2,1,0:T(8,128)S(1)} %copy-done.1, bf16[2,128,256]{2,1,0:T(8,128)(2,1)S(1)} %copy-done.2, f32[512,128]{1,0:T(8,128)S(1)} %bitcast.10, f32[256,128]{1,0:T(8,128)S(1)} %get-tuple-element.37.keep_ref, ...), custom_call_target="tpu_custom_call" | custom-call | tf_op jit(solution)/shard_map/middle/pallas_call | solution.py:500
  49.0 7.5 %all-to-all-start.2 = ((f32[256,1,384]{2,1,0:T(1,128)}), f32[256,1,384]{2,1,0:T(1,128)S(1)}, u32[]{:S(2)}, u32[]{:S(2)}) async-start(f32[256,1,384]{2,1,0:T(1,128)} %bitcast.3), calls=%async_computation.2 | async-start | bytes 786432 | tf_op jit(solution)/shard_map/all_to_all | solution.py:480
  56.5 0.0 copy-done.8
  56.5 0.1 copy.18.second_ref
  56.6 0.7 copy-done.9
  57.3 0.1 broadcast_select_fusion.bias_ref
  57.3 0.6 copy-done.5
  58.0 0.0 copy-done.6
  58.0 0.0 copy-done.7
  58.0 0.7 state.1
  58.7 15.2 %all-to-all-done.2 = f32[256,1,384]{2,1,0:T(1,128)S(1)} async-done(((f32[256,1,384]{2,1,0:T(1,128)}), f32[256,1,384]{2,1,0:T(1,128)S(1)}, u32[]{:S(2)}, u32[]{:S(2)}) %all-to-all-start.2) | async-done | bytes 393248 | tf_op jit(solution)/shard_map/all_to_all | solution.py:480
  73.8 0.0 copy-done.3
  73.9 0.0 copy-done.4
  73.9 4.8 %closure.1 = f32[8,40,256]{2,1,0:T(8,128)S(1)} custom-call(bf16[576,160]{1,0:T(8,128)(2,1)S(1)} %get-tuple-element.31.w1_ref, bf16[576,160]{1,0:T(8,128)(2,1)S(1)} %get-tuple-element.32.w2_ref, bf16[160,576]{1,0:T(8,128)(2,1)S(1)} %get-tuple-element.33.turn_ref, bf16[160,2048]{1,0:T(8,128)(2,1)S(1)} %get-tuple-element.34.state_ref, ...), custom_call_target="tpu_custom_call" | custom-call | tf_op jit(solution)/shard_map/closure/pallas_call | solution.py:520
  78.6 11.3 %all_to_all.26.in_ref = f32[8,40,256]{2,1,0:T(8,128)S(1)} all-to-all(f32[8,40,256]{2,1,0:T(8,128)S(1)} %closure.1), channel_id=1, replica_groups=mesh['row'=8,'col'=32] {'row'}, dimensions={0} | all-to-all | bytes 655360 | tf_op jit(solution)/shard_map/all_to_all | solution.py:480
  90.0 0.8 unpack.1
  90.8 15.7 %all_to_all.27 = f32[32,1,1280]{2,1,0:T(1,128)S(1)} all-to-all(f32[32,1,1280]{2,1,0:T(1,128)S(1)} %bitcast.12), channel_id=1, replica_groups=mesh['row'=8,'col'=32] {'col'}, dimensions={0} | all-to-all | bytes 327680 | tf_op jit(solution)/shard_map/all_to_all | solution.py:480
  106.5 0.7 sums.1
  (10 shorter events, 0.0 us)
Async XLA Ops:
  2.0 14.5 %copy-start = (bf16[4,256,256]{2,1,0:T(8,128)(2,1)S(1)}, bf16[4,256,256]{2,1,0:T(8,128)(2,1)}, u32[]{:S(2)}) copy-start(bf16[4,256,256]{2,1,0:T(8,128)(2,1)} %constant.31.clone.dft_ref) | copy-start | bytes 1572868
  17.8 28.6 %copy-start.1 = (f32[2,256,128]{2,1,0:T(8,128)S(1)}, f32[2,256,128]{2,1,0:T(8,128)}, u32[]{:S(2)}) copy-start(f32[2,256,128]{2,1,0:T(8,128)} %constant.33.clone.twist_ref) | copy-start | bytes 786436
  17.8 28.6 %copy-start.2 = (bf16[2,128,256]{2,1,0:T(8,128)(2,1)S(1)}, bf16[2,128,256]{2,1,0:T(8,128)(2,1)}, u32[]{:S(2)}) copy-start(bf16[2,128,256]{2,1,0:T(8,128)(2,1)} %constant.32.clone.group_ref) | copy-start | bytes 393220
  17.8 28.6 %all-to-all-start.1 = ((f32[256,2,128]{2,1,0:T(2,128)}), f32[256,2,128]{2,1,0:T(2,128)S(1)}, u32[]{:S(2)}, u32[]{:S(2)}) async-start(f32[256,2,128]{2,1,0:T(2,128)} %bitcast), calls=%async_computation.1 | async-start | bytes 524288 | tf_op jit(solution)/shard_map/all_to_all | solution.py:480
  31.8 5.9 %collective-permute-start = (f32[4,2048]{1,0:T(4,128)S(1)}, f32[4,2048]{1,0:T(4,128)S(1)}, u32[]{:S(2)}, u32[]{:S(2)}) collective-permute-start(f32[4,2048]{1,0:T(4,128)S(1)} %get-tuple-element.27), channel_id=1, source_target_pairs={{0,32},{32,64},{64,96},{96,128},{128,160},{160,192},{192,224},{224... | collective-permute-start | bytes 98312 | tf_op jit(solution)/shard_map/ppermute | solution.py:493
  33.3 4.4 %collective-permute-start.1 = (f32[4,2048]{1,0:T(4,128)S(1)}, f32[4,2048]{1,0:T(4,128)S(1)}, u32[]{:S(2)}, u32[]{:S(2)}) collective-permute-start(f32[4,2048]{1,0:T(4,128)S(1)} %get-tuple-element.28), channel_id=1, source_target_pairs={{32,0},{64,32},{96,64},{128,96},{160,128},{192,160},{224,192},{1,2... | collective-permute-start | bytes 98312 | tf_op jit(solution)/shard_map/ppermute | solution.py:494
  49.0 7.5 %copy-start.8 = (bf16[32,18]{0,1:T(8,128)(2,1)S(1)}, bf16[32,18]{0,1:T(8,128)(2,1)}, u32[]{:S(2)}) copy-start(bf16[32,18]{0,1:T(8,128)(2,1)} %param.17) | copy-start | bytes 3460
  49.0 24.8 %all-to-all-start.2 = ((f32[256,1,384]{2,1,0:T(1,128)}), f32[256,1,384]{2,1,0:T(1,128)S(1)}, u32[]{:S(2)}, u32[]{:S(2)}) async-start(f32[256,1,384]{2,1,0:T(1,128)} %bitcast.3), calls=%async_computation.2 | async-start | bytes 786432 | tf_op jit(solution)/shard_map/all_to_all | solution.py:480
  56.6 0.7 copy-start.9
  57.3 0.7 copy-start.5
  57.3 0.7 copy-start.6
  57.3 0.7 copy-start.7
  58.0 15.9 %copy-start.3 = (bf16[256,128]{1,0:T(8,128)(2,1)S(1)}, bf16[256,128]{1,0:T(8,128)(2,1)}, u32[]{:S(2)}) copy-start(bf16[256,128]{1,0:T(8,128)(2,1)} %constant.37.clone.take1_ref) | copy-start | bytes 196612
  58.0 15.9 %copy-start.4 = (bf16[256,128]{1,0:T(8,128)(2,1)S(1)}, bf16[256,128]{1,0:T(8,128)(2,1)}, u32[]{:S(2)}) copy-start(bf16[256,128]{1,0:T(8,128)(2,1)} %constant.38.clone.take2_ref) | copy-start | bytes 196612

commit v4 on v3

--- a/solution.py
+++ b/solution.py
@@ -28,7 +28,7 @@
 def tables():
     index = np.arange(256)
     angle = 2 * np.pi * (np.outer(index, index) % 256) / 256
-    dft = np.concatenate([pair(np.cos(angle)), pair(np.sin(angle))])
+    dft = pair(np.concatenate([np.cos(angle), np.sin(angle)]))
     small = 2 * np.pi * (np.outer(np.arange(16), np.arange(16)) % 16) / 16
     eye = np.eye(8)
     group = np.concatenate([np.kron(eye, np.cos(small)), np.kron(eye, np.sin(small))], 1)
@@ -69,17 +69,20 @@
     return lax.dot_general(left, right, dims, preferred_element_type=f32)
 
 
-def left_dot(table_ref, base, values, dims=NN, keep=None):
+def left_dot(table_ref, values, dims=NN):
     high, low = split(values)
-    t_high, t_low = table_ref[base], table_ref[base + 1]
-    if keep is not None:
-        t_high, t_low = t_high[:, :keep], t_low[:, :keep]
-    return dot(t_high, high, dims) + (dot(t_high, low, dims) + dot(t_low, high, dims))
-
-
-def right_dot(values, table_ref):
+    dim = dims[0][1][0] ^ 1
+    size = values.shape[dim]
+    wide = dot(table_ref[0], jnp.concatenate([high, low], dim), dims)
+    both = wide[:, :size] + (wide[:, size:] + dot(table_ref[1], high, dims))
+    return both[:256], both[256:]
+
+
+def right_dot(values, high_table, low_table, dims=NN):
     high, low = split(values)
-    return dot(high, table_ref[0]) + (dot(low, table_ref[0]) + dot(high, table_ref[1]))
+    size = values.shape[0]
+    tall = dot(jnp.concatenate([high, low], 0), high_table, dims)
+    return tall[:size] + (tall[size:] + dot(high, low_table, dims))
 
 
 def far(values):
@@ -127,8 +130,7 @@
     stack = jnp.concatenate(
         reals + [even] + imags + [zero] + [zero] * 3 + [last_re] + [zero] * 3 + [last_im], 0
     )
-    cosine = left_dot(dft_ref, 0, stack, NT)
-    sine = left_dot(dft_ref, 2, stack, NT)
+    cosine, sine = left_dot(dft_ref, stack, NT)
     main_re = cosine[:, 0:128] + sine[:, 128:256]
     main_im = cosine[:, 128:256] - sine[:, 0:128]
     odd_re = cosine[:128, 256:384] + sine[:128, 384:512]
@@ -182,21 +184,21 @@
     place = place_ref[0]
     re, im = in_ref[pl.ds(0, 256, 2), :], in_ref[pl.ds(1, 256, 2), :]
     both = jnp.concatenate([re, im], 1)
-    cosine, sine = left_dot(dft_ref, 0, both), left_dot(dft_ref, 2, both)
+    cosine, sine = left_dot(dft_ref, both)
     f_re, f_im = cosine[:, :128] + sine[:, 128:], cosine[:, 128:] - sine[:, :128]
     cos, sin = twist_ref[0], twist_ref[1]
     t_re, t_im = f_re * cos + f_im * sin, f_im * cos - f_re * sin
-    g = right_dot(jnp.concatenate([t_re, t_im], 0), group_ref)
+    g = right_dot(jnp.concatenate([t_re, t_im], 0), group_ref[0], group_ref[1])
     g_re, g_im = g[:256, :128] + g[256:, 128:], g[256:, :128] - g[:256, 128:]
     keep, mix = keep_ref[...], mix_ref[...]
     lane = lax.broadcasted_iota(jnp.int32, (256, 128), 1)
     p_re = keep * g_re + mix * swap16(g_re, lane)
     p_im = keep * g_im + mix * swap16(g_im, lane)
-    h = right_dot(jnp.concatenate([p_re, p_im], 0), group_ref)
+    h = right_dot(jnp.concatenate([p_re, p_im], 0), group_ref[0], group_ref[1])
     h_re, h_im = h[:256, :128] - h[256:, 128:], h[256:, :128] + h[:256, 128:]
     t_re, t_im = h_re * cos - h_im * sin, h_im * cos + h_re * sin
     both = jnp.concatenate([t_re, t_im], 1)
-    cosine, sine = left_dot(dft_ref, 0, both), left_dot(dft_ref, 2, both)
+    cosine, sine = left_dot(dft_ref, both)
     scale = 1.0 / (NX * NY)
     o_re = (cosine[:, :128] - sine[:, 128:]) * scale
     o_im = (cosine[:, 128:] + sine[:, :128]) * scale
@@ -245,29 +247,26 @@
             0,
         ),
     ]
-    m_high, m_low = split(jnp.concatenate(mains, 1).T)
-    o_high, o_low = split(jnp.concatenate([low_re, low_im, low_h], 1).T)
-
-    def turn(high, low, base, keep):
-        t_high, t_low = dft_ref[base][:keep], dft_ref[base + 1][:keep]
-        return dot(high, t_high) + (dot(low, t_high) + dot(high, t_low))
-
-    m_cos, m_sin = turn(m_high, m_low, 0, 256), turn(m_high, m_low, 2, 256)
-    o_cos, o_sin = turn(o_high, o_low, 0, 128), turn(o_high, o_low, 2, 128)
+    main = right_dot(jnp.concatenate(mains, 1).T, dft_ref[0], dft_ref[1], NT)
+    odd = jnp.concatenate([low_re, low_im, low_h], 1).T
+    odd = jnp.concatenate([odd[128 * k + 96 : 128 * k + 128] for k in range(3)], 0)
+    odd = right_dot(odd, dft_ref[0][:, :128], dft_ref[1][:, :128], NT)
+    m_cos, m_sin, o_cos, o_sin = main[:, :256], main[:, 256:], odd[:, :256], odd[:, 256:]
     root = math.sqrt(0.5)
-    near_row = (lax.broadcasted_iota(jnp.int32, (128, 256), 0) & 8) == 0
 
     def imag_rows(values):
-        return jnp.where(near_row, pltpu.roll(values, 124, 0), pltpu.roll(values, 4, 0))
+        rows = values.shape[0]
+        near_row = (lax.broadcasted_iota(jnp.int32, values.shape, 0) & 8) == 0
+        return jnp.where(near_row, pltpu.roll(values, rows - 4, 0), pltpu.roll(values, 4, 0))
 
     for k in (0, 256):
         if k == 0:
             re, im = m_cos[0:128] - m_sin[128:256], m_cos[128:256] + m_sin[0:128]
-            last_re, last_im = o_cos[96:128] - o_sin[224:256], o_cos[224:256] + o_sin[96:128]
+            last_re, last_im = o_cos[0:32] - o_sin[32:64], o_cos[32:64] + o_sin[0:32]
         else:
-            m_c, m_s, o_c, o_s = (v[256:384] for v in (m_cos, m_sin, o_cos, o_sin))
+            m_c, m_s, o_c, o_s = m_cos[256:384], m_sin[256:384], o_cos[64:96], o_sin[64:96]
             re, im = m_c - imag_rows(m_s), imag_rows(m_c) + m_s
-            last_re, last_im = (o_c - imag_rows(o_s))[96:], (imag_rows(o_c) + o_s)[96:]
+            last_re, last_im = o_c - imag_rows(o_s), imag_rows(o_c) + o_s
         w4 = last_re * twist_ref[3:4, :] - last_im * twist_ref[7:8, :]
         w0 = re[96:128]
         ws = []
@@ -492,7 +491,7 @@
     up = [(order[i], order[(i + 1) % DEV]) for i in range(DEV)]
     before = lax.ppermute(high, ("row", "col"), up)
     after = lax.ppermute(low, ("row", "col"), [(j, i) for i, j in up])
-    modes = exchange(modes.reshape(DEV, 2, 128), every).reshape(512, 128)
+    modes = exchange(modes.reshape(DEV, 1, 256), every).reshape(512, 128)
     keep, mix = call(
         waves_kernel, [shape(256, 128), shape(256, 128)], scalars=1, count=1, name="waves"
     )(place)

time: 108 us -> 108 us (level)
  no operation moved by 1% of the time
where the time goes in v4:
time: 108 us; the launch traced here: 107 us
  blocking collectives  41.6 us (39%)
  waiting for transfers between devices  25.7 us (24%)
  starting transfers between devices  25.4 us (24%)
  Pallas kernels  12.6 us (12%)
  local copies, waits for them, and re-layouts  1.42 us (1%)
    all_to_all x3, blocking collectives, exchange(): return lax.all_to_all(values, axis, 0, 0, tiled=True)  41.6 us
    all_to_all x2, waiting for transfers between devices, exchange(): return lax.all_to_all(values, axis, 0, 0, tiled=True)  23.9 us
    all_to_all x2, starting transfers between devices, exchange(): return lax.all_to_all(values, axis, 0, 0, tiled=True)  21.5 us
    pallas_call x1, Pallas kernels, shards(): call(closure_kernel, shape(8, 40, 256), scratch, count=10, name='closure'...  4.62 us
    pallas_call x1, Pallas kernels, shards(): call(middle_kernel, shape(768, 128), scalars=1, count=7, name='middle')  2.91 us
    ppermute x1, starting transfers between devices, shards(): after = lax.ppermute(low, ('row', 'col'), [(j, i) for i, j in up])  2.55 us
  transfers between devices with their start and end apart: 4, of which 3 were waited for; matrix products, arithmetic and copies ran while one was open for 0% of the time, Pallas kernels for 1%

profile of v4, /device:TPU:1, one launch (start us, length us, event | category | flops | bytes accessed | tf_op | source)
XLA Modules:
  0.0 107.5 jit_solution(4274657077915594706)
XLA Ops:
  0.6 1.4 %pack.1 = (f32[8,64,256]{2,1,0:T(8,128)S(1)}, f32[8,256]{1,0:T(8,128)S(1)}) custom-call(f32[2,256,128]{2,1,0:T(8,128)} %cot_ref.1, f32[2,256,128]{2,1,0:T(8,128)} %state_ref.1, f32[8,256]{1,0:T(8,128)} %constant.34.clone.twist_far), custom_call_target="tpu_custom_call" | custom-call | tf_op jit(solution)/shard_map/pack/pallas_call | solution.py:482
  2.0 0.0 copy-start
  2.0 14.5 %all_to_all.25.in_ref.own_ref = f32[8,64,256]{2,1,0:T(8,128)S(1)} all-to-all(f32[8,64,256]{2,1,0:T(8,128)S(1)} %get-tuple-element.24), channel_id=1, replica_groups=mesh['row'=8,'col'=32] {'row'}, dimensions={0} | all-to-all | bytes 1048576 | tf_op jit(solution)/shard_map/all_to_all | solution.py:479
  16.5 0.0 copy-done
  16.5 1.3 %ahead.1 = (f32[512,128]{1,0:T(8,128)}, f32[4,2048]{1,0:T(4,128)S(1)}, f32[4,2048]{1,0:T(4,128)S(1)}) custom-call(bf16[2,512,256]{2,1,0:T(8,128)(2,1)S(1)} %copy-done, f32[8,256]{1,0:T(8,128)S(1)} %get-tuple-element.25.twist_ref, f32[8,64,256]{2,1,0:T(8,128)S(1)} %all_to_all.25.in_ref.own_ref), custom_call_target="tpu_custom_call" | custom-call | tf_op jit(solution)/shard_map/ahead/pallas_call | solution.py:486
  17.9 14.0 %all-to-all-start.1 = ((f32[256,1,256]{2,1,0:T(1,128)}), f32[256,1,256]{2,1,0:T(1,128)S(1)}, u32[]{:S(2)}, u32[]{:S(2)}) async-start(f32[256,1,256]{2,1,0:T(1,128)} %bitcast), calls=%async_computation.1 | async-start | bytes 524288 | tf_op jit(solution)/shard_map/all_to_all | solution.py:479
  31.8 1.4 %collective-permute-start = (f32[4,2048]{1,0:T(4,128)S(1)}, f32[4,2048]{1,0:T(4,128)S(1)}, u32[]{:S(2)}, u32[]{:S(2)}) collective-permute-start(f32[4,2048]{1,0:T(4,128)S(1)} %get-tuple-element.27), channel_id=1, source_target_pairs={{0,32},{32,64},{64,96},{96,128},{128,160},{160,192},{192,224},{224... | collective-permute-start | bytes 98312 | tf_op jit(solution)/shard_map/ppermute | solution.py:492
  33.3 2.5 %collective-permute-start.1 = (f32[4,2048]{1,0:T(4,128)S(1)}, f32[4,2048]{1,0:T(4,128)S(1)}, u32[]{:S(2)}, u32[]{:S(2)}) collective-permute-start(f32[4,2048]{1,0:T(4,128)S(1)} %get-tuple-element.28), channel_id=1, source_target_pairs={{32,0},{64,32},{96,64},{128,96},{160,128},{192,160},{224,192},{1,2... | collective-permute-start | bytes 98312 | tf_op jit(solution)/shard_map/ppermute | solution.py:493
  35.8 0.1 waves.1
  35.9 1.8 %collective-permute-done.before_ref = f32[4,2048]{1,0:T(4,128)S(1)} collective-permute-done((f32[4,2048]{1,0:T(4,128)S(1)}, f32[4,2048]{1,0:T(4,128)S(1)}, u32[]{:S(2)}, u32[]{:S(2)}) %collective-permute-start) | collective-permute-done | bytes 32800 | tf_op jit(solution)/shard_map/ppermute | solution.py:492
  37.7 0.0 collective-permute-done.1.after_ref
  37.7 8.7 %all-to-all-done.1 = f32[256,1,256]{2,1,0:T(1,128)S(1)} async-done(((f32[256,1,256]{2,1,0:T(1,128)}), f32[256,1,256]{2,1,0:T(1,128)S(1)}, u32[]{:S(2)}, u32[]{:S(2)}) %all-to-all-start.1) | async-done | bytes 262176 | tf_op jit(solution)/shard_map/all_to_all | solution.py:479
  46.5 0.0 copy-done.1
  46.5 0.0 copy-done.2
  46.5 2.9 %middle.1 = f32[768,128]{1,0:T(8,128)} custom-call(s32[1]{0:T(128)} %bitcast.2.place_ref, bf16[2,512,256]{2,1,0:T(8,128)(2,1)S(1)} %copy-done, f32[2,256,128]{2,1,0:T(8,128)S(1)} %copy-done.1, bf16[2,128,256]{2,1,0:T(8,128)(2,1)S(1)} %copy-done.2, f32[512,128]{1,0:T(8,128)S(1)} %bitcast.10, f32[256,128]{1,0:T(8,128)S(1)} %get-tuple-element.37.keep_ref, ...), custom_call_target="tpu_custom_call" | custom-call | tf_op jit(solution)/shard_map/middle/pallas_call | solution.py:499
  49.4 7.5 %all-to-all-start.2 = ((f32[256,1,384]{2,1,0:T(1,128)}), f32[256,1,384]{2,1,0:T(1,128)S(1)}, u32[]{:S(2)}, u32[]{:S(2)}) async-start(f32[256,1,384]{2,1,0:T(1,128)} %bitcast.3), calls=%async_computation.2 | async-start | bytes 786432 | tf_op jit(solution)/shard_map/all_to_all | solution.py:479
  56.9 0.0 copy-done.8
  56.9 0.1 copy.19.second_ref
  57.0 0.7 copy-done.9
  57.6 0.1 broadcast_select_fusion.bias_ref
  57.7 0.6 copy-done.5
  58.3 0.0 copy-done.6
  58.4 0.0 copy-done.7
  58.4 0.7 state.1
  59.1 15.2 %all-to-all-done.2 = f32[256,1,384]{2,1,0:T(1,128)S(1)} async-done(((f32[256,1,384]{2,1,0:T(1,128)}), f32[256,1,384]{2,1,0:T(1,128)S(1)}, u32[]{:S(2)}, u32[]{:S(2)}) %all-to-all-start.2) | async-done | bytes 393248 | tf_op jit(solution)/shard_map/all_to_all | solution.py:479
  74.2 0.0 copy-done.3
  74.2 0.0 copy-done.4
  74.2 4.6 %closure.1 = f32[8,40,256]{2,1,0:T(8,128)S(1)} custom-call(bf16[576,160]{1,0:T(8,128)(2,1)S(1)} %get-tuple-element.31.w1_ref, bf16[576,160]{1,0:T(8,128)(2,1)S(1)} %get-tuple-element.32.w2_ref, bf16[160,576]{1,0:T(8,128)(2,1)S(1)} %get-tuple-element.33.turn_ref, bf16[160,2048]{1,0:T(8,128)(2,1)S(1)} %get-tuple-element.34.state_ref, ...), custom_call_target="tpu_custom_call" | custom-call | tf_op jit(solution)/shard_map/closure/pallas_call | solution.py:519
  78.9 11.3 %all_to_all.26.in_ref = f32[8,40,256]{2,1,0:T(8,128)S(1)} all-to-all(f32[8,40,256]{2,1,0:T(8,128)S(1)} %closure.1), channel_id=1, replica_groups=mesh['row'=8,'col'=32] {'row'}, dimensions={0} | all-to-all | bytes 655360 | tf_op jit(solution)/shard_map/all_to_all | solution.py:479
  90.2 0.8 unpack.1
  91.0 15.7 %all_to_all.27 = f32[32,1,1280]{2,1,0:T(1,128)S(1)} all-to-all(f32[32,1,1280]{2,1,0:T(1,128)S(1)} %bitcast.12), channel_id=1, replica_groups=mesh['row'=8,'col'=32] {'col'}, dimensions={0} | all-to-all | bytes 327680 | tf_op jit(solution)/shard_map/all_to_all | solution.py:479
  106.8 0.7 sums.1
  (10 shorter events, 0.0 us)
Async XLA Ops:
  2.0 14.5 %copy-start = (bf16[2,512,256]{2,1,0:T(8,128)(2,1)S(1)}, bf16[2,512,256]{2,1,0:T(8,128)(2,1)}, u32[]{:S(2)}) copy-start(bf16[2,512,256]{2,1,0:T(8,128)(2,1)} %constant.31.clone.dft_ref) | copy-start | bytes 1572868
  17.9 28.6 %copy-start.1 = (f32[2,256,128]{2,1,0:T(8,128)S(1)}, f32[2,256,128]{2,1,0:T(8,128)}, u32[]{:S(2)}) copy-start(f32[2,256,128]{2,1,0:T(8,128)} %constant.33.clone.twist_ref) | copy-start | bytes 786436
  17.9 28.6 %copy-start.2 = (bf16[2,128,256]{2,1,0:T(8,128)(2,1)S(1)}, bf16[2,128,256]{2,1,0:T(8,128)(2,1)}, u32[]{:S(2)}) copy-start(bf16[2,128,256]{2,1,0:T(8,128)(2,1)} %constant.32.clone.group_ref) | copy-start | bytes 393220
  17.9 28.6 %all-to-all-start.1 = ((f32[256,1,256]{2,1,0:T(1,128)}), f32[256,1,256]{2,1,0:T(1,128)S(1)}, u32[]{:S(2)}, u32[]{:S(2)}) async-start(f32[256,1,256]{2,1,0:T(1,128)} %bitcast), calls=%async_computation.1 | async-start | bytes 524288 | tf_op jit(solution)/shard_map/all_to_all | solution.py:479
  31.8 5.9 %collective-permute-start = (f32[4,2048]{1,0:T(4,128)S(1)}, f32[4,2048]{1,0:T(4,128)S(1)}, u32[]{:S(2)}, u32[]{:S(2)}) collective-permute-start(f32[4,2048]{1,0:T(4,128)S(1)} %get-tuple-element.27), channel_id=1, source_target_pairs={{0,32},{32,64},{64,96},{96,128},{128,160},{160,192},{192,224},{224... | collective-permute-start | bytes 98312 | tf_op jit(solution)/shard_map/ppermute | solution.py:492
  33.3 4.4 %collective-permute-start.1 = (f32[4,2048]{1,0:T(4,128)S(1)}, f32[4,2048]{1,0:T(4,128)S(1)}, u32[]{:S(2)}, u32[]{:S(2)}) collective-permute-start(f32[4,2048]{1,0:T(4,128)S(1)} %get-tuple-element.28), channel_id=1, source_target_pairs={{32,0},{64,32},{96,64},{128,96},{160,128},{192,160},{224,192},{1,2... | collective-permute-start | bytes 98312 | tf_op jit(solution)/shard_map/ppermute | solution.py:493
  49.4 7.5 %copy-start.8 = (bf16[32,18]{0,1:T(8,128)(2,1)S(1)}, bf16[32,18]{0,1:T(8,128)(2,1)}, u32[]{:S(2)}) copy-start(bf16[32,18]{0,1:T(8,128)(2,1)} %param.17) | copy-start | bytes 3460
  49.4 24.8 %all-to-all-start.2 = ((f32[256,1,384]{2,1,0:T(1,128)}), f32[256,1,384]{2,1,0:T(1,128)S(1)}, u32[]{:S(2)}, u32[]{:S(2)}) async-start(f32[256,1,384]{2,1,0:T(1,128)} %bitcast.3), calls=%async_computation.2 | async-start | bytes 786432 | tf_op jit(solution)/shard_map/all_to_all | solution.py:479
  57.0 0.7 copy-start.9
  57.6 0.7 copy-start.5
  57.6 0.7 copy-start.6
  57.6 0.7 copy-start.7
  58.4 15.9 %copy-start.3 = (bf16[256,128]{1,0:T(8,128)(2,1)S(1)}, bf16[256,128]{1,0:T(8,128)(2,1)}, u32[]{:S(2)}) copy-start(bf16[256,128]{1,0:T(8,128)(2,1)} %constant.37.clone.take1_ref) | copy-start | bytes 196612
  58.4 15.9 %copy-start.4 = (bf16[256,128]{1,0:T(8,128)(2,1)S(1)}, bf16[256,128]{1,0:T(8,128)(2,1)}, u32[]{:S(2)}) copy-start(bf16[256,128]{1,0:T(8,128)(2,1)} %constant.38.clone.take2_ref) | copy-start | bytes 196612

commit v5 on v4

--- a/solution.py
+++ b/solution.py
@@ -76,6 +76,20 @@
     wide = dot(table_ref[0], jnp.concatenate([high, low], dim), dims)
     both = wide[:, :size] + (wide[:, size:] + dot(table_ref[1], high, dims))
     return both[:256], both[256:]
+
+
+def apart_dot(table_ref, values):
+    high, low = split(values)
+    parts = []
+    for k in (0, 256):
+        t_high, t_low = table_ref[0, k : k + 256, :], table_ref[1, k : k + 256, :]
+        parts.append(dot(t_high, high) + (dot(t_high, low) + dot(t_low, high)))
+    return parts
+
+
+def right_apart(values, table_ref):
+    high, low = split(values)
+    return dot(high, table_ref[0]) + (dot(low, table_ref[0]) + dot(high, table_ref[1]))
 
 
 def right_dot(values, high_table, low_table, dims=NN):
@@ -154,8 +168,7 @@
             ]
 
 
-def waves_kernel(place_ref, keep_ref, mix_ref):
-    place = place_ref[0]
+def waves(place):
     lane = lax.broadcasted_iota(jnp.int32, (256, 128), 1)
     row = lax.broadcasted_iota(jnp.int32, (256, 128), 0)
     slot = lane // 32
@@ -170,8 +183,7 @@
     inverse = 1.0 / (kx * kx + ky * ky)
     cross = jnp.where((mx == -(NX // 2)) | (my == -(NY // 2)), 0.0, kx * ky)
     own = jnp.where((lane & 16) == 0, kx * kx, ky * ky)
-    keep_ref[...] = 1.0 - own * inverse
-    mix_ref[...] = -cross * inverse
+    return 1.0 - own * inverse, -cross * inverse, lane
 
 
 def swap16(values, lane):
@@ -179,26 +191,25 @@
 
 
 def middle_kernel(
-    place_ref, dft_ref, twist_ref, group_ref, in_ref, keep_ref, mix_ref, out_ref
+    place_ref, dft_ref, twist_ref, group_ref, in_ref, out_ref
 ):
     place = place_ref[0]
     re, im = in_ref[pl.ds(0, 256, 2), :], in_ref[pl.ds(1, 256, 2), :]
     both = jnp.concatenate([re, im], 1)
-    cosine, sine = left_dot(dft_ref, both)
+    cosine, sine = apart_dot(dft_ref, both)
     f_re, f_im = cosine[:, :128] + sine[:, 128:], cosine[:, 128:] - sine[:, :128]
     cos, sin = twist_ref[0], twist_ref[1]
     t_re, t_im = f_re * cos + f_im * sin, f_im * cos - f_re * sin
-    g = right_dot(jnp.concatenate([t_re, t_im], 0), group_ref[0], group_ref[1])
+    g = right_apart(jnp.concatenate([t_re, t_im], 0), group_ref)
     g_re, g_im = g[:256, :128] + g[256:, 128:], g[256:, :128] - g[:256, 128:]
-    keep, mix = keep_ref[...], mix_ref[...]
-    lane = lax.broadcasted_iota(jnp.int32, (256, 128), 1)
+    keep, mix, lane = waves(place)
     p_re = keep * g_re + mix * swap16(g_re, lane)
     p_im = keep * g_im + mix * swap16(g_im, lane)
-    h = right_dot(jnp.concatenate([p_re, p_im], 0), group_ref[0], group_ref[1])
+    h = right_apart(jnp.concatenate([p_re, p_im], 0), group_ref)
     h_re, h_im = h[:256, :128] - h[256:, 128:], h[256:, :128] + h[:256, 128:]
     t_re, t_im = h_re * cos - h_im * sin, h_im * cos + h_re * sin
     both = jnp.concatenate([t_re, t_im], 1)
-    cosine, sine = left_dot(dft_ref, both)
+    cosine, sine = apart_dot(dft_ref, both)
     scale = 1.0 / (NX * NY)
     o_re = (cosine[:, :128] - sine[:, 128:]) * scale
     o_im = (cosine[:, 128:] + sine[:, :128]) * scale
@@ -317,18 +328,35 @@
 
 
 def state_kernel(
-    own_ref, before_ref, after_ref, first_ref, bias_ref, second_ref, pick1_ref, pick2_ref,
+    first_far, second_far, bias_far, pick_far, before_far, after_far, own_ref,
     w1_out, w2_out, turn_ref, state_low, field_ref,
-    build_ref, w1_ref, w2_ref,
+    build_ref, w1_ref, w2_ref, first_ref, second_ref, bias_ref, pick_ref,
+    before_ref, after_ref, sems,
 ):
+    copies = [
+        pltpu.make_async_copy(source, target, sems.at[k])
+        for k, (source, target) in enumerate(
+            (
+                (first_far, first_ref), (second_far, second_ref),
+                (bias_far, bias_ref), (pick_far, pick_ref),
+                (before_far, before_ref), (after_far, after_ref),
+            )
+        )
+    ]
+    for copy in copies:
+        copy.start()
+    for copy in copies:
+        copy.wait()
     lane = lax.broadcasted_iota(jnp.int32, (FEATS, 256), 1)
-    bias = bias_ref[...]
+    square = lax.broadcasted_iota(jnp.int32, (FEATS, FEATS), 0)
+    own = square == lax.broadcasted_iota(jnp.int32, (FEATS, FEATS), 1)
+    bias = jnp.sum(jnp.where(own, bias_ref[...], 0.0), 1, keepdims=True)
     bias_high = bias.astype(bf16).astype(f32)
     bias_part = jnp.where(
         lane == 6 * WIDE, bias_high, jnp.where(lane == 6 * WIDE + 1, bias - bias_high, 0.0)
     )
-    base1 = dot(first_ref[...].astype(f32).T.astype(bf16), pick1_ref[...])
-    base2 = dot(second_ref[...], pick2_ref[...])
+    base1 = dot(first_ref[...].astype(f32).T.astype(bf16), pick_ref[0])
+    base2 = dot(second_ref[...].astype(f32).T.astype(bf16), pick_ref[1])
     for j in range(18):
         rows = slice(32 * j, 32 * j + 32)
         moved1 = pltpu.roll(base1, j, 1) if j else base1
@@ -472,8 +500,6 @@
     )
     every = ("col", "row")
     place = (lax.axis_index("col") * ROWS + lax.axis_index("row")).astype(jnp.int32).reshape(1)
-    lanes = lax.broadcasted_iota(jnp.int32, (FEATS, 256), 1)
-    bias = jnp.where(lanes >= 6 * WIDE, first_bias[:, None], 0.0)
 
     def exchange(values, axis):
         return lax.all_to_all(values, axis, 0, 0, tiled=True)
@@ -492,22 +518,29 @@
     before = lax.ppermute(high, ("row", "col"), up)
     after = lax.ppermute(low, ("row", "col"), [(j, i) for i, j in up])
     modes = exchange(modes.reshape(DEV, 1, 256), every).reshape(512, 128)
-    keep, mix = call(
-        waves_kernel, [shape(256, 128), shape(256, 128)], scalars=1, count=1, name="waves"
-    )(place)
-    modes, before, after = lax.optimization_barrier((modes, before, after))
-    modes = call(middle_kernel, shape(768, 128), scalars=1, count=7, name="middle")(place, dft, twist_y, group, modes, keep, mix)
-    modes = exchange(modes.reshape(DEV, 1, 384), every).reshape(768, 128)
     prepared = call(
         state_kernel,
         [
             shape(576, 160, dtype=bf16), shape(576, 160, dtype=bf16),
             shape(160, 576, dtype=bf16), shape(160, NX, dtype=bf16), shape(2, WIDE, NX),
         ],
-        [pltpu.VMEM((160, NX), f32), pltpu.VMEM((576, 256), f32), pltpu.VMEM((576, 256), f32)],
-        count=8,
+        [
+            pltpu.VMEM((160, NX), f32), pltpu.VMEM((576, 256), f32), pltpu.VMEM((576, 256), f32),
+            pltpu.VMEM((18, FEATS), bf16), pltpu.VMEM((18, FEATS), bf16),
+            pltpu.VMEM((1, FEATS), f32), pltpu.VMEM((2, 18, 256), bf16),
+            pltpu.VMEM((4, NX), f32), pltpu.VMEM((4, NX), f32),
+            pltpu.SemaphoreType.DMA((6,)),
+        ],
+        count=7,
+        remote=6,
         name="state",
-    )(lines, before, after, first_kernel, bias, second_kernel, first_pick, second_pick)
+    )(
+        far(first_kernel), far(second_kernel.T), far(first_bias.reshape(1, FEATS)),
+        far(jnp.asarray(np.stack([first_pick, second_pick]))), far(before), far(after), lines,
+    )
+    modes, prepared = lax.optimization_barrier((modes, prepared))
+    modes = call(middle_kernel, shape(768, 128), scalars=1, count=5, name="middle")(place, dft, twist_y, group, modes)
+    modes = exchange(modes.reshape(DEV, 1, 384), every).reshape(768, 128)
     scratch = [
         pltpu.VMEM((2, WIDE, NX), f32),
         pltpu.VMEM((160, NX), f32),

time: 108 us -> 109 us (level)
  blocking collectives: 41.6 us -> 68.5 us
  waiting for transfers between devices: 25.7 us -> 8.34 us
  starting transfers between devices: 25.4 us -> 18 us
    all_to_all x3 -> x4, blocking collectives: 41.6 us -> 68.5 us  [exchange(): return lax.all_to_all(values, axis, 0, 0, tiled=True)]
    all_to_all x2 -> x1, waiting for transfers between devices: 23.9 us -> 6.45 us  [exchange(): return lax.all_to_all(values, axis, 0, 0, tiled=True)]
    all_to_all x2 -> x1, starting transfers between devices: 21.5 us -> 14 us  [exchange(): return lax.all_to_all(values, axis, 0, 0, tiled=True)]
    pallas_call x2 -> x1, Pallas kernels: 3 us -> 1.8 us  [shards(): call(middle_kernel, shape(768, 128), scalars=1, count=5, name='middle')]
  transfers between devices with their start and end apart: 4 -> 3, of which waited for: 3 -> 2; matrix products, arithmetic and copies ran while one was open for 0% -> 0% of each run, Pallas kernels for 1% -> 2%
where the time goes in v5:
time: 109 us; the launch traced here: 108 us
  blocking collectives  68.5 us (63%)
  starting transfers between devices  18 us (17%)
  Pallas kernels  12.3 us (11%)
  waiting for transfers between devices  8.34 us (8%)
    all_to_all x4, blocking collectives, exchange(): return lax.all_to_all(values, axis, 0, 0, tiled=True)  68.5 us
    all_to_all x1, starting transfers between devices, exchange(): return lax.all_to_all(values, axis, 0, 0, tiled=True)  14 us
    all_to_all x1, waiting for transfers between devices, exchange(): return lax.all_to_all(values, axis, 0, 0, tiled=True)  6.45 us
    pallas_call x1, Pallas kernels, shards(): call(closure_kernel, shape(8, 40, 256), scratch, count=10, name='closure'...  4.61 us
    ppermute x1, starting transfers between devices, shards(): after = lax.ppermute(low, ('row', 'col'), [(j, i) for i, j in up])  2.55 us
  transfers between devices with their start and end apart: 3, of which 2 were waited for; matrix products, arithmetic and copies ran while one was open for 0% of the time, Pallas kernels for 2%

profile of v5, /device:TPU:1, one launch (start us, length us, event | category | flops | bytes accessed | tf_op | source)
XLA Modules:
  0.0 108.5 jit_solution(3828895877767475354)
XLA Ops:
  0.6 1.4 %pack.1 = (f32[8,64,256]{2,1,0:T(8,128)S(1)}, f32[8,256]{1,0:T(8,128)S(1)}) custom-call(f32[2,256,128]{2,1,0:T(8,128)} %cot_ref.1, f32[2,256,128]{2,1,0:T(8,128)} %state_ref.1, f32[8,256]{1,0:T(8,128)} %constant.28.clone.twist_far), custom_call_target="tpu_custom_call" | custom-call | tf_op jit(solution)/shard_map/pack/pallas_call | solution.py:508
  2.0 0.0 copy-start
  2.0 14.5 %all_to_all.25.in_ref.own_ref = f32[8,64,256]{2,1,0:T(8,128)S(1)} all-to-all(f32[8,64,256]{2,1,0:T(8,128)S(1)} %get-tuple-element.26), channel_id=1, replica_groups=mesh['row'=8,'col'=32] {'row'}, dimensions={0} | all-to-all | bytes 1048576 | tf_op jit(solution)/shard_map/all_to_all | solution.py:505
  16.5 0.0 copy-done
  16.5 1.3 %ahead.1 = (f32[512,128]{1,0:T(8,128)}, f32[4,2048]{1,0:T(4,128)S(1)}, f32[4,2048]{1,0:T(4,128)S(1)}) custom-call(bf16[2,512,256]{2,1,0:T(8,128)(2,1)S(1)} %copy-done, f32[8,256]{1,0:T(8,128)S(1)} %get-tuple-element.25.twist_ref, f32[8,64,256]{2,1,0:T(8,128)S(1)} %all_to_all.25.in_ref.own_ref), custom_call_target="tpu_custom_call" | custom-call | tf_op jit(solution)/shard_map/ahead/pallas_call | solution.py:512
  17.9 14.0 %all-to-all-start.1 = ((f32[256,1,256]{2,1,0:T(1,128)}), f32[256,1,256]{2,1,0:T(1,128)S(1)}, u32[]{:S(2)}, u32[]{:S(2)}) async-start(f32[256,1,256]{2,1,0:T(1,128)} %bitcast), calls=%async_computation.1 | async-start | bytes 524288 | tf_op jit(solution)/shard_map/all_to_all | solution.py:505
  31.8 1.4 %collective-permute-start = (f32[4,2048]{1,0:T(4,128)S(1)}, f32[4,2048]{1,0:T(4,128)S(1)}, u32[]{:S(2)}, u32[]{:S(2)}) collective-permute-start(f32[4,2048]{1,0:T(4,128)S(1)} %get-tuple-element.28), channel_id=1, source_target_pairs={{0,32},{32,64},{64,96},{96,128},{128,160},{160,192},{192,224},{224... | collective-permute-start | bytes 98312 | tf_op jit(solution)/shard_map/ppermute | solution.py:518
  33.3 2.5 %collective-permute-start.1 = (f32[4,2048]{1,0:T(4,128)S(1)}, f32[4,2048]{1,0:T(4,128)S(1)}, u32[]{:S(2)}, u32[]{:S(2)}) collective-permute-start(f32[4,2048]{1,0:T(4,128)S(1)} %get-tuple-element.29), channel_id=1, source_target_pairs={{32,0},{64,32},{96,64},{128,96},{160,128},{192,160},{224,192},{1,2... | collective-permute-start | bytes 98312 | tf_op jit(solution)/shard_map/ppermute | solution.py:519
  35.8 1.9 %collective-permute-done.before_far = f32[4,2048]{1,0:T(4,128)S(1)} collective-permute-done((f32[4,2048]{1,0:T(4,128)S(1)}, f32[4,2048]{1,0:T(4,128)S(1)}, u32[]{:S(2)}, u32[]{:S(2)}) %collective-permute-start) | collective-permute-done | bytes 32800 | tf_op jit(solution)/shard_map/ppermute | solution.py:518
  37.7 0.0 copy-start.5
  37.7 0.0 collective-permute-done.1.after_far
  37.7 0.0 copy-start.6
  37.7 0.6 copy-done.5
  38.3 0.0 copy-done.6
  38.3 0.0 copy-start.1
  38.3 0.0 copy-start.2
  38.3 1.7 %state.1 = (bf16[576,160]{1,0:T(8,128)(2,1)S(1)}, bf16[576,160]{1,0:T(8,128)(2,1)S(1)}, bf16[160,576]{1,0:T(8,128)(2,1)S(1)}, bf16[160,2048]{1,0:T(8,128)(2,1)S(1)}, f32[2,24,2048]{2,1,0:T(8,128)S(1)}) custom-call(bf16[18,32]{1,0:T(8,128)(2,1)} %first_far.1, bf16[18,32]{1,0:T(8,128)(2,1)} %bitcast.16, f32[1,32]{1,0:T(1,128)} %bitcast.17, ...), custom_call_target="tpu_custom_call" | custom-call | tf_op jit(solution)/shard_map/state/pallas_call | solution.py:521
  40.0 6.4 %all-to-all-done.1 = f32[256,1,256]{2,1,0:T(1,128)S(1)} async-done(((f32[256,1,256]{2,1,0:T(1,128)}), f32[256,1,256]{2,1,0:T(1,128)S(1)}, u32[]{:S(2)}, u32[]{:S(2)}) %all-to-all-start.1) | async-done | bytes 262176 | tf_op jit(solution)/shard_map/all_to_all | solution.py:505
  46.5 0.0 copy-done.1
  46.5 0.0 copy-done.2
  46.5 1.8 %middle.1 = f32[768,128]{1,0:T(8,128)S(1)} custom-call(s32[1]{0:T(128)} %bitcast.4.place_ref, bf16[2,512,256]{2,1,0:T(8,128)(2,1)S(1)} %copy-done, f32[2,256,128]{2,1,0:T(8,128)S(1)} %copy-done.1, bf16[2,128,256]{2,1,0:T(8,128)(2,1)S(1)} %copy-done.2, f32[512,128]{1,0:T(8,128)S(1)} %bitcast.13), custom_call_target="tpu_custom_call" | custom-call | tf_op jit(solution)/shard_map/middle/pallas_call | solution.py:542
  48.3 0.0 copy-start.3
  48.3 0.0 copy-start.4
  48.3 26.6 %all_to_all.26 = f32[256,1,384]{2,1,0:T(1,128)S(1)} all-to-all(f32[256,1,384]{2,1,0:T(1,128)S(1)} %bitcast.12), channel_id=1, replica_groups=mesh['row'=8,'col'=32] {'col','row'}, dimensions={0} | all-to-all | bytes 786432 | tf_op jit(solution)/shard_map/all_to_all | solution.py:505
  74.9 0.0 copy-done.3
  74.9 0.0 copy-done.4
  74.9 4.6 %closure.1 = f32[8,40,256]{2,1,0:T(8,128)S(1)} custom-call(bf16[576,160]{1,0:T(8,128)(2,1)S(1)} %get-tuple-element.35.w1_ref, bf16[576,160]{1,0:T(8,128)(2,1)S(1)} %get-tuple-element.36.w2_ref, bf16[160,576]{1,0:T(8,128)(2,1)S(1)} %get-tuple-element.37.turn_ref, bf16[160,2048]{1,0:T(8,128)(2,1)S(1)} %get-tuple-element.38.state_ref, ...), custom_call_target="tpu_custom_call" | custom-call | tf_op jit(solution)/shard_map/closure/pallas_call | solution.py:552
  79.5 11.6 %all_to_all.27.in_ref = f32[8,40,256]{2,1,0:T(8,128)S(1)} all-to-all(f32[8,40,256]{2,1,0:T(8,128)S(1)} %closure.1), channel_id=1, replica_groups=mesh['row'=8,'col'=32] {'row'}, dimensions={0} | all-to-all | bytes 655360 | tf_op jit(solution)/shard_map/all_to_all | solution.py:505
  91.2 0.8 unpack.1
  92.0 15.7 %all_to_all.28 = f32[32,1,1280]{2,1,0:T(1,128)S(1)} all-to-all(f32[32,1,1280]{2,1,0:T(1,128)S(1)} %bitcast.15), channel_id=1, replica_groups=mesh['row'=8,'col'=32] {'col'}, dimensions={0} | all-to-all | bytes 327680 | tf_op jit(solution)/shard_map/all_to_all | solution.py:505
  107.8 0.7 sums.1
Async XLA Ops:
  2.0 14.5 %copy-start = (bf16[2,512,256]{2,1,0:T(8,128)(2,1)S(1)}, bf16[2,512,256]{2,1,0:T(8,128)(2,1)}, u32[]{:S(2)}) copy-start(bf16[2,512,256]{2,1,0:T(8,128)(2,1)} %constant.25.clone.dft_ref) | copy-start | bytes 1572868
  17.9 28.6 %all-to-all-start.1 = ((f32[256,1,256]{2,1,0:T(1,128)}), f32[256,1,256]{2,1,0:T(1,128)S(1)}, u32[]{:S(2)}, u32[]{:S(2)}) async-start(f32[256,1,256]{2,1,0:T(1,128)} %bitcast), calls=%async_computation.1 | async-start | bytes 524288 | tf_op jit(solution)/shard_map/all_to_all | solution.py:505
  31.8 5.9 %collective-permute-start = (f32[4,2048]{1,0:T(4,128)S(1)}, f32[4,2048]{1,0:T(4,128)S(1)}, u32[]{:S(2)}, u32[]{:S(2)}) collective-permute-start(f32[4,2048]{1,0:T(4,128)S(1)} %get-tuple-element.28), channel_id=1, source_target_pairs={{0,32},{32,64},{64,96},{96,128},{128,160},{160,192},{192,224},{224... | collective-permute-start | bytes 98312 | tf_op jit(solution)/shard_map/ppermute | solution.py:518
  33.3 4.4 %collective-permute-start.1 = (f32[4,2048]{1,0:T(4,128)S(1)}, f32[4,2048]{1,0:T(4,128)S(1)}, u32[]{:S(2)}, u32[]{:S(2)}) collective-permute-start(f32[4,2048]{1,0:T(4,128)S(1)} %get-tuple-element.29), channel_id=1, source_target_pairs={{32,0},{64,32},{96,64},{128,96},{160,128},{192,160},{224,192},{1,2... | collective-permute-start | bytes 98312 | tf_op jit(solution)/shard_map/ppermute | solution.py:519
  37.7 0.6 copy-start.5
  37.7 0.6 copy-start.6
  38.3 8.1 %copy-start.1 = (f32[2,256,128]{2,1,0:T(8,128)S(1)}, f32[2,256,128]{2,1,0:T(8,128)}, u32[]{:S(2)}) copy-start(f32[2,256,128]{2,1,0:T(8,128)} %constant.27.clone.twist_ref) | copy-start | bytes 786436
  38.3 8.1 %copy-start.2 = (bf16[2,128,256]{2,1,0:T(8,128)(2,1)S(1)}, bf16[2,128,256]{2,1,0:T(8,128)(2,1)}, u32[]{:S(2)}) copy-start(bf16[2,128,256]{2,1,0:T(8,128)(2,1)} %constant.26.clone.group_ref) | copy-start | bytes 393220
  48.3 26.7 %copy-start.3 = (bf16[256,128]{1,0:T(8,128)(2,1)S(1)}, bf16[256,128]{1,0:T(8,128)(2,1)}, u32[]{:S(2)}) copy-start(bf16[256,128]{1,0:T(8,128)(2,1)} %constant.30.clone.take1_ref) | copy-start | bytes 196612
  48.3 26.7 %copy-start.4 = (bf16[256,128]{1,0:T(8,128)(2,1)S(1)}, bf16[256,128]{1,0:T(8,128)(2,1)}, u32[]{:S(2)}) copy-start(bf16[256,128]{1,0:T(8,128)(2,1)} %constant.31.clone.take2_ref) | copy-start | bytes 196612

commit v6 on v5

--- a/solution.py
+++ b/solution.py
@@ -327,11 +327,10 @@
     target[0:160, :] = build_ref[...].astype(bf16)
 
 
-def state_kernel(
-    first_far, second_far, bias_far, pick_far, before_far, after_far, own_ref,
-    w1_out, w2_out, turn_ref, state_low, field_ref,
-    build_ref, w1_ref, w2_ref, first_ref, second_ref, bias_ref, pick_ref,
-    before_ref, after_ref, sems,
+def bands_kernel(
+    first_far, second_far, bias_far, pick_far,
+    w1_out, w2_out, turn_ref,
+    w1_ref, w2_ref, first_ref, second_ref, bias_ref, pick_ref, sems,
 ):
     copies = [
         pltpu.make_async_copy(source, target, sems.at[k])
@@ -339,7 +338,6 @@
             (
                 (first_far, first_ref), (second_far, second_ref),
                 (bias_far, bias_ref), (pick_far, pick_ref),
-                (before_far, before_ref), (after_far, after_ref),
             )
         )
     ]
@@ -363,6 +361,18 @@
         moved2 = pltpu.roll(base2, j, 1) if j else base2
         w1_ref[rows, :] = moved1 + bias_part
         w2_ref[rows, :] = moved2
+    w1 = w1_ref[...]
+    turn_ref[...] = w1.T[:160].astype(bf16)
+    w1_out[...] = w1[:, :160].astype(bf16)
+    w2_out[...] = w2_ref[:, :160].astype(bf16)
+
+
+def closure_kernel(
+    w1_ref, w2_ref, turn_ref, own_ref, before_ref, after_ref,
+    dft_ref, twist_ref, take1_ref, take2_ref, in_ref,
+    out_ref,
+    field_ref, proj_ref, build_ref, state_low, scaled_low, grads, acts,
+):
     for c in range(2):
         field_ref[c, 20:24, :] = jnp.zeros((4, NX), f32)
         for r in range(8):
@@ -372,24 +382,11 @@
         field_ref[c, 0:2, :] = before_ref[2 * c : 2 * c + 2, :]
         field_ref[c, 18:20, :] = after_ref[2 * c : 2 * c + 2, :]
     fill_taps(build_ref, state_low, (field_ref[0], field_ref[1]), 1)
-    w1 = w1_ref[...]
-    turn_ref[...] = w1.T[:160].astype(bf16)
-    w1_out[...] = w1[:, :160].astype(bf16)
-    w2_out[...] = w2_ref[:, :160].astype(bf16)
-
-
-def closure_kernel(
-    w1_ref, w2_ref, turn_ref, state_ref, field_ref, dft_ref, twist_ref, take1_ref, take2_ref,
-    in_ref,
-    out_ref,
-    proj_ref, build_ref, state_low, scaled_low, grads, acts,
-):
     back_part(in_ref, dft_ref, twist_ref, proj_ref)
-    state_low[0:160, :] = state_ref[...]
     state_low[160:256, :] = jnp.zeros((96, NX), bf16)
     scaled_low[160:256, :] = jnp.zeros((96, NX), bf16)
     fill_taps(build_ref, scaled_low, (STEP * proj_ref[0], STEP * proj_ref[1]), -1)
-    active = jnp.tanh(dot(w1_ref[...], state_ref[...]))
+    active = jnp.tanh(dot(w1_ref[...], state_low[0:160, :]))
     acts[...] = active[32:544].astype(bf16)
     back = dot(w2_ref[...], scaled_low[0:160, :])
     grads[...] = (back * (1.0 - active * active)).astype(bf16)
@@ -519,29 +516,28 @@
     after = lax.ppermute(low, ("row", "col"), [(j, i) for i, j in up])
     modes = exchange(modes.reshape(DEV, 1, 256), every).reshape(512, 128)
     prepared = call(
-        state_kernel,
+        bands_kernel,
         [
-            shape(576, 160, dtype=bf16), shape(576, 160, dtype=bf16),
-            shape(160, 576, dtype=bf16), shape(160, NX, dtype=bf16), shape(2, WIDE, NX),
+            shape(576, 160, dtype=bf16), shape(576, 160, dtype=bf16), shape(160, 576, dtype=bf16),
         ],
         [
-            pltpu.VMEM((160, NX), f32), pltpu.VMEM((576, 256), f32), pltpu.VMEM((576, 256), f32),
+            pltpu.VMEM((576, 256), f32), pltpu.VMEM((576, 256), f32),
             pltpu.VMEM((18, FEATS), bf16), pltpu.VMEM((18, FEATS), bf16),
             pltpu.VMEM((1, FEATS), f32), pltpu.VMEM((2, 18, 256), bf16),
-            pltpu.VMEM((4, NX), f32), pltpu.VMEM((4, NX), f32),
-            pltpu.SemaphoreType.DMA((6,)),
+            pltpu.SemaphoreType.DMA((4,)),
         ],
-        count=7,
-        remote=6,
-        name="state",
+        count=4,
+        remote=4,
+        name="bands",
     )(
         far(first_kernel), far(second_kernel.T), far(first_bias.reshape(1, FEATS)),
-        far(jnp.asarray(np.stack([first_pick, second_pick]))), far(before), far(after), lines,
-    )
-    modes, prepared = lax.optimization_barrier((modes, prepared))
+        far(jnp.asarray(np.stack([first_pick, second_pick]))),
+    )
+    modes, prepared, before, after = lax.optimization_barrier((modes, prepared, before, after))
     modes = call(middle_kernel, shape(768, 128), scalars=1, count=5, name="middle")(place, dft, twist_y, group, modes)
     modes = exchange(modes.reshape(DEV, 1, 384), every).reshape(768, 128)
     scratch = [
+        pltpu.VMEM((2, WIDE, NX), f32),
         pltpu.VMEM((2, WIDE, NX), f32),
         pltpu.VMEM((160, NX), f32),
         pltpu.VMEM((256, NX), bf16),
@@ -550,8 +546,8 @@
         pltpu.VMEM((512, NX), bf16),
     ]
     result = call(
-        closure_kernel, shape(8, 40, 256), scratch, count=10, name="closure", mib=40
-    )(*prepared, dft, twist_x, first_take, second_take, modes)
+        closure_kernel, shape(8, 40, 256), scratch, count=11, name="closure", mib=40
+    )(*prepared, lines, before, after, dft, twist_x, first_take, second_take, modes)
     result = exchange(result, "row")
     grad_state, part = call(
         unpack_kernel, [shape(2, 256, 128), shape(320, 128)], count=1, name="unpack"

time: 109 us -> 107 us (0.982)
  blocking collectives: 68.5 us -> 66.2 us
    all_to_all x4, blocking collectives: 68.5 us -> 66.2 us  [exchange(): return lax.all_to_all(values, axis, 0, 0, tiled=True)]
    all_to_all x1, waiting for transfers between devices: 6.45 us -> 8.74 us  [exchange(): return lax.all_to_all(values, axis, 0, 0, tiled=True)]
    ppermute x1, waiting for transfers between devices: 1.88 us -> 0.47 us  [shards(): before = lax.ppermute(high, ('row', 'col'), up)]
  transfers between devices with their start and end apart: 3 -> 3, of which waited for: 2 -> 2; matrix products, arithmetic and copies ran while one was open for 0% -> 0% of each run, Pallas kernels for 2% -> 1%
where the time goes in v6:
time: 107 us; the launch traced here: 106 us
  blocking collectives  66.2 us (62%)
  starting transfers between devices  18 us (17%)
  Pallas kernels  12.1 us (11%)
  waiting for transfers between devices  9.21 us (9%)
    all_to_all x4, blocking collectives, exchange(): return lax.all_to_all(values, axis, 0, 0, tiled=True)  66.2 us
    all_to_all x1, starting transfers between devices, exchange(): return lax.all_to_all(values, axis, 0, 0, tiled=True)  14 us
    all_to_all x1, waiting for transfers between devices, exchange(): return lax.all_to_all(values, axis, 0, 0, tiled=True)  8.74 us
    pallas_call x1, Pallas kernels, shards(): call(closure_kernel, shape(8, 40, 256), scratch, count=11, name='closure'...  4.65 us
    ppermute x1, starting transfers between devices, shards(): after = lax.ppermute(low, ('row', 'col'), [(j, i) for i, j in up])  2.55 us
  transfers between devices with their start and end apart: 3, of which 2 were waited for; matrix products, arithmetic and copies ran while one was open for 0% of the time, Pallas kernels for 1%

profile of v6, /device:TPU:1, one launch (start us, length us, event | category | flops | bytes accessed | tf_op | source)
XLA Modules:
  0.0 106.2 jit_solution(6346196398098571274)
XLA Ops:
  0.6 1.4 %pack.1 = (f32[8,64,256]{2,1,0:T(8,128)S(1)}, f32[8,256]{1,0:T(8,128)S(1)}) custom-call(f32[2,256,128]{2,1,0:T(8,128)} %cot_ref.1, f32[2,256,128]{2,1,0:T(8,128)} %state_ref.1, f32[8,256]{1,0:T(8,128)} %constant.28.clone.twist_far), custom_call_target="tpu_custom_call" | custom-call | tf_op jit(solution)/shard_map/pack/pallas_call | solution.py:505
  2.0 0.0 copy-start
  2.0 14.5 %all_to_all.25.in_ref.own_ref = f32[8,64,256]{2,1,0:T(8,128)S(1)} all-to-all(f32[8,64,256]{2,1,0:T(8,128)S(1)} %get-tuple-element.24), channel_id=1, replica_groups=mesh['row'=8,'col'=32] {'row'}, dimensions={0} | all-to-all | bytes 1048576 | tf_op jit(solution)/shard_map/all_to_all | solution.py:502
  16.5 0.0 copy-done
  16.5 1.3 %ahead.1 = (f32[512,128]{1,0:T(8,128)}, f32[4,2048]{1,0:T(4,128)S(1)}, f32[4,2048]{1,0:T(4,128)S(1)}) custom-call(bf16[2,512,256]{2,1,0:T(8,128)(2,1)S(1)} %copy-done, f32[8,256]{1,0:T(8,128)S(1)} %get-tuple-element.23.twist_ref, f32[8,64,256]{2,1,0:T(8,128)S(1)} %all_to_all.25.in_ref.own_ref), custom_call_target="tpu_custom_call" | custom-call | tf_op jit(solution)/shard_map/ahead/pallas_call | solution.py:509
  17.9 0.0 copy-start.1
  17.9 0.0 copy-start.2
  17.9 14.0 %all-to-all-start.1 = ((f32[256,1,256]{2,1,0:T(1,128)}), f32[256,1,256]{2,1,0:T(1,128)S(1)}, u32[]{:S(2)}, u32[]{:S(2)}) async-start(f32[256,1,256]{2,1,0:T(1,128)} %bitcast), calls=%async_computation.1 | async-start | bytes 524288 | tf_op jit(solution)/shard_map/all_to_all | solution.py:502
  31.8 1.4 %collective-permute-start = (f32[4,2048]{1,0:T(4,128)S(1)}, f32[4,2048]{1,0:T(4,128)S(1)}, u32[]{:S(2)}, u32[]{:S(2)}) collective-permute-start(f32[4,2048]{1,0:T(4,128)S(1)} %get-tuple-element.29), channel_id=1, source_target_pairs={{0,32},{32,64},{64,96},{96,128},{128,160},{160,192},{192,224},{224... | collective-permute-start | bytes 98312 | tf_op jit(solution)/shard_map/ppermute | solution.py:515
  33.3 2.5 %collective-permute-start.1 = (f32[4,2048]{1,0:T(4,128)S(1)}, f32[4,2048]{1,0:T(4,128)S(1)}, u32[]{:S(2)}, u32[]{:S(2)}) collective-permute-start(f32[4,2048]{1,0:T(4,128)S(1)} %get-tuple-element.30), channel_id=1, source_target_pairs={{32,0},{64,32},{96,64},{128,96},{160,128},{192,160},{224,192},{1,2... | collective-permute-start | bytes 98312 | tf_op jit(solution)/shard_map/ppermute | solution.py:516
  35.8 1.4 %bands.1 = (bf16[576,160]{1,0:T(8,128)(2,1)S(1)}, bf16[576,160]{1,0:T(8,128)(2,1)S(1)}, bf16[160,576]{1,0:T(8,128)(2,1)S(1)}) custom-call(bf16[18,32]{1,0:T(8,128)(2,1)} %first_far.1, bf16[18,32]{1,0:T(8,128)(2,1)} %bitcast.16, f32[1,32]{1,0:T(1,128)} %bitcast.17, bf16[2,18,256]{2,1,0:T(8,128)(2,1)} %constant.29.clone.pick_far), custom_call_target="tpu_custom_call" | custom-call | tf_op jit(solution)/shard_map/bands/pallas_call | solution.py:518
  37.2 0.5 collective-permute-done.before_ref
  37.7 0.0 collective-permute-done.1.after_ref
  37.7 8.7 %all-to-all-done.1 = f32[256,1,256]{2,1,0:T(1,128)S(1)} async-done(((f32[256,1,256]{2,1,0:T(1,128)}), f32[256,1,256]{2,1,0:T(1,128)S(1)}, u32[]{:S(2)}, u32[]{:S(2)}) %all-to-all-start.1) | async-done | bytes 262176 | tf_op jit(solution)/shard_map/all_to_all | solution.py:502
  46.5 0.0 copy-done.1
  46.5 0.0 copy-done.2
  46.5 1.8 %middle.1 = f32[768,128]{1,0:T(8,128)S(1)} custom-call(s32[1]{0:T(128)} %bitcast.4.place_ref, bf16[2,512,256]{2,1,0:T(8,128)(2,1)S(1)} %copy-done, f32[2,256,128]{2,1,0:T(8,128)S(1)} %copy-done.1, bf16[2,128,256]{2,1,0:T(8,128)(2,1)S(1)} %copy-done.2, f32[512,128]{1,0:T(8,128)S(1)} %bitcast.13), custom_call_target="tpu_custom_call" | custom-call | tf_op jit(solution)/shard_map/middle/pallas_call | solution.py:537
  48.3 0.0 copy-start.3
  48.3 0.0 copy-start.4
  48.3 24.3 %all_to_all.26 = f32[256,1,384]{2,1,0:T(1,128)S(1)} all-to-all(f32[256,1,384]{2,1,0:T(1,128)S(1)} %bitcast.11), channel_id=1, replica_groups=mesh['row'=8,'col'=32] {'col','row'}, dimensions={0} | all-to-all | bytes 786432 | tf_op jit(solution)/shard_map/all_to_all | solution.py:502
  72.6 0.0 copy-done.3
  72.6 0.0 copy-done.4
  72.6 4.6 %closure.1 = f32[8,40,256]{2,1,0:T(8,128)S(1)} custom-call(bf16[576,160]{1,0:T(8,128)(2,1)S(1)} %get-tuple-element.31.w1_ref, bf16[576,160]{1,0:T(8,128)(2,1)S(1)} %get-tuple-element.32.w2_ref, bf16[160,576]{1,0:T(8,128)(2,1)S(1)} %get-tuple-element.33.turn_ref, f32[8,64,256]{2,1,0:T(8,128)S(1)} %all_to_all.25.in_ref.own_ref, ...), custom_call_target="tpu_custom_call" | custom-call | tf_op jit(solution)/shard_map/closure/pallas_call | solution.py:548
  77.3 11.6 %all_to_all.27.in_ref = f32[8,40,256]{2,1,0:T(8,128)S(1)} all-to-all(f32[8,40,256]{2,1,0:T(8,128)S(1)} %closure.1), channel_id=1, replica_groups=mesh['row'=8,'col'=32] {'row'}, dimensions={0} | all-to-all | bytes 655360 | tf_op jit(solution)/shard_map/all_to_all | solution.py:502
  88.9 0.8 unpack.1
  89.8 15.7 %all_to_all.28 = f32[32,1,1280]{2,1,0:T(1,128)S(1)} all-to-all(f32[32,1,1280]{2,1,0:T(1,128)S(1)} %bitcast.15), channel_id=1, replica_groups=mesh['row'=8,'col'=32] {'col'}, dimensions={0} | all-to-all | bytes 327680 | tf_op jit(solution)/shard_map/all_to_all | solution.py:502
  105.5 0.7 sums.1
Async XLA Ops:
  2.0 14.5 %copy-start = (bf16[2,512,256]{2,1,0:T(8,128)(2,1)S(1)}, bf16[2,512,256]{2,1,0:T(8,128)(2,1)}, u32[]{:S(2)}) copy-start(bf16[2,512,256]{2,1,0:T(8,128)(2,1)} %constant.25.clone.dft_ref) | copy-start | bytes 1572868
  17.9 28.6 %copy-start.1 = (f32[2,256,128]{2,1,0:T(8,128)S(1)}, f32[2,256,128]{2,1,0:T(8,128)}, u32[]{:S(2)}) copy-start(f32[2,256,128]{2,1,0:T(8,128)} %constant.27.clone.twist_ref) | copy-start | bytes 786436
  17.9 28.6 %copy-start.2 = (bf16[2,128,256]{2,1,0:T(8,128)(2,1)S(1)}, bf16[2,128,256]{2,1,0:T(8,128)(2,1)}, u32[]{:S(2)}) copy-start(bf16[2,128,256]{2,1,0:T(8,128)(2,1)} %constant.26.clone.group_ref) | copy-start | bytes 393220
  17.9 28.6 %all-to-all-start.1 = ((f32[256,1,256]{2,1,0:T(1,128)}), f32[256,1,256]{2,1,0:T(1,128)S(1)}, u32[]{:S(2)}, u32[]{:S(2)}) async-start(f32[256,1,256]{2,1,0:T(1,128)} %bitcast), calls=%async_computation.1 | async-start | bytes 524288 | tf_op jit(solution)/shard_map/all_to_all | solution.py:502
  31.8 5.9 %collective-permute-start = (f32[4,2048]{1,0:T(4,128)S(1)}, f32[4,2048]{1,0:T(4,128)S(1)}, u32[]{:S(2)}, u32[]{:S(2)}) collective-permute-start(f32[4,2048]{1,0:T(4,128)S(1)} %get-tuple-element.29), channel_id=1, source_target_pairs={{0,32},{32,64},{64,96},{96,128},{128,160},{160,192},{192,224},{224... | collective-permute-start | bytes 98312 | tf_op jit(solution)/shard_map/ppermute | solution.py:515
  33.3 4.4 %collective-permute-start.1 = (f32[4,2048]{1,0:T(4,128)S(1)}, f32[4,2048]{1,0:T(4,128)S(1)}, u32[]{:S(2)}, u32[]{:S(2)}) collective-permute-start(f32[4,2048]{1,0:T(4,128)S(1)} %get-tuple-element.30), channel_id=1, source_target_pairs={{32,0},{64,32},{96,64},{128,96},{160,128},{192,160},{224,192},{1,2... | collective-permute-start | bytes 98312 | tf_op jit(solution)/shard_map/ppermute | solution.py:516
  48.3 24.4 %copy-start.3 = (bf16[256,128]{1,0:T(8,128)(2,1)S(1)}, bf16[256,128]{1,0:T(8,128)(2,1)}, u32[]{:S(2)}) copy-start(bf16[256,128]{1,0:T(8,128)(2,1)} %constant.31.clone.take2_ref) | copy-start | bytes 196612
  48.3 24.4 %copy-start.4 = (bf16[256,128]{1,0:T(8,128)(2,1)S(1)}, bf16[256,128]{1,0:T(8,128)(2,1)}, u32[]{:S(2)}) copy-start(bf16[256,128]{1,0:T(8,128)(2,1)} %constant.30.clone.take1_ref) | copy-start | bytes 196612

commit v7 on v6

--- a/solution.py
+++ b/solution.py
@@ -442,13 +442,16 @@
             out_ref[r, 16 * c : 16 * c + 16, :] = total[:, 256 * r : 256 * r + 256]
 
 
-def unpack_kernel(in_ref, out_ref, part_ref):
+def part_kernel(in_ref, part_ref):
     total = in_ref[0, 32:40, :]
     for r in range(1, 8):
         total = total + in_ref[r, 32:40, :]
     ten = jnp.concatenate([total[:, 0:128], total[0:2, 128:256]], 0)
     for d in range(COLS):
         part_ref[10 * d : 10 * d + 10, :] = ten
+
+
+def unpack_kernel(in_ref, out_ref):
     for c in range(2):
         lines = jnp.concatenate([in_ref[r, 16 * c : 16 * c + 16, :] for r in range(8)], 0)
         out_ref[c] = lines.T
@@ -549,13 +552,12 @@
         closure_kernel, shape(8, 40, 256), scratch, count=11, name="closure", mib=40
     )(*prepared, lines, before, after, dft, twist_x, first_take, second_take, modes)
     result = exchange(result, "row")
-    grad_state, part = call(
-        unpack_kernel, [shape(2, 256, 128), shape(320, 128)], count=1, name="unpack"
-    )(result)
+    part = call(part_kernel, shape(320, 128), count=1, name="part")(result)
     part = exchange(part.reshape(COLS, 1, 1280), "col").reshape(320, 128)
     grad_first, grad_second, grad_bias = call(
         sums_kernel, [shape(18, 32), shape(18, 32), shape(1, 32)], count=1, name="sums"
     )(part)
+    grad_state = call(unpack_kernel, shape(2, 256, 128), count=1, name="unpack")(result)
     return grad_state, grad_first, grad_second.T, grad_bias.reshape(32)
 
 

time: 107 us -> 107 us (level)
  blocking collectives: 66.2 us -> 50.5 us
  waiting for transfers between devices: 9.21 us -> 19.8 us
  starting transfers between devices: 18 us -> 22.6 us
    all_to_all x4 -> x3, blocking collectives: 66.2 us -> 50.5 us  [exchange(): return lax.all_to_all(values, axis, 0, 0, tiled=True)]
    all_to_all x1 -> x2, waiting for transfers between devices: 8.74 us -> 19.3 us  [exchange(): return lax.all_to_all(values, axis, 0, 0, tiled=True)]
    all_to_all x1 -> x2, starting transfers between devices: 14 us -> 18.6 us  [exchange(): return lax.all_to_all(values, axis, 0, 0, tiled=True)]
  transfers between devices with their start and end apart: 3 -> 4, of which waited for: 2 -> 3; matrix products, arithmetic and copies ran while one was open for 0% -> 0% of each run, Pallas kernels for 1% -> 2%
where the time goes in v7:
time: 107 us; the launch traced here: 106 us
  blocking collectives  50.5 us (47%)
  starting transfers between devices  22.6 us (21%)
  waiting for transfers between devices  19.8 us (19%)
  Pallas kernels  12.8 us (12%)
    all_to_all x3, blocking collectives, exchange(): return lax.all_to_all(values, axis, 0, 0, tiled=True)  50.5 us
    all_to_all x2, waiting for transfers between devices, exchange(): return lax.all_to_all(values, axis, 0, 0, tiled=True)  19.3 us
    all_to_all x2, starting transfers between devices, exchange(): return lax.all_to_all(values, axis, 0, 0, tiled=True)  18.6 us
    pallas_call x1, Pallas kernels, shards(): call(closure_kernel, shape(8, 40, 256), scratch, count=11, name='closure'...  4.65 us
    ppermute x1, starting transfers between devices, shards(): after = lax.ppermute(low, ('row', 'col'), [(j, i) for i, j in up])  2.55 us
  transfers between devices with their start and end apart: 4, of which 3 were waited for; matrix products, arithmetic and copies ran while one was open for 0% of the time, Pallas kernels for 2%

profile of v7, /device:TPU:1, one launch (start us, length us, event | category | flops | bytes accessed | tf_op | source)
XLA Modules:
  0.0 106.4 jit_solution(3110812102383758270)
XLA Ops:
  0.6 1.4 %pack.1 = (f32[8,64,256]{2,1,0:T(8,128)S(1)}, f32[8,256]{1,0:T(8,128)S(1)}) custom-call(f32[2,256,128]{2,1,0:T(8,128)} %cot_ref.1, f32[2,256,128]{2,1,0:T(8,128)} %state_ref.1, f32[8,256]{1,0:T(8,128)} %constant.28.clone.twist_far), custom_call_target="tpu_custom_call" | custom-call | tf_op jit(solution)/shard_map/pack/pallas_call | solution.py:508
  2.0 0.0 copy-start
  2.0 14.5 %all_to_all.25.in_ref.own_ref = f32[8,64,256]{2,1,0:T(8,128)S(1)} all-to-all(f32[8,64,256]{2,1,0:T(8,128)S(1)} %get-tuple-element.22), channel_id=1, replica_groups=mesh['row'=8,'col'=32] {'row'}, dimensions={0} | all-to-all | bytes 1048576 | tf_op jit(solution)/shard_map/all_to_all | solution.py:505
  16.5 0.0 copy-done
  16.5 1.3 %ahead.1 = (f32[512,128]{1,0:T(8,128)}, f32[4,2048]{1,0:T(4,128)S(1)}, f32[4,2048]{1,0:T(4,128)S(1)}) custom-call(bf16[2,512,256]{2,1,0:T(8,128)(2,1)S(1)} %copy-done, f32[8,256]{1,0:T(8,128)S(1)} %get-tuple-element.21.twist_ref, f32[8,64,256]{2,1,0:T(8,128)S(1)} %all_to_all.25.in_ref.own_ref), custom_call_target="tpu_custom_call" | custom-call | tf_op jit(solution)/shard_map/ahead/pallas_call | solution.py:512
  17.9 0.0 copy-start.1
  17.9 0.0 copy-start.2
  17.9 14.0 %all-to-all-start.1 = ((f32[256,1,256]{2,1,0:T(1,128)}), f32[256,1,256]{2,1,0:T(1,128)S(1)}, u32[]{:S(2)}, u32[]{:S(2)}) async-start(f32[256,1,256]{2,1,0:T(1,128)} %bitcast), calls=%async_computation.1 | async-start | bytes 524288 | tf_op jit(solution)/shard_map/all_to_all | solution.py:505
  31.8 1.4 %collective-permute-start = (f32[4,2048]{1,0:T(4,128)S(1)}, f32[4,2048]{1,0:T(4,128)S(1)}, u32[]{:S(2)}, u32[]{:S(2)}) collective-permute-start(f32[4,2048]{1,0:T(4,128)S(1)} %get-tuple-element.27), channel_id=1, source_target_pairs={{0,32},{32,64},{64,96},{96,128},{128,160},{160,192},{192,224},{224... | collective-permute-start | bytes 98312 | tf_op jit(solution)/shard_map/ppermute | solution.py:518
  33.3 2.5 %collective-permute-start.1 = (f32[4,2048]{1,0:T(4,128)S(1)}, f32[4,2048]{1,0:T(4,128)S(1)}, u32[]{:S(2)}, u32[]{:S(2)}) collective-permute-start(f32[4,2048]{1,0:T(4,128)S(1)} %get-tuple-element.28), channel_id=1, source_target_pairs={{32,0},{64,32},{96,64},{128,96},{160,128},{192,160},{224,192},{1,2... | collective-permute-start | bytes 98312 | tf_op jit(solution)/shard_map/ppermute | solution.py:519
  35.8 1.4 %bands.1 = (bf16[576,160]{1,0:T(8,128)(2,1)S(1)}, bf16[576,160]{1,0:T(8,128)(2,1)S(1)}, bf16[160,576]{1,0:T(8,128)(2,1)S(1)}) custom-call(bf16[18,32]{1,0:T(8,128)(2,1)} %first_far.1, bf16[18,32]{1,0:T(8,128)(2,1)} %bitcast.15, f32[1,32]{1,0:T(1,128)} %bitcast.16, bf16[2,18,256]{2,1,0:T(8,128)(2,1)} %constant.29.clone.pick_far), custom_call_target="tpu_custom_call" | custom-call | tf_op jit(solution)/shard_map/bands/pallas_call | solution.py:521
  37.2 0.5 collective-permute-done.before_ref
  37.7 0.0 collective-permute-done.1.after_ref
  37.7 8.7 %all-to-all-done.1 = f32[256,1,256]{2,1,0:T(1,128)S(1)} async-done(((f32[256,1,256]{2,1,0:T(1,128)}), f32[256,1,256]{2,1,0:T(1,128)S(1)}, u32[]{:S(2)}, u32[]{:S(2)}) %all-to-all-start.1) | async-done | bytes 262176 | tf_op jit(solution)/shard_map/all_to_all | solution.py:505
  46.5 0.0 copy-done.1
  46.5 0.0 copy-done.2
  46.5 1.8 %middle.1 = f32[768,128]{1,0:T(8,128)S(1)} custom-call(s32[1]{0:T(128)} %bitcast.4.place_ref, bf16[2,512,256]{2,1,0:T(8,128)(2,1)S(1)} %copy-done, f32[2,256,128]{2,1,0:T(8,128)S(1)} %copy-done.1, bf16[2,128,256]{2,1,0:T(8,128)(2,1)S(1)} %copy-done.2, f32[512,128]{1,0:T(8,128)S(1)} %bitcast.13), custom_call_target="tpu_custom_call" | custom-call | tf_op jit(solution)/shard_map/middle/pallas_call | solution.py:540
  48.3 0.0 copy-start.3
  48.3 0.0 copy-start.4
  48.3 24.3 %all_to_all.26 = f32[256,1,384]{2,1,0:T(1,128)S(1)} all-to-all(f32[256,1,384]{2,1,0:T(1,128)S(1)} %bitcast.11), channel_id=1, replica_groups=mesh['row'=8,'col'=32] {'col','row'}, dimensions={0} | all-to-all | bytes 786432 | tf_op jit(solution)/shard_map/all_to_all | solution.py:505
  72.6 0.0 copy-done.3
  72.6 0.0 copy-done.4
  72.6 4.6 %closure.1 = f32[8,40,256]{2,1,0:T(8,128)S(1)} custom-call(bf16[576,160]{1,0:T(8,128)(2,1)S(1)} %get-tuple-element.29.w1_ref, bf16[576,160]{1,0:T(8,128)(2,1)S(1)} %get-tuple-element.30.w2_ref, bf16[160,576]{1,0:T(8,128)(2,1)S(1)} %get-tuple-element.31.turn_ref, f32[8,64,256]{2,1,0:T(8,128)S(1)} %all_to_all.25.in_ref.own_ref, ...), custom_call_target="tpu_custom_call" | custom-call | tf_op jit(solution)/shard_map/closure/pallas_call | solution.py:551
  77.3 11.6 %all_to_all.27.in_ref = f32[8,40,256]{2,1,0:T(8,128)S(1)} all-to-all(f32[8,40,256]{2,1,0:T(8,128)S(1)} %closure.1), channel_id=1, replica_groups=mesh['row'=8,'col'=32] {'row'}, dimensions={0} | all-to-all | bytes 655360 | tf_op jit(solution)/shard_map/all_to_all | solution.py:505
  88.9 0.7 part.1
  89.6 4.6 %all-to-all-start.4 = ((f32[32,1,1280]{2,1,0:T(1,128)}), f32[32,1,1280]{2,1,0:T(1,128)S(1)}, u32[]{:S(2)}, u32[]{:S(2)}) async-start(f32[32,1,1280]{2,1,0:T(1,128)} %bitcast.7), calls=%async_computation.4 | async-start | bytes 327680 | tf_op jit(solution)/shard_map/all_to_all | solution.py:505
  94.2 0.8 unpack.1
  95.0 10.6 %all-to-all-done.4 = f32[32,1,1280]{2,1,0:T(1,128)S(1)} async-done(((f32[32,1,1280]{2,1,0:T(1,128)}), f32[32,1,1280]{2,1,0:T(1,128)S(1)}, u32[]{:S(2)}, u32[]{:S(2)}) %all-to-all-start.4) | async-done | bytes 163872 | tf_op jit(solution)/shard_map/all_to_all | solution.py:505
  105.6 0.7 sums.1
Async XLA Ops:
  2.0 14.5 %copy-start = (bf16[2,512,256]{2,1,0:T(8,128)(2,1)S(1)}, bf16[2,512,256]{2,1,0:T(8,128)(2,1)}, u32[]{:S(2)}) copy-start(bf16[2,512,256]{2,1,0:T(8,128)(2,1)} %constant.25.clone.dft_ref) | copy-start | bytes 1572868
  17.9 28.6 %copy-start.1 = (f32[2,256,128]{2,1,0:T(8,128)S(1)}, f32[2,256,128]{2,1,0:T(8,128)}, u32[]{:S(2)}) copy-start(f32[2,256,128]{2,1,0:T(8,128)} %constant.27.clone.twist_ref) | copy-start | bytes 786436
  17.9 28.6 %copy-start.2 = (bf16[2,128,256]{2,1,0:T(8,128)(2,1)S(1)}, bf16[2,128,256]{2,1,0:T(8,128)(2,1)}, u32[]{:S(2)}) copy-start(bf16[2,128,256]{2,1,0:T(8,128)(2,1)} %constant.26.clone.group_ref) | copy-start | bytes 393220
  17.9 28.6 %all-to-all-start.1 = ((f32[256,1,256]{2,1,0:T(1,128)}), f32[256,1,256]{2,1,0:T(1,128)S(1)}, u32[]{:S(2)}, u32[]{:S(2)}) async-start(f32[256,1,256]{2,1,0:T(1,128)} %bitcast), calls=%async_computation.1 | async-start | bytes 524288 | tf_op jit(solution)/shard_map/all_to_all | solution.py:505
  31.8 5.9 %collective-permute-start = (f32[4,2048]{1,0:T(4,128)S(1)}, f32[4,2048]{1,0:T(4,128)S(1)}, u32[]{:S(2)}, u32[]{:S(2)}) collective-permute-start(f32[4,2048]{1,0:T(4,128)S(1)} %get-tuple-element.27), channel_id=1, source_target_pairs={{0,32},{32,64},{64,96},{96,128},{128,160},{160,192},{192,224},{224... | collective-permute-start | bytes 98312 | tf_op jit(solution)/shard_map/ppermute | solution.py:518
  33.3 4.4 %collective-permute-start.1 = (f32[4,2048]{1,0:T(4,128)S(1)}, f32[4,2048]{1,0:T(4,128)S(1)}, u32[]{:S(2)}, u32[]{:S(2)}) collective-permute-start(f32[4,2048]{1,0:T(4,128)S(1)} %get-tuple-element.28), channel_id=1, source_target_pairs={{32,0},{64,32},{96,64},{128,96},{160,128},{192,160},{224,192},{1,2... | collective-permute-start | bytes 98312 | tf_op jit(solution)/shard_map/ppermute | solution.py:519
  48.3 24.4 %copy-start.3 = (bf16[256,128]{1,0:T(8,128)(2,1)S(1)}, bf16[256,128]{1,0:T(8,128)(2,1)}, u32[]{:S(2)}) copy-start(bf16[256,128]{1,0:T(8,128)(2,1)} %constant.31.clone.take2_ref) | copy-start | bytes 196612
  48.3 24.4 %copy-start.4 = (bf16[256,128]{1,0:T(8,128)(2,1)S(1)}, bf16[256,128]{1,0:T(8,128)(2,1)}, u32[]{:S(2)}) copy-start(bf16[256,128]{1,0:T(8,128)(2,1)} %constant.30.clone.take1_ref) | copy-start | bytes 196612
  89.6 16.0 %all-to-all-start.4 = ((f32[32,1,1280]{2,1,0:T(1,128)}), f32[32,1,1280]{2,1,0:T(1,128)S(1)}, u32[]{:S(2)}, u32[]{:S(2)}) async-start(f32[32,1,1280]{2,1,0:T(1,128)} %bitcast.7), calls=%async_computation.4 | async-start | bytes 327680 | tf_op jit(solution)/shard_map/all_to_all | solution.py:505

commit v8 on v7

--- a/solution.py
+++ b/solution.py
@@ -451,13 +451,7 @@
         part_ref[10 * d : 10 * d + 10, :] = ten
 
 
-def unpack_kernel(in_ref, out_ref):
-    for c in range(2):
-        lines = jnp.concatenate([in_ref[r, 16 * c : 16 * c + 16, :] for r in range(8)], 0)
-        out_ref[c] = lines.T
-
-
-def sums_kernel(in_ref, first_ref, second_ref, bias_ref):
+def final_kernel(result_ref, in_ref, out_ref, first_ref, second_ref, bias_ref):
     total = in_ref[0:10, :]
     for d in range(1, COLS):
         total = total + in_ref[10 * d : 10 * d + 10, :]
@@ -469,6 +463,9 @@
     second_ref[0:1, :] = moved[1][9:10, 0:32]
     second_ref[1:11, :] = moved[2][:, 0:32]
     second_ref[11:18, :] = moved[3][0:7, 0:32]
+    for c in range(2):
+        lines = jnp.concatenate([result_ref[r, 16 * c : 16 * c + 16, :] for r in range(8)], 0)
+        out_ref[c] = lines.T
 
 
 def call(kernel, outs, scratch=(), scalars=0, count=0, name=None, remote=0, mib=8):
@@ -554,10 +551,12 @@
     result = exchange(result, "row")
     part = call(part_kernel, shape(320, 128), count=1, name="part")(result)
     part = exchange(part.reshape(COLS, 1, 1280), "col").reshape(320, 128)
-    grad_first, grad_second, grad_bias = call(
-        sums_kernel, [shape(18, 32), shape(18, 32), shape(1, 32)], count=1, name="sums"
-    )(part)
-    grad_state = call(unpack_kernel, shape(2, 256, 128), count=1, name="unpack")(result)
+    grad_state, grad_first, grad_second, grad_bias = call(
+        final_kernel,
+        [shape(2, 256, 128), shape(18, 32), shape(18, 32), shape(1, 32)],
+        count=2,
+        name="final",
+    )(result, part)
     return grad_state, grad_first, grad_second.T, grad_bias.reshape(32)
 
 

time: 107 us -> 106 us (level)
  blocking collectives: 50.5 us -> 66.2 us
  waiting for transfers between devices: 19.8 us -> 9.21 us
  starting transfers between devices: 22.6 us -> 18 us
  Pallas kernels: 12.8 us -> 11.5 us
    all_to_all x3 -> x4, blocking collectives: 50.5 us -> 66.2 us  [exchange(): return lax.all_to_all(values, axis, 0, 0, tiled=True)]
    all_to_all x2 -> x1, waiting for transfers between devices: 19.3 us -> 8.74 us  [exchange(): return lax.all_to_all(values, axis, 0, 0, tiled=True)]
    all_to_all x2 -> x1, starting transfers between devices: 18.6 us -> 14 us  [exchange(): return lax.all_to_all(values, axis, 0, 0, tiled=True)]
  transfers between devices with their start and end apart: 4 -> 3, of which waited for: 3 -> 2; matrix products, arithmetic and copies ran while one was open for 0% -> 0% of each run, Pallas kernels for 2% -> 1%
where the time goes in v8:
time: 106 us
  blocking collectives  66.2 us (62%)
  starting transfers between devices  18 us (17%)
  Pallas kernels  11.5 us (11%)
  waiting for transfers between devices  9.21 us (9%)
    all_to_all x4, blocking collectives, exchange(): return lax.all_to_all(values, axis, 0, 0, tiled=True)  66.2 us
    all_to_all x1, starting transfers between devices, exchange(): return lax.all_to_all(values, axis, 0, 0, tiled=True)  14 us
    all_to_all x1, waiting for transfers between devices, exchange(): return lax.all_to_all(values, axis, 0, 0, tiled=True)  8.74 us
    pallas_call x1, Pallas kernels, shards(): call(closure_kernel, shape(8, 40, 256), scratch, count=11, name='closure'...  4.65 us
    ppermute x1, starting transfers between devices, shards(): after = lax.ppermute(low, ('row', 'col'), [(j, i) for i, j in up])  2.55 us
  transfers between devices with their start and end apart: 3, of which 2 were waited for; matrix products, arithmetic and copies ran while one was open for 0% of the time, Pallas kernels for 1%

profile of v8, /device:TPU:1, one launch (start us, length us, event | category | flops | bytes accessed | tf_op | source)
XLA Modules:
  0.0 105.6 jit_solution(14300265334287126694)
XLA Ops:
  0.6 1.4 %pack.1 = (f32[8,64,256]{2,1,0:T(8,128)S(1)}, f32[8,256]{1,0:T(8,128)S(1)}) custom-call(f32[2,256,128]{2,1,0:T(8,128)} %cot_ref.1, f32[2,256,128]{2,1,0:T(8,128)} %state_ref.1, f32[8,256]{1,0:T(8,128)} %constant.28.clone.twist_far), custom_call_target="tpu_custom_call" | custom-call | tf_op jit(solution)/shard_map/pack/pallas_call | solution.py:505
  2.0 0.0 copy-start
  2.0 14.5 %all_to_all.25.in_ref.own_ref = f32[8,64,256]{2,1,0:T(8,128)S(1)} all-to-all(f32[8,64,256]{2,1,0:T(8,128)S(1)} %get-tuple-element.23), channel_id=1, replica_groups=mesh['row'=8,'col'=32] {'row'}, dimensions={0} | all-to-all | bytes 1048576 | tf_op jit(solution)/shard_map/all_to_all | solution.py:502
  16.5 0.0 copy-done
  16.5 1.3 %ahead.1 = (f32[512,128]{1,0:T(8,128)}, f32[4,2048]{1,0:T(4,128)S(1)}, f32[4,2048]{1,0:T(4,128)S(1)}) custom-call(bf16[2,512,256]{2,1,0:T(8,128)(2,1)S(1)} %copy-done, f32[8,256]{1,0:T(8,128)S(1)} %get-tuple-element.22.twist_ref, f32[8,64,256]{2,1,0:T(8,128)S(1)} %all_to_all.25.in_ref.own_ref), custom_call_target="tpu_custom_call" | custom-call | tf_op jit(solution)/shard_map/ahead/pallas_call | solution.py:509
  17.9 0.0 copy-start.1
  17.9 0.0 copy-start.2
  17.9 14.0 %all-to-all-start.1 = ((f32[256,1,256]{2,1,0:T(1,128)}), f32[256,1,256]{2,1,0:T(1,128)S(1)}, u32[]{:S(2)}, u32[]{:S(2)}) async-start(f32[256,1,256]{2,1,0:T(1,128)} %bitcast), calls=%async_computation.1 | async-start | bytes 524288 | tf_op jit(solution)/shard_map/all_to_all | solution.py:502
  31.8 1.4 %collective-permute-start = (f32[4,2048]{1,0:T(4,128)S(1)}, f32[4,2048]{1,0:T(4,128)S(1)}, u32[]{:S(2)}, u32[]{:S(2)}) collective-permute-start(f32[4,2048]{1,0:T(4,128)S(1)} %get-tuple-element.28), channel_id=1, source_target_pairs={{0,32},{32,64},{64,96},{96,128},{128,160},{160,192},{192,224},{224... | collective-permute-start | bytes 98312 | tf_op jit(solution)/shard_map/ppermute | solution.py:515
  33.3 2.5 %collective-permute-start.1 = (f32[4,2048]{1,0:T(4,128)S(1)}, f32[4,2048]{1,0:T(4,128)S(1)}, u32[]{:S(2)}, u32[]{:S(2)}) collective-permute-start(f32[4,2048]{1,0:T(4,128)S(1)} %get-tuple-element.29), channel_id=1, source_target_pairs={{32,0},{64,32},{96,64},{128,96},{160,128},{192,160},{224,192},{1,2... | collective-permute-start | bytes 98312 | tf_op jit(solution)/shard_map/ppermute | solution.py:516
  35.8 1.4 %bands.1 = (bf16[576,160]{1,0:T(8,128)(2,1)S(1)}, bf16[576,160]{1,0:T(8,128)(2,1)S(1)}, bf16[160,576]{1,0:T(8,128)(2,1)S(1)}) custom-call(bf16[18,32]{1,0:T(8,128)(2,1)} %first_far.1, bf16[18,32]{1,0:T(8,128)(2,1)} %bitcast.16, f32[1,32]{1,0:T(1,128)} %bitcast.17, bf16[2,18,256]{2,1,0:T(8,128)(2,1)} %constant.29.clone.pick_far), custom_call_target="tpu_custom_call" | custom-call | tf_op jit(solution)/shard_map/bands/pallas_call | solution.py:518
  37.2 0.5 collective-permute-done.before_ref
  37.7 0.0 collective-permute-done.1.after_ref
  37.7 8.7 %all-to-all-done.1 = f32[256,1,256]{2,1,0:T(1,128)S(1)} async-done(((f32[256,1,256]{2,1,0:T(1,128)}), f32[256,1,256]{2,1,0:T(1,128)S(1)}, u32[]{:S(2)}, u32[]{:S(2)}) %all-to-all-start.1) | async-done | bytes 262176 | tf_op jit(solution)/shard_map/all_to_all | solution.py:502
  46.5 0.0 copy-done.1
  46.5 0.0 copy-done.2
  46.5 1.8 %middle.1 = f32[768,128]{1,0:T(8,128)S(1)} custom-call(s32[1]{0:T(128)} %bitcast.4.place_ref, bf16[2,512,256]{2,1,0:T(8,128)(2,1)S(1)} %copy-done, f32[2,256,128]{2,1,0:T(8,128)S(1)} %copy-done.1, bf16[2,128,256]{2,1,0:T(8,128)(2,1)S(1)} %copy-done.2, f32[512,128]{1,0:T(8,128)S(1)} %bitcast.13), custom_call_target="tpu_custom_call" | custom-call | tf_op jit(solution)/shard_map/middle/pallas_call | solution.py:537
  48.3 0.0 copy-start.3
  48.3 0.0 copy-start.4
  48.3 24.3 %all_to_all.26 = f32[256,1,384]{2,1,0:T(1,128)S(1)} all-to-all(f32[256,1,384]{2,1,0:T(1,128)S(1)} %bitcast.11), channel_id=1, replica_groups=mesh['row'=8,'col'=32] {'col','row'}, dimensions={0} | all-to-all | bytes 786432 | tf_op jit(solution)/shard_map/all_to_all | solution.py:502
  72.6 0.0 copy-done.3
  72.6 0.0 copy-done.4
  72.6 4.7 %closure.1 = f32[8,40,256]{2,1,0:T(8,128)S(1)} custom-call(bf16[576,160]{1,0:T(8,128)(2,1)S(1)} %get-tuple-element.30.w1_ref, bf16[576,160]{1,0:T(8,128)(2,1)S(1)} %get-tuple-element.31.w2_ref, bf16[160,576]{1,0:T(8,128)(2,1)S(1)} %get-tuple-element.32.turn_ref, f32[8,64,256]{2,1,0:T(8,128)S(1)} %all_to_all.25.in_ref.own_ref, ...), custom_call_target="tpu_custom_call" | custom-call | tf_op jit(solution)/shard_map/closure/pallas_call | solution.py:548
  77.3 11.6 %all_to_all.27.in_ref.result_ref = f32[8,40,256]{2,1,0:T(8,128)S(1)} all-to-all(f32[8,40,256]{2,1,0:T(8,128)S(1)} %closure.1), channel_id=1, replica_groups=mesh['row'=8,'col'=32] {'row'}, dimensions={0} | all-to-all | bytes 655360 | tf_op jit(solution)/shard_map/all_to_all | solution.py:502
  89.0 15.7 %all_to_all.28 = f32[32,1,1280]{2,1,0:T(1,128)S(1)} all-to-all(f32[32,1,1280]{2,1,0:T(1,128)S(1)} %bitcast.15), channel_id=1, replica_groups=mesh['row'=8,'col'=32] {'col'}, dimensions={0} | all-to-all | bytes 327680 | tf_op jit(solution)/shard_map/all_to_all | solution.py:502
  104.7 0.9 final.1
  (1 shorter events, 0.0 us)
Async XLA Ops:
  2.0 14.5 %copy-start = (bf16[2,512,256]{2,1,0:T(8,128)(2,1)S(1)}, bf16[2,512,256]{2,1,0:T(8,128)(2,1)}, u32[]{:S(2)}) copy-start(bf16[2,512,256]{2,1,0:T(8,128)(2,1)} %constant.25.clone.dft_ref) | copy-start | bytes 1572868
  17.9 28.6 %copy-start.1 = (f32[2,256,128]{2,1,0:T(8,128)S(1)}, f32[2,256,128]{2,1,0:T(8,128)}, u32[]{:S(2)}) copy-start(f32[2,256,128]{2,1,0:T(8,128)} %constant.27.clone.twist_ref) | copy-start | bytes 786436
  17.9 28.6 %copy-start.2 = (bf16[2,128,256]{2,1,0:T(8,128)(2,1)S(1)}, bf16[2,128,256]{2,1,0:T(8,128)(2,1)}, u32[]{:S(2)}) copy-start(bf16[2,128,256]{2,1,0:T(8,128)(2,1)} %constant.26.clone.group_ref) | copy-start | bytes 393220
  17.9 28.6 %all-to-all-start.1 = ((f32[256,1,256]{2,1,0:T(1,128)}), f32[256,1,256]{2,1,0:T(1,128)S(1)}, u32[]{:S(2)}, u32[]{:S(2)}) async-start(f32[256,1,256]{2,1,0:T(1,128)} %bitcast), calls=%async_computation.1 | async-start | bytes 524288 | tf_op jit(solution)/shard_map/all_to_all | solution.py:502
  31.8 5.9 %collective-permute-start = (f32[4,2048]{1,0:T(4,128)S(1)}, f32[4,2048]{1,0:T(4,128)S(1)}, u32[]{:S(2)}, u32[]{:S(2)}) collective-permute-start(f32[4,2048]{1,0:T(4,128)S(1)} %get-tuple-element.28), channel_id=1, source_target_pairs={{0,32},{32,64},{64,96},{96,128},{128,160},{160,192},{192,224},{224... | collective-permute-start | bytes 98312 | tf_op jit(solution)/shard_map/ppermute | solution.py:515
  33.3 4.4 %collective-permute-start.1 = (f32[4,2048]{1,0:T(4,128)S(1)}, f32[4,2048]{1,0:T(4,128)S(1)}, u32[]{:S(2)}, u32[]{:S(2)}) collective-permute-start(f32[4,2048]{1,0:T(4,128)S(1)} %get-tuple-element.29), channel_id=1, source_target_pairs={{32,0},{64,32},{96,64},{128,96},{160,128},{192,160},{224,192},{1,2... | collective-permute-start | bytes 98312 | tf_op jit(solution)/shard_map/ppermute | solution.py:516
  48.3 24.4 %copy-start.3 = (bf16[256,128]{1,0:T(8,128)(2,1)S(1)}, bf16[256,128]{1,0:T(8,128)(2,1)}, u32[]{:S(2)}) copy-start(bf16[256,128]{1,0:T(8,128)(2,1)} %constant.31.clone.take2_ref) | copy-start | bytes 196612
  48.3 24.4 %copy-start.4 = (bf16[256,128]{1,0:T(8,128)(2,1)S(1)}, bf16[256,128]{1,0:T(8,128)(2,1)}, u32[]{:S(2)}) copy-start(bf16[256,128]{1,0:T(8,128)(2,1)} %constant.30.clone.take1_ref) | copy-start | bytes 196612

commit v9 on v8

--- a/solution.py
+++ b/solution.py
@@ -7,6 +7,7 @@
 from jax.experimental import pallas as pl
 from jax.experimental.pallas import tpu as pltpu
 from jax.sharding import PartitionSpec as P
+
 
 NX, NY = 2048, 4096
 ROWS, COLS = 8, 32
@@ -468,7 +469,7 @@
         out_ref[c] = lines.T
 
 
-def call(kernel, outs, scratch=(), scalars=0, count=0, name=None, remote=0, mib=8):
+def call(kernel, outs, scratch=(), scalars=0, count=0, remote=0, mib=8):
     space = [pl.BlockSpec(memory_space=pltpu.SMEM)] * scalars
     space += [pl.BlockSpec(memory_space=pltpu.HBM)] * remote
     space += [pl.BlockSpec(memory_space=pltpu.VMEM)] * (count - scalars - remote)
@@ -481,7 +482,6 @@
         out_specs=[out_space] * len(outs) if many else out_space,
         scratch_shapes=list(scratch),
         compiler_params=pltpu.CompilerParams(vmem_limit_bytes=mib * 2**20),
-        name=name,
     )
 
 
@@ -503,12 +503,12 @@
 
     space = [pltpu.VMEM((4, 256, 128), f32), pltpu.SemaphoreType.DMA((5,))]
     packed, twist_x = call(
-        pack_kernel, [shape(8, 64, 256), shape(8, 256)], space, count=3, name="pack", remote=3
+        pack_kernel, [shape(8, 64, 256), shape(8, 256)], space, count=3, remote=3
     )(far(cotangent), far(state), far(twist_x))
     lines = exchange(packed, "row")
     modes, low, high = call(
         ahead_kernel, [shape(512, 128), shape(4, NX), shape(4, NX)],
-        count=3, name="ahead",
+        count=3,
     )(dft, twist_x, lines)
     order = [(i % ROWS) * COLS + i // ROWS for i in range(DEV)]
     up = [(order[i], order[(i + 1) % DEV]) for i in range(DEV)]
@@ -528,13 +528,13 @@
         ],
         count=4,
         remote=4,
-        name="bands",
     )(
         far(first_kernel), far(second_kernel.T), far(first_bias.reshape(1, FEATS)),
         far(jnp.asarray(np.stack([first_pick, second_pick]))),
     )
-    modes, prepared, before, after = lax.optimization_barrier((modes, prepared, before, after))
-    modes = call(middle_kernel, shape(768, 128), scalars=1, count=5, name="middle")(place, dft, twist_y, group, modes)
+    modes, prepared = lax.optimization_barrier((modes, prepared))
+    modes = call(middle_kernel, shape(768, 128), scalars=1, count=5)(place, dft, twist_y, group, modes)
+    modes, before, after = lax.optimization_barrier((modes, before, after))
     modes = exchange(modes.reshape(DEV, 1, 384), every).reshape(768, 128)
     scratch = [
         pltpu.VMEM((2, WIDE, NX), f32),
@@ -546,16 +546,13 @@
         pltpu.VMEM((512, NX), bf16),
     ]
     result = call(
-        closure_kernel, shape(8, 40, 256), scratch, count=11, name="closure", mib=40
+        closure_kernel, shape(8, 40, 256), scratch, count=11, mib=40
     )(*prepared, lines, before, after, dft, twist_x, first_take, second_take, modes)
     result = exchange(result, "row")
-    part = call(part_kernel, shape(320, 128), count=1, name="part")(result)
+    part = call(part_kernel, shape(320, 128), count=1)(result)
     part = exchange(part.reshape(COLS, 1, 1280), "col").reshape(320, 128)
     grad_state, grad_first, grad_second, grad_bias = call(
-        final_kernel,
-        [shape(2, 256, 128), shape(18, 32), shape(18, 32), shape(1, 32)],
-        count=2,
-        name="final",
+        final_kernel, [shape(2, 256, 128), shape(18, 32), shape(18, 32), shape(1, 32)], count=2
     )(result, part)
     return grad_state, grad_first, grad_second.T, grad_bias.reshape(32)
 

time: 106 us -> 105 us (level)
  blocking collectives: 66.2 us -> 65.1 us
    all_to_all x4, blocking collectives: 66.2 us -> 65.1 us  [exchange(): return lax.all_to_all(values, axis, 0, 0, tiled=True)]
  transfers between devices with their start and end apart: 3 -> 3, of which waited for: 2 -> 1; matrix products, arithmetic and copies ran while one was open for 0% -> 0% of each run, Pallas kernels for 1% -> 3%
where the time goes in v9:
time: 105 us
  blocking collectives  65.1 us (62%)
  starting transfers between devices  18 us (17%)
  Pallas kernels  11.5 us (11%)
  waiting for transfers between devices  9.22 us (9%)
    all_to_all x4, blocking collectives, exchange(): return lax.all_to_all(values, axis, 0, 0, tiled=True)  65.1 us
    all_to_all x1, starting transfers between devices, exchange(): return lax.all_to_all(values, axis, 0, 0, tiled=True)  14 us
    all_to_all x1, waiting for transfers between devices, exchange(): return lax.all_to_all(values, axis, 0, 0, tiled=True)  9.21 us
    pallas_call x1, Pallas kernels, shards(): call(closure_kernel, shape(8, 40, 256), scratch, count=11, mib=40)  4.65 us
    ppermute x1, starting transfers between devices, shards(): after = lax.ppermute(low, ('row', 'col'), [(j, i) for i, j in up])  2.55 us
  transfers between devices with their start and end apart: 3, of which 1 were waited for; matrix products, arithmetic and copies ran while one was open for 0% of the time, Pallas kernels for 3%

profile of v9, /device:TPU:1, one launch (start us, length us, event | category | flops | bytes accessed | tf_op | source)
XLA Modules:
  0.0 104.5 jit_solution(13883413471773939910)
XLA Ops:
  0.6 1.4 %shard_map.147 = (f32[8,64,256]{2,1,0:T(8,128)S(1)}, f32[8,256]{1,0:T(8,128)S(1)}) custom-call(f32[2,256,128]{2,1,0:T(8,128)} %cot_ref.1, f32[2,256,128]{2,1,0:T(8,128)} %state_ref.1, f32[8,256]{1,0:T(8,128)} %constant.28.clone.twist_far), custom_call_target="tpu_custom_call" | custom-call | tf_op jit(solution)/shard_map/pallas_call | solution.py:505
  2.0 0.0 copy-start
  2.0 14.5 %all_to_all.25.in_ref.own_ref = f32[8,64,256]{2,1,0:T(8,128)S(1)} all-to-all(f32[8,64,256]{2,1,0:T(8,128)S(1)} %get-tuple-element.24), channel_id=1, replica_groups=mesh['row'=8,'col'=32] {'row'}, dimensions={0} | all-to-all | bytes 1048576 | tf_op jit(solution)/shard_map/all_to_all | solution.py:502
  16.5 0.0 copy-done
  16.5 1.3 %shard_map.148 = (f32[512,128]{1,0:T(8,128)}, f32[4,2048]{1,0:T(4,128)S(1)}, f32[4,2048]{1,0:T(4,128)S(1)}) custom-call(bf16[2,512,256]{2,1,0:T(8,128)(2,1)S(1)} %copy-done, f32[8,256]{1,0:T(8,128)S(1)} %get-tuple-element.23.twist_ref, f32[8,64,256]{2,1,0:T(8,128)S(1)} %all_to_all.25.in_ref.own_ref), custom_call_target="tpu_custom_call" | custom-call | tf_op jit(solution)/shard_map/pallas_call | solution.py:509
  17.9 0.0 copy-start.1
  17.9 0.0 copy-start.2
  17.9 14.0 %all-to-all-start.1 = ((f32[256,1,256]{2,1,0:T(1,128)}), f32[256,1,256]{2,1,0:T(1,128)S(1)}, u32[]{:S(2)}, u32[]{:S(2)}) async-start(f32[256,1,256]{2,1,0:T(1,128)} %bitcast), calls=%async_computation.1 | async-start | bytes 524288 | tf_op jit(solution)/shard_map/all_to_all | solution.py:502
  31.8 1.4 %collective-permute-start = (f32[4,2048]{1,0:T(4,128)S(1)}, f32[4,2048]{1,0:T(4,128)S(1)}, u32[]{:S(2)}, u32[]{:S(2)}) collective-permute-start(f32[4,2048]{1,0:T(4,128)S(1)} %get-tuple-element.33), channel_id=1, source_target_pairs={{0,32},{32,64},{64,96},{96,128},{128,160},{160,192},{192,224},{224... | collective-permute-start | bytes 98312 | tf_op jit(solution)/shard_map/ppermute | solution.py:515
  33.3 2.5 %collective-permute-start.1 = (f32[4,2048]{1,0:T(4,128)S(1)}, f32[4,2048]{1,0:T(4,128)S(1)}, u32[]{:S(2)}, u32[]{:S(2)}) collective-permute-start(f32[4,2048]{1,0:T(4,128)S(1)} %get-tuple-element.34), channel_id=1, source_target_pairs={{32,0},{64,32},{96,64},{128,96},{160,128},{192,160},{224,192},{1,2... | collective-permute-start | bytes 98312 | tf_op jit(solution)/shard_map/ppermute | solution.py:516
  35.8 1.4 %shard_map.149 = (bf16[576,160]{1,0:T(8,128)(2,1)S(1)}, bf16[576,160]{1,0:T(8,128)(2,1)S(1)}, bf16[160,576]{1,0:T(8,128)(2,1)S(1)}) custom-call(bf16[18,32]{1,0:T(8,128)(2,1)} %first_far.1, bf16[18,32]{1,0:T(8,128)(2,1)} %bitcast.16, f32[1,32]{1,0:T(1,128)} %bitcast.17, bf16[2,18,256]{2,1,0:T(8,128)(2,1)} %constant.29.clone.pick_far), custom_call_target="tpu_custom_call" | custom-call | tf_op jit(solution)/shard_map/pallas_call | solution.py:518
  37.2 9.2 %all-to-all-done.1 = f32[256,1,256]{2,1,0:T(1,128)S(1)} async-done(((f32[256,1,256]{2,1,0:T(1,128)}), f32[256,1,256]{2,1,0:T(1,128)S(1)}, u32[]{:S(2)}, u32[]{:S(2)}) %all-to-all-start.1) | async-done | bytes 262176 | tf_op jit(solution)/shard_map/all_to_all | solution.py:502
  46.5 0.0 copy-done.1
  46.5 0.0 copy-done.2
  46.5 1.8 %shard_map.150 = f32[768,128]{1,0:T(8,128)S(1)} custom-call(s32[1]{0:T(128)} %bitcast.4.place_ref, bf16[2,512,256]{2,1,0:T(8,128)(2,1)S(1)} %copy-done, f32[2,256,128]{2,1,0:T(8,128)S(1)} %copy-done.1, bf16[2,128,256]{2,1,0:T(8,128)(2,1)S(1)} %copy-done.2, f32[512,128]{1,0:T(8,128)S(1)} %bitcast.13), custom_call_target="tpu_custom_call" | custom-call | tf_op jit(solution)/shard_map/pallas_call | solution.py:536
  48.3 0.0 collective-permute-done.before_ref
  48.3 0.0 collective-permute-done.1.after_ref
  48.3 0.0 copy-start.3
  48.3 0.0 copy-start.4
  48.3 23.6 %all_to_all.26 = f32[256,1,384]{2,1,0:T(1,128)S(1)} all-to-all(f32[256,1,384]{2,1,0:T(1,128)S(1)} %bitcast.11), channel_id=1, replica_groups=mesh['row'=8,'col'=32] {'col','row'}, dimensions={0} | all-to-all | bytes 786432 | tf_op jit(solution)/shard_map/all_to_all | solution.py:502
  71.9 0.0 copy-done.3
  71.9 0.0 copy-done.4
  71.9 4.6 %shard_map.151 = f32[8,40,256]{2,1,0:T(8,128)S(1)} custom-call(bf16[576,160]{1,0:T(8,128)(2,1)S(1)} %get-tuple-element.29.w1_ref, bf16[576,160]{1,0:T(8,128)(2,1)S(1)} %get-tuple-element.30.w2_ref, bf16[160,576]{1,0:T(8,128)(2,1)S(1)} %get-tuple-element.31.turn_ref, f32[8,64,256]{2,1,0:T(8,128)S(1)} %all_to_all.25.in_ref.own_ref, ...), custom_call_target="tpu_custom_call" | custom-call | tf_op jit(solution)/shard_map/pallas_call | solution.py:548
  76.5 11.3 %all_to_all.27.in_ref.result_ref = f32[8,40,256]{2,1,0:T(8,128)S(1)} all-to-all(f32[8,40,256]{2,1,0:T(8,128)S(1)} %shard_map.151), channel_id=1, replica_groups=mesh['row'=8,'col'=32] {'row'}, dimensions={0} | all-to-all | bytes 655360 | tf_op jit(solution)/shard_map/all_to_all | solution.py:502
  87.9 15.7 %all_to_all.28 = f32[32,1,1280]{2,1,0:T(1,128)S(1)} all-to-all(f32[32,1,1280]{2,1,0:T(1,128)S(1)} %bitcast.15), channel_id=1, replica_groups=mesh['row'=8,'col'=32] {'col'}, dimensions={0} | all-to-all | bytes 327680 | tf_op jit(solution)/shard_map/all_to_all | solution.py:502
  103.6 0.9 shard_map.153
  (1 shorter events, 0.0 us)
Async XLA Ops:
  2.0 14.5 %copy-start = (bf16[2,512,256]{2,1,0:T(8,128)(2,1)S(1)}, bf16[2,512,256]{2,1,0:T(8,128)(2,1)}, u32[]{:S(2)}) copy-start(bf16[2,512,256]{2,1,0:T(8,128)(2,1)} %constant.25.clone.dft_ref) | copy-start | bytes 1572868
  17.9 28.6 %copy-start.1 = (f32[2,256,128]{2,1,0:T(8,128)S(1)}, f32[2,256,128]{2,1,0:T(8,128)}, u32[]{:S(2)}) copy-start(f32[2,256,128]{2,1,0:T(8,128)} %constant.27.clone.twist_ref) | copy-start | bytes 786436
  17.9 28.6 %copy-start.2 = (bf16[2,128,256]{2,1,0:T(8,128)(2,1)S(1)}, bf16[2,128,256]{2,1,0:T(8,128)(2,1)}, u32[]{:S(2)}) copy-start(bf16[2,128,256]{2,1,0:T(8,128)(2,1)} %constant.26.clone.group_ref) | copy-start | bytes 393220
  17.9 28.6 %all-to-all-start.1 = ((f32[256,1,256]{2,1,0:T(1,128)}), f32[256,1,256]{2,1,0:T(1,128)S(1)}, u32[]{:S(2)}, u32[]{:S(2)}) async-start(f32[256,1,256]{2,1,0:T(1,128)} %bitcast), calls=%async_computation.1 | async-start | bytes 524288 | tf_op jit(solution)/shard_map/all_to_all | solution.py:502
  31.8 16.4 %collective-permute-start = (f32[4,2048]{1,0:T(4,128)S(1)}, f32[4,2048]{1,0:T(4,128)S(1)}, u32[]{:S(2)}, u32[]{:S(2)}) collective-permute-start(f32[4,2048]{1,0:T(4,128)S(1)} %get-tuple-element.33), channel_id=1, source_target_pairs={{0,32},{32,64},{64,96},{96,128},{128,160},{160,192},{192,224},{224... | collective-permute-start | bytes 98312 | tf_op jit(solution)/shard_map/ppermute | solution.py:515
  33.3 15.0 %collective-permute-start.1 = (f32[4,2048]{1,0:T(4,128)S(1)}, f32[4,2048]{1,0:T(4,128)S(1)}, u32[]{:S(2)}, u32[]{:S(2)}) collective-permute-start(f32[4,2048]{1,0:T(4,128)S(1)} %get-tuple-element.34), channel_id=1, source_target_pairs={{32,0},{64,32},{96,64},{128,96},{160,128},{192,160},{224,192},{1,2... | collective-permute-start | bytes 98312 | tf_op jit(solution)/shard_map/ppermute | solution.py:516
  48.3 23.6 %copy-start.3 = (bf16[256,128]{1,0:T(8,128)(2,1)S(1)}, bf16[256,128]{1,0:T(8,128)(2,1)}, u32[]{:S(2)}) copy-start(bf16[256,128]{1,0:T(8,128)(2,1)} %constant.31.clone.take2_ref) | copy-start | bytes 196612
  48.3 23.6 %copy-start.4 = (bf16[256,128]{1,0:T(8,128)(2,1)S(1)}, bf16[256,128]{1,0:T(8,128)(2,1)}, u32[]{:S(2)}) copy-start(bf16[256,128]{1,0:T(8,128)(2,1)} %constant.30.clone.take1_ref) | copy-start | bytes 196612
